TPU v7x, 32 devices: a whole 2x2x4 slice. The times are simulated.
32 devices in a mesh: fsdp: 16 (over z, y, core), tp: 2 (over x).
Axes of the slice: x: 2, y: 2, z: 4, core: 2. Of those that a mesh axis runs over, the one named last changes fastest.
Arguments:
- inputs: bfloat16 [32768, 768], P(('fsdp', 'tp')), may hold values from -6 to 6
- w_query: bfloat16 [768, 768], P('fsdp', 'tp'), may hold values from -0.21875 to 0.21875
- w_key: bfloat16 [768, 768], P('fsdp', 'tp'), may hold values from -0.21875 to 0.21875
- w_value: bfloat16 [768, 768], P('fsdp', 'tp'), may hold values from -0.21875 to 0.21875
- b_query: bfloat16 [768], P(('tp', 'fsdp')), may hold values from -4.5 to 3
- b_key: bfloat16 [768], P(('tp', 'fsdp')), may hold values from -4.5 to 3
- b_value: bfloat16 [768], P(('tp', 'fsdp')), may hold values from -0.29882812 to 0.29882812
- w_out: bfloat16 [768, 768], P('tp', 'fsdp'), may hold values from -6 to 6
- b_out: bfloat16 [768], P('fsdp'), may hold values from -3 to 3
- norm_gain: bfloat16 [768], P('fsdp'), may hold values from 0.25 to 1.75
- norm_shift: bfloat16 [768], P('fsdp'), may hold values from -3 to 3
- w_up: bfloat16 [768, 3072], P('fsdp', 'tp'), may hold values from -0.21875 to 0.21875
- b_up: bfloat16 [3072], P(('tp', 'fsdp')), may hold values from -3 to 3
- w_down: bfloat16 [3072, 768], P('tp', 'fsdp'), may hold values from -0.15625 to 0.15625
- b_down: bfloat16 [768], P('fsdp'), may hold values from -3 to 3
- final_gain: bfloat16 [768], P('fsdp'), may hold values from 0.25 to 1.75
- final_shift: bfloat16 [768], P('fsdp'), may hold values from -3 to 3
- piece_starts: int32 [16, 4], P('fsdp'), may hold values from 0 to 1792, as said below
- grad_output: bfloat16 [32768, 768], P(('fsdp', 'tp')), may hold values from -6 to 6
Outputs:
- output: bfloat16 [32768, 768], P(('fsdp', 'tp'))
- grad_inputs: bfloat16 [32768, 768], P(('fsdp', 'tp'))
- grad_w_query: float32 [768, 768], P('fsdp', 'tp')
- grad_w_key: float32 [768, 768], P('fsdp', 'tp')
- grad_w_value: float32 [768, 768], P('fsdp', 'tp')
- grad_b_query: float32 [768], P(('tp', 'fsdp'))
- grad_b_key: float32 [768], P(('tp', 'fsdp'))
- grad_b_value: float32 [768], P(('tp', 'fsdp'))
- grad_w_out: float32 [768, 768], P('tp', 'fsdp')
- grad_b_out: float32 [768], P('fsdp')
- grad_norm_gain: float32 [768], P('fsdp')
- grad_norm_shift: float32 [768], P('fsdp')
- grad_w_up: float32 [768, 3072], P('fsdp', 'tp')
- grad_b_up: float32 [3072], P(('tp', 'fsdp'))
- grad_w_down: float32 [3072, 768], P('tp', 'fsdp')
- grad_b_down: float32 [768], P('fsdp')
- grad_final_gain: float32 [768], P('fsdp')
- grad_final_shift: float32 [768], P('fsdp')
Inputs may be any that keep to these rules, and one draw needn't show every extreme that they name: `piece_starts`: each sequence has 4 picture pieces of 256 tokens with distinct starts, each a multiple of 256.
All inputs are finite; a program needn't handle non-finite values.
Results may differ from a plain program's by a relative error of at most 0.019.
Values may be sent and summed in bfloat16 or wider, within the bound.
No kernel may reach another device: no remote copies, remote signals or barrier semaphores. Data moves between devices by JAX's collectives and lax.ppermute only.
A program may use at most 192 MiB of HBM per device.

v0:
```python
import jax
import jax.numpy as jnp
from jax import lax
from jax.sharding import PartitionSpec as P

HEAD_DIM = 64
PIECE = 256


HIGHEST = lax.Precision.HIGHEST
epsilon = 1e-05


def contract(left, right, left_dim, right_dim):
    return lax.dot_general(
        left, right, (((left_dim,), (right_dim,)), ((), ())), preferred_element_type=jnp.float32
    )


def features(projected, cosines, sines):
    positive = jax.nn.softplus(projected)
    return jnp.concatenate([positive * cosines, positive * sines], axis=-1)


def gelu_exact(values):
    return jax.nn.gelu(values, approximate=False)


def block_mask(flags, width):
    places = jnp.arange(width, dtype=jnp.int32)
    causal = places[None, :] <= places[:, None]
    same_piece = places[:, None] // PIECE == places[None, :] // PIECE
    return jnp.logical_or(causal, jnp.logical_and(same_piece, flags[:, None])).astype(jnp.float32)


def norm_forward(values, gain, shift):
    average = jnp.mean(values, axis=1, keepdims=True)
    centred = values - average
    scale = lax.rsqrt(jnp.mean(centred * centred, axis=1, keepdims=True) + epsilon)
    normal = centred * scale
    return (normal * gain + shift, normal, scale)


def norm_backward(upstream, normal, scale, gain):
    scaled = upstream * gain
    inner = (
        scaled
        - jnp.mean(scaled, axis=1, keepdims=True)
        - normal * jnp.mean(scaled * normal, axis=1, keepdims=True)
    )
    return (inner * scale, jnp.sum(upstream * normal, axis=0), jnp.sum(upstream, axis=0))


def attention_forward(query_features, key_features, values, flags, width):
    length, heads, breadth = query_features.shape
    depth = values.shape[2]
    count = length // width

    def step(carry, block):
        numerator_state, denominator_state = carry
        query_block, key_block, value_block, flag_block = block
        allowed = block_mask(flag_block, width)
        scores = (
            jnp.einsum("ihf,jhf->hij", query_block, key_block, preferred_element_type=jnp.float32)
            * allowed
        )
        weights = scores.astype(jnp.bfloat16)
        state_low = numerator_state.astype(jnp.bfloat16)
        numerator = jnp.einsum(
            "hij,jhd->ihd", weights, value_block, preferred_element_type=jnp.float32
        ) + jnp.einsum("ihf,hfd->ihd", query_block, state_low, preferred_element_type=jnp.float32)
        denominator = jnp.sum(scores, axis=2).T + jnp.einsum(
            "ihf,hf->ih", query_block.astype(jnp.float32), denominator_state, precision=HIGHEST
        )
        mixed = (numerator / jnp.maximum(denominator, 1.0)[:, :, None]).astype(jnp.bfloat16)
        next_carry = (
            numerator_state
            + jnp.einsum(
                "jhf,jhd->hfd", key_block, value_block, preferred_element_type=jnp.float32
            ),
            denominator_state + jnp.sum(key_block.astype(jnp.float32), axis=0),
        )
        return (next_carry, (mixed, numerator, denominator, state_low, denominator_state))

    start = (
        jnp.zeros((heads, breadth, depth), jnp.float32),
        jnp.zeros((heads, breadth), jnp.float32),
    )
    blocks = (
        query_features.reshape(count, width, heads, breadth),
        key_features.reshape(count, width, heads, breadth),
        values.reshape(count, width, heads, depth),
        flags.reshape(count, width),
    )
    unused, (mixed, numerator, denominator, numerator_states, denominator_states) = lax.scan(
        step, start, blocks
    )
    return (
        mixed.reshape(length, heads * depth),
        numerator.reshape(length, heads, depth),
        denominator.reshape(length, heads),
        numerator_states,
        denominator_states,
    )


def attention_backward(
    grad_mixed,
    query_features,
    key_features,
    values,
    flags,
    numerator,
    denominator,
    numerator_states,
    denominator_states,
    width,
):
    length, heads, breadth = query_features.shape
    depth = values.shape[2]
    count = length // width

    def step(carry, block):
        numerator_total, denominator_total = carry
        (
            grad_block,
            query_block,
            key_block,
            value_block,
            flag_block,
            numerator_block,
            denominator_block,
            state_low,
            denominator_state,
        ) = block
        allowed = block_mask(flag_block, width)
        floored = jnp.maximum(denominator_block, 1.0)
        grad_numerator = (grad_block / floored[:, :, None]).astype(jnp.bfloat16)
        grad_denominator = jnp.where(
            denominator_block > 1.0,
            -jnp.sum(grad_block * numerator_block, axis=2) / (floored * floored),
            0.0,
        )
        scores = (
            jnp.einsum("ihf,jhf->hij", query_block, key_block, preferred_element_type=jnp.float32)
            * allowed
        )
        weights = scores.astype(jnp.bfloat16)
        grad_weights = jnp.einsum(
            "ihd,jhd->hij", grad_numerator, value_block, preferred_element_type=jnp.float32
        )
        grad_scores = ((grad_weights + grad_denominator.T[:, :, None]) * allowed).astype(
            jnp.bfloat16
        )
        later_low = numerator_total.astype(jnp.bfloat16)
        grad_query = (
            jnp.einsum("hij,jhf->ihf", grad_scores, key_block, preferred_element_type=jnp.float32)
            + jnp.einsum(
                "ihd,hfd->ihf", grad_numerator, state_low, preferred_element_type=jnp.float32
            )
            + grad_denominator[:, :, None] * denominator_state[None]
        )
        grad_key = (
            jnp.einsum("hij,ihf->jhf", grad_scores, query_block, preferred_element_type=jnp.float32)
            + jnp.einsum("jhd,hfd->jhf", value_block, later_low, preferred_element_type=jnp.float32)
            + denominator_total[None]
        )
        grad_value = jnp.einsum(
            "hij,ihd->jhd", weights, grad_numerator, preferred_element_type=jnp.float32
        ) + jnp.einsum("jhf,hfd->jhd", key_block, later_low, preferred_element_type=jnp.float32)
        next_carry = (
            numerator_total
            + jnp.einsum(
                "ihf,ihd->hfd", query_block, grad_numerator, preferred_element_type=jnp.float32
            ),
            denominator_total
            + jnp.einsum(
                "ihf,ih->hf", query_block.astype(jnp.float32), grad_denominator, precision=HIGHEST
            ),
        )
        return (next_carry, (grad_query, grad_key, grad_value))

    start = (
        jnp.zeros((heads, breadth, depth), jnp.float32),
        jnp.zeros((heads, breadth), jnp.float32),
    )
    blocks = (
        grad_mixed.reshape(count, width, heads, depth),
        query_features.reshape(count, width, heads, breadth),
        key_features.reshape(count, width, heads, breadth),
        values.reshape(count, width, heads, depth),
        flags.reshape(count, width),
        numerator.reshape(count, width, heads, depth),
        denominator.reshape(count, width, heads),
        numerator_states,
        denominator_states,
    )
    unused, (grad_query, grad_key, grad_value) = lax.scan(step, start, blocks, reverse=True)
    return (
        grad_query.reshape(length, heads, breadth),
        grad_key.reshape(length, heads, breadth),
        grad_value.reshape(length, heads, depth),
    )


def local(
    inputs,
    w_query,
    w_key,
    w_value,
    b_query,
    b_key,
    b_value,
    w_out,
    b_out,
    norm_gain,
    norm_shift,
    w_up,
    b_up,
    w_down,
    b_down,
    final_gain,
    final_shift,
    piece_starts,
    grad_output,
):
    local_rows, model_width = inputs.shape
    halves = lax.axis_size("tp")
    replicas = lax.axis_size("fsdp")
    length = local_rows * halves
    width = min(512, length)
    head_count = w_query.shape[1] // HEAD_DIM
    places = jnp.arange(length, dtype=jnp.int32)
    flags = jnp.any(piece_starts[0][:, None] == (places // PIECE * PIECE)[None, :], axis=0)
    angle = 0.5 * jnp.pi / length * jnp.arange(length, dtype=jnp.float32)
    cosines = jnp.cos(angle)[:, None, None]
    sines = jnp.sin(angle)[:, None, None]

    def featurize(projected):
        return features(projected, cosines, sines)

    def forward(arguments):
        (
            layer_input,
            query_shard,
            key_shard,
            value_shard,
            query_bias,
            key_bias,
            value_bias,
            out_shard,
            out_bias,
            first_gain,
            first_shift,
            up_shard,
            up_bias,
            down_shard,
            down_bias,
            second_gain,
            second_shift,
        ) = arguments
        (
            full_query,
            full_key,
            full_value,
            full_out,
            bias_query,
            bias_key,
            bias_value,
            bias_out,
            gain_first,
            shift_first,
        ) = (
            lax.all_gather(query_shard, "fsdp", axis=0, tiled=True),
            lax.all_gather(key_shard, "fsdp", axis=0, tiled=True),
            lax.all_gather(value_shard, "fsdp", axis=0, tiled=True),
            lax.all_gather(out_shard, "fsdp", axis=1, tiled=True),
            lax.all_gather(query_bias, "fsdp", axis=0, tiled=True),
            lax.all_gather(key_bias, "fsdp", axis=0, tiled=True),
            lax.all_gather(value_bias, "fsdp", axis=0, tiled=True),
            lax.all_gather(out_bias, "fsdp", axis=0, tiled=True),
            lax.all_gather(first_gain, "fsdp", axis=0, tiled=True),
            lax.all_gather(first_shift, "fsdp", axis=0, tiled=True),
        )
        full_up, full_down, bias_up, bias_down, gain_second, shift_second = (
            lax.all_gather(up_shard, "fsdp", axis=0, tiled=True),
            lax.all_gather(down_shard, "fsdp", axis=1, tiled=True),
            lax.all_gather(up_bias, "fsdp", axis=0, tiled=True),
            lax.all_gather(down_bias, "fsdp", axis=0, tiled=True),
            lax.all_gather(second_gain, "fsdp", axis=0, tiled=True),
            lax.all_gather(second_shift, "fsdp", axis=0, tiled=True),
        )
        sequence = lax.all_gather(layer_input, "tp", axis=0, tiled=True)
        queries = (
            jnp.dot(sequence, full_query, preferred_element_type=jnp.float32)
            + bias_query.astype(jnp.float32)
        ).reshape(length, head_count, HEAD_DIM)
        keys = (
            jnp.dot(sequence, full_key, preferred_element_type=jnp.float32)
            + bias_key.astype(jnp.float32)
        ).reshape(length, head_count, HEAD_DIM)
        values = (
            (
                jnp.dot(sequence, full_value, preferred_element_type=jnp.float32)
                + bias_value.astype(jnp.float32)
            )
            .astype(jnp.bfloat16)
            .reshape(length, head_count, HEAD_DIM)
        )
        query_features = featurize(queries).astype(jnp.bfloat16)
        key_features = featurize(keys).astype(jnp.bfloat16)
        mixed, numerator, denominator, numerator_states, denominator_states = attention_forward(
            query_features, key_features, values, flags, width
        )
        attended = lax.psum_scatter(
            jnp.dot(mixed, full_out, preferred_element_type=jnp.float32),
            "tp",
            scatter_dimension=0,
            tiled=True,
        )
        hidden, normal_first, scale_first = norm_forward(
            layer_input.astype(jnp.float32) + attended + bias_out.astype(jnp.float32),
            gain_first.astype(jnp.float32),
            shift_first.astype(jnp.float32),
        )
        hidden_low = hidden.astype(jnp.bfloat16)
        lifted_input = lax.all_gather(hidden_low, "tp", axis=0, tiled=True)
        lifted = jnp.dot(
            lifted_input, full_up, preferred_element_type=jnp.float32
        ) + bias_up.astype(jnp.float32)
        active = gelu_exact(lifted).astype(jnp.bfloat16)
        lowered = lax.psum_scatter(
            jnp.dot(active, full_down, preferred_element_type=jnp.float32),
            "tp",
            scatter_dimension=0,
            tiled=True,
        )
        output, normal_second, scale_second = norm_forward(
            hidden + lowered + bias_down.astype(jnp.float32),
            gain_second.astype(jnp.float32),
            shift_second.astype(jnp.float32),
        )
        kept = (
            sequence,
            full_query,
            full_key,
            full_value,
            full_out,
            full_up,
            full_down,
            gain_first,
            gain_second,
            queries,
            keys,
            values,
            query_features,
            key_features,
            mixed,
            numerator,
            denominator,
            numerator_states,
            denominator_states,
            normal_first,
            scale_first,
            lifted_input,
            lifted,
            active,
            normal_second,
            scale_second,
        )
        return (output, kept)

    arguments = (
        inputs,
        w_query,
        w_key,
        w_value,
        b_query,
        b_key,
        b_value,
        w_out,
        b_out,
        norm_gain,
        norm_shift,
        w_up,
        b_up,
        w_down,
        b_down,
        final_gain,
        final_shift,
    )
    output = forward(arguments)[0]
    refreshed = lax.optimization_barrier((output, arguments))
    kept = forward(refreshed[1])[1]
    (
        sequence,
        full_query,
        full_key,
        full_value,
        full_out,
        full_up,
        full_down,
        gain_first,
        gain_second,
        queries,
        keys,
        values,
        query_features,
        key_features,
        mixed,
        numerator,
        denominator,
        numerator_states,
        denominator_states,
        normal_first,
        scale_first,
        lifted_input,
        lifted,
        active,
        normal_second,
        scale_second,
    ) = kept
    grad_second, grad_gain_second, grad_shift_second = norm_backward(
        grad_output.astype(jnp.float32),
        normal_second,
        scale_second,
        gain_second.astype(jnp.float32),
    )
    grad_bias_down = jnp.sum(grad_second, axis=0)
    branch_low = grad_second.astype(jnp.bfloat16)
    branch_all = lax.all_gather(branch_low, "tp", axis=0, tiled=True)
    grad_active = contract(branch_all, full_down, 1, 1)
    grad_lifted = jax.vjp(gelu_exact, lifted)[1](grad_active)[0]
    lifted_low = grad_lifted.astype(jnp.bfloat16)
    grad_hidden_part = lax.psum_scatter(
        contract(lifted_low, full_up, 1, 1), "tp", scatter_dimension=0, tiled=True
    )
    grad_up_part = contract(lifted_input, lifted_low, 0, 0)
    grad_down_part = contract(active, branch_all, 0, 0)
    grad_up_bias_part = jnp.sum(grad_lifted, axis=0)
    grad_hidden = grad_second + grad_hidden_part
    grad_first, grad_gain_first, grad_shift_first = norm_backward(
        grad_hidden, normal_first, scale_first, gain_first.astype(jnp.float32)
    )
    grad_bias_out = jnp.sum(grad_first, axis=0)
    first_all = lax.all_gather(grad_first.astype(jnp.bfloat16), "tp", axis=0, tiled=True)
    grad_out_part = contract(mixed, first_all, 0, 0)
    grad_mixed = contract(first_all, full_out, 1, 1).reshape(length, head_count, HEAD_DIM)
    grad_query_features, grad_key_features, grad_values = attention_backward(
        grad_mixed,
        query_features,
        key_features,
        values,
        flags,
        numerator,
        denominator,
        numerator_states,
        denominator_states,
        width,
    )
    grad_queries = jax.vjp(featurize, queries)[1](grad_query_features)[0].reshape(length, -1)
    grad_keys = jax.vjp(featurize, keys)[1](grad_key_features)[0].reshape(length, -1)
    grad_values = grad_values.reshape(length, -1)
    query_low = grad_queries.astype(jnp.bfloat16)
    key_low = grad_keys.astype(jnp.bfloat16)
    value_low = grad_values.astype(jnp.bfloat16)
    input_part = (
        contract(query_low, full_query, 1, 1)
        + contract(key_low, full_key, 1, 1)
        + contract(value_low, full_value, 1, 1)
    )
    vectors = jnp.stack(
        [
            grad_bias_out,
            grad_gain_first,
            grad_shift_first,
            grad_bias_down,
            grad_gain_second,
            grad_shift_second,
        ]
    )
    doubled = jnp.broadcast_to(vectors[None], (halves,) + vectors.shape)
    input_sum, vector_sum = (
        lax.psum_scatter(input_part, "tp", scatter_dimension=0, tiled=True),
        lax.psum_scatter(doubled, "tp", scatter_dimension=0, tiled=True),
    )
    vector_sum = vector_sum[0]
    grad_inputs = (grad_first + input_sum).astype(jnp.bfloat16)
    attention_sums = (
        lax.psum_scatter(
            contract(sequence, query_low, 0, 0), "fsdp", scatter_dimension=0, tiled=True
        ),
        lax.psum_scatter(
            contract(sequence, key_low, 0, 0), "fsdp", scatter_dimension=0, tiled=True
        ),
        lax.psum_scatter(
            contract(sequence, value_low, 0, 0), "fsdp", scatter_dimension=0, tiled=True
        ),
        lax.psum_scatter(grad_out_part, "fsdp", scatter_dimension=1, tiled=True),
        lax.psum_scatter(jnp.sum(grad_queries, axis=0), "fsdp", scatter_dimension=0, tiled=True),
        lax.psum_scatter(jnp.sum(grad_keys, axis=0), "fsdp", scatter_dimension=0, tiled=True),
        lax.psum_scatter(jnp.sum(grad_values, axis=0), "fsdp", scatter_dimension=0, tiled=True),
        lax.psum_scatter(vector_sum[0], "fsdp", scatter_dimension=0, tiled=True),
        lax.psum_scatter(vector_sum[1], "fsdp", scatter_dimension=0, tiled=True),
        lax.psum_scatter(vector_sum[2], "fsdp", scatter_dimension=0, tiled=True),
    )
    feedforward_sums = (
        lax.psum_scatter(grad_up_part, "fsdp", scatter_dimension=0, tiled=True),
        lax.psum_scatter(grad_down_part, "fsdp", scatter_dimension=1, tiled=True),
        lax.psum_scatter(grad_up_bias_part, "fsdp", scatter_dimension=0, tiled=True),
        lax.psum_scatter(vector_sum[3], "fsdp", scatter_dimension=0, tiled=True),
        lax.psum_scatter(vector_sum[4], "fsdp", scatter_dimension=0, tiled=True),
        lax.psum_scatter(vector_sum[5], "fsdp", scatter_dimension=0, tiled=True),
    )
    attention_sums = [value / replicas for value in attention_sums]
    feedforward_sums = [value / replicas for value in feedforward_sums]
    return (
        output.astype(jnp.bfloat16),
        grad_inputs,
        attention_sums[0],
        attention_sums[1],
        attention_sums[2],
        attention_sums[4],
        attention_sums[5],
        attention_sums[6],
        attention_sums[3],
        attention_sums[7],
        attention_sums[8],
        attention_sums[9],
        feedforward_sums[0],
        feedforward_sums[2],
        feedforward_sums[1],
        feedforward_sums[3],
        feedforward_sums[4],
        feedforward_sums[5],
    )


def solution(mesh):
    return jax.shard_map(
        local,
        mesh=mesh,
        in_specs=(
            P(("fsdp", "tp"), None),
            P("fsdp", "tp"),
            P("fsdp", "tp"),
            P("fsdp", "tp"),
            P(("tp", "fsdp")),
            P(("tp", "fsdp")),
            P(("tp", "fsdp")),
            P("tp", "fsdp"),
            P("fsdp"),
            P("fsdp"),
            P("fsdp"),
            P("fsdp", "tp"),
            P(("tp", "fsdp")),
            P("tp", "fsdp"),
            P("fsdp"),
            P("fsdp"),
            P("fsdp"),
            P("fsdp", None),
            P(("fsdp", "tp"), None),
        ),
        out_specs=(
            P(("fsdp", "tp"), None),
            P(("fsdp", "tp"), None),
            P("fsdp", "tp"),
            P("fsdp", "tp"),
            P("fsdp", "tp"),
            P(("tp", "fsdp")),
            P(("tp", "fsdp")),
            P(("tp", "fsdp")),
            P("tp", "fsdp"),
            P("fsdp"),
            P("fsdp"),
            P("fsdp"),
            P("fsdp", "tp"),
            P(("tp", "fsdp")),
            P("tp", "fsdp"),
            P("fsdp"),
            P("fsdp"),
            P("fsdp"),
        ),
        check_vma=False,
    )
```

profile of v0, /device:TPU:0, one launch (start us, length us, event | category | flops | bytes accessed | tf_op | source)
XLA Modules:
  0.0 1756.0 jit_solution(11940892225476442693)
XLA Ops:
  20.6 63.0 %all-reduce.31 = (bf16[768]{0:T(1024)(128)(2,1)S(1)}, bf16[768]{0:T(1024)(128)(2,1)S(1)}, bf16[768]{0:T(1024)(128)(2,1)S(1)}, bf16[384]{0:T(512)(128)(2,1)S(1)},...) all-reduce(bf16[768]{0:T(1024)(128)(2,1)S(1)} %dynamic-update-slice, ...), channel_id=1, replica_groups=mesh['fsdp'=16,'tp'=2] {'fsdp'}, use_global_device_ids=true, to_apply=%add.5 | all-reduce | flops 7296 | bytes 29184
  85.1 19.3 %all_gather.112 = bf16[768,384]{1,0:T(8,128)(2,1)S(1)} all-gather(bf16[48,384]{1,0:T(8,128)(2,1)} %param.27), channel_id=1, replica_groups=mesh['fsdp'=16,'tp'=2] {'fsdp'}, dimensions={0}, use_global_device_ids=true | all-gather | bytes 626688 | tf_op jit(solution)/shard_map/all_gather | solution.py:275
  104.4 22.1 %all_gather.116 = bf16[768,384]{1,0:T(8,128)(2,1)} all-gather(bf16[48,384]{1,0:T(8,128)(2,1)} %param.26), channel_id=1, replica_groups=mesh['fsdp'=16,'tp'=2] {'fsdp'}, dimensions={0}, use_global_device_ids=true | all-gather | bytes 626688 | tf_op jit(solution)/shard_map/all_gather | solution.py:274
  126.5 20.7 %all_gather.114 = bf16[768,384]{1,0:T(8,128)(2,1)} all-gather(bf16[48,384]{1,0:T(8,128)(2,1)} %param.28), channel_id=1, replica_groups=mesh['fsdp'=16,'tp'=2] {'fsdp'}, dimensions={0}, use_global_device_ids=true | all-gather | bytes 626688 | tf_op jit(solution)/shard_map/all_gather | solution.py:276
  147.1 21.9 %all_gather.118 = bf16[384,768]{0,1:T(8,128)(2,1)} all-gather(bf16[384,48]{0,1:T(8,128)(2,1)S(1)} %copy-done.30), channel_id=1, replica_groups=mesh['fsdp'=16,'tp'=2] {'fsdp'}, dimensions={1}, use_global_device_ids=true | all-gather | bytes 626688 | tf_op jit(solution)/shard_map/all_gather | solution.py:277
  169.0 5.4 convolution_add_fusion.6
  180.4 5.5 convolution_add_fusion.5
  191.8 9.7 multiply_convert_fusion.21
  201.6 5.5 pad_maximum_fusion
  212.0 6.2 copy.211
  233.8 46.9 %while.68 = (s32[]{:T(128)}, f32[6,128,64]{1,2,0:T(8,128)S(1)}, f32[6,128]{1,0:T(8,128)S(1)}, bf16[4,512,6,64]{1,3,2,0:T(8,128)(2,1)}, bf16[4,512,6,128]{3,1,2,0...) while((s32[]{:T(128)}, f32[6,128,64]{1,2,0:T(8,128)S(1)}, ...), condition=%wide.region_4.5_spmd.clone, body=%wide.region_1.4_spmd.clone.sunk | while | flops 718495488 | bytes 23891576 | solution.py:95
  289.6 73.3 %reduce-scatter.14.cloned.1.call-done = f32[1024,768]{1,0:T(8,128)} async-done(((f32[2048,768]{1,0:T(8,128)}), f32[1024,768]{1,0:T(8,128)}) %reduce-scatter.14.cloned.1.call-update) | async-done | bytes 3145744 | tf_op jit(solution)/shard_map/reduce_scatter | solution.py:315
  368.6 5.6 all-gather.17.cloned.1.call-done
  374.2 45.4 %all-gather.13.cloned.1.call-done = bf16[2048,768]{1,0:T(8,128)(2,1)} async-done(((bf16[1024,768]{1,0:T(8,128)(2,1)}), bf16[2048,768]{1,0:T(8,128)(2,1)}) %all-gather.13.cloned.1.call-update) | async-done | bytes 3145744 | tf_op jit(solution)/shard_map/all_gather | solution.py:327
  419.6 39.6 %fusion.156 = f32[2048,768]{1,0:T(8,128)} fusion(bf16[1536,768]{0,1:T(8,128)(2,1)} %all-gather.17.cloned.1.call-done, bf16[2048,768]{1,0:T(8,128)(2,1)} %all-gather.13.cloned.1.call-done, bf16[768,1536]{1,0:T(8,128)(2,1)} %all-gather.15.cloned.1.call-done, f32[1536]{0:T(1024)S(1)} %convert_element_type.270), kind=kOutput, calls=%fused_computation.249 | convolution fusion | flops 9871294464 | bytes 14161920 | tf_op jit(solution)/shard_map/dot_general | solution.py:333
  459.9 76.4 %reduce-scatter.16.cloned.1.call-done = f32[1024,768]{1,0:T(8,128)} async-done(((f32[2048,768]{1,0:T(8,128)}), f32[1024,768]{1,0:T(8,128)}) %reduce-scatter.16.cloned.1.call-update) | async-done | bytes 3145744 | tf_op jit(solution)/shard_map/reduce_scatter | solution.py:332
  544.7 61.1 %all-reduce.30 = (bf16[384]{0:T(512)(128)(2,1)S(1)}, bf16[384]{0:T(512)(128)(2,1)S(1)}, bf16[384]{0:T(512)(128)(2,1)S(1)}, bf16[768]{0:T(1024)(128)(2,1)S(1)}, b...) all-reduce(bf16[384]{0:T(512)(128)(2,1)S(1)} %dynamic-update-slice., ...), channel_id=1, replica_groups=mesh['fsdp'=16,'tp'=2] {'fsdp'}, use_global_device_ids=true, to_apply=%add.11 | all-reduce | flops 6528 | bytes 26112
  605.8 20.3 %all_gather.135 = bf16[768,384]{1,0:T(8,128)(2,1)} all-gather(bf16[48,384]{1,0:T(8,128)(2,1)S(1)} %copy-done.27), channel_id=1, replica_groups=mesh['fsdp'=16,'tp'=2] {'fsdp'}, dimensions={0}, use_global_device_ids=true | all-gather | bytes 626688 | tf_op jit(solution)/shard_map/all_gather | solution.py:274
  626.1 22.1 %all_gather.131 = bf16[768,384]{1,0:T(8,128)(2,1)} all-gather(bf16[48,384]{1,0:T(8,128)(2,1)S(1)} %copy-done.28), channel_id=1, replica_groups=mesh['fsdp'=16,'tp'=2] {'fsdp'}, dimensions={0}, use_global_device_ids=true | all-gather | bytes 626688 | tf_op jit(solution)/shard_map/all_gather | solution.py:275
  648.2 20.4 %all_gather.133 = bf16[768,384]{1,0:T(8,128)(2,1)} all-gather(bf16[48,384]{1,0:T(8,128)(2,1)S(1)} %copy-done.29), channel_id=1, replica_groups=mesh['fsdp'=16,'tp'=2] {'fsdp'}, dimensions={0}, use_global_device_ids=true | all-gather | bytes 626688 | tf_op jit(solution)/shard_map/all_gather | solution.py:276
  668.6 21.9 %all_gather.137 = bf16[384,768]{0,1:T(8,128)(2,1)} all-gather(bf16[384,48]{0,1:T(8,128)(2,1)S(1)} %copy-done.31), channel_id=1, replica_groups=mesh['fsdp'=16,'tp'=2] {'fsdp'}, dimensions={1}, use_global_device_ids=true | all-gather | bytes 626688 | tf_op jit(solution)/shard_map/all_gather | solution.py:277
  702.7 5.4 reshape.682
  708.1 10.4 multiply_convert_fusion.17
  745.6 6.2 copy.215
  755.1 57.7 %while.69 = (s32[]{:T(128)}, f32[6,128,64]{1,2,0:T(8,128)S(1)}, f32[6,128]{1,0:T(8,128)S(1)}, bf16[4,512,6,64]{1,3,2,0:T(8,128)(2,1)}, f32[4,512,6,64]{1,3,2,0:T...) while((s32[]{:T(128)}, f32[6,128,64]{1,2,0:T(8,128)S(1)}, ...), condition=%wide.region_15.16_spmd.clone, body=%wide.region_12.15_spmd.clone.sunk | while | flops 718548480 | bytes 26600604 | solution.py:95
  823.5 72.8 %reduce-scatter.18.cloned.1.call-done = f32[1024,768]{1,0:T(8,128)} async-done(((f32[2048,768]{1,0:T(8,128)}), f32[1024,768]{1,0:T(8,128)}) %reduce-scatter.18.cloned.1.call-update) | async-done | bytes 3145744 | tf_op jit(solution)/shard_map/reduce_scatter | solution.py:315
  902.0 44.2 %all-gather.21.cloned.1.call-done = bf16[2048,768]{1,0:T(8,128)(2,1)} async-done(((bf16[1024,768]{1,0:T(8,128)(2,1)}), bf16[2048,768]{1,0:T(8,128)(2,1)}) %all-gather.21.cloned.1.call-update) | async-done | bytes 3145744 | tf_op jit(solution)/shard_map/all_gather | solution.py:327
  946.2 35.1 %multiply_convert_fusion.13 = (bf16[2048,1536]{1,0:T(8,128)(2,1)}, f32[2048,1536]{1,0:T(8,128)}, f32[2048,1536]{1,0:T(8,128)}) fusion(f32[1536]{0:T(1024)S(1)} %convert_element_type.287, bf16[2048,768]{1,0:T(8,128)(2,1)} %all-gather.21.cloned.1.call-done, bf16[768,1536]{1,0:T(8,128)(2,1)} %all-gather.23.cloned.1.call-done), kind=kOutput, calls=%fused_computation.197 | convolution fusion | flops 5039456256 | bytes 36968448 | tf_op jit(solution)/shard_map/dot_general | solution.py:328
  981.3 10.1 all-gather.25.cloned.1.call-done
  991.4 9.6 fusion.222
  1001.7 75.0 %reduce-scatter.20.cloned.1.call-done = f32[1024,768]{1,0:T(8,128)} async-done(((f32[2048,768]{1,0:T(8,128)}), f32[1024,768]{1,0:T(8,128)}) %reduce-scatter.20.cloned.1.call-update) | async-done | bytes 3145744 | tf_op jit(solution)/shard_map/reduce_scatter | solution.py:332
  1087.6 44.8 %all-gather.27.cloned.1.call-done = bf16[2048,768]{1,0:T(8,128)(2,1)} async-done(((bf16[1024,768]{1,0:T(8,128)(2,1)}), bf16[2048,768]{1,0:T(8,128)(2,1)}) %all-gather.27.cloned.1.call-update) | async-done | bytes 3145744 | tf_op jit(solution)/shard_map/all_gather | solution.py:431
  1132.5 17.6 %fusion.219 = (f32[1536]{0:T(1024)}, bf16[2048,1536]{1,0:T(8,128)(2,1)S(1)}) fusion(f32[2048,1536]{1,0:T(8,128)} %get-tuple-element.1122, bf16[2048,768]{1,0:T(8,128)(2,1)} %all-gather.27.cloned.1.call-done, bf16[1536,768]{0,1:T(8,128)(2,1)} %all-gather.25.cloned.1.call-done, f32[2048,1536]{1,0:T(8,128)} %get-tuple-element.1159, ...), kind=kOutput, calls=%fused_computation.385 | convolution fusion | flops 4882168320 | bytes 36974592 | tf_op jit(solution)/shard_map/dot_general | solution.py:15
  1152.7 6.9 fusion.163
  1159.7 77.0 %reduce-scatter.22.cloned.1.call-done = f32[1024,768]{1,0:T(8,128)} async-done(((f32[2048,768]{1,0:T(8,128)}), f32[1024,768]{1,0:T(8,128)}) %reduce-scatter.22.cloned.1.call-update) | async-done | bytes 3145744 | tf_op jit(solution)/shard_map/reduce_scatter | solution.py:435
  1245.9 9.5 fusion.230
  1257.4 9.7 fusion.161
  1271.5 6.1 copy.226
  1282.4 7.5 all-gather.29.cloned.1.call-done
  1289.8 5.2 fusion.229
  1310.7 151.8 %while.70 = (s32[]{:T(128)}, f32[6,128,64]{1,2,0:T(8,128)}, f32[6,128]{1,0:T(8,128)}, f32[4,512,6,128]{3,1,0,2:T(8,128)}, f32[4,512,6,128]{3,1,0,2:T(8,128)}, /*...) while((s32[]{:T(128)}, f32[6,128,64]{1,2,0:T(8,128)}, ...), condition=%wide.region_28.29_spmd.clone, body=%wide.region_26.28_spmd.clone.sunk | while | flops 1829002752 | bytes 65662336 | solution.py:198
  1471.6 18.7 %fusion.209 = (f32[6,64]{1,0:T(8,128)S(1)}, bf16[2048,6,64]{2,0,1:T(8,128)(2,1)}, f32[6,64]{1,0:T(8,128)S(1)}, bf16[2048,6,64]{2,0,1:T(8,128)(2,1)S(1)}) fusion(f32[2048,6,64]{2,0,1:T(8,128)} %copy.235, f32[2048]{0:T(1024)S(1)} %copy-done.36, f32[2048,6,128]{2,0,1:T(8,128)} %bitcast.403, f32[2048]{0:T(1024)S(1)} %copy-done.37, f32[2048,6,64]{2,0,1:T(8,128)} %copy.226, ...), kind=kLoop, calls=%fused_computation.378 | loop fusion | flops 26737920 | bytes 22039552 | tf_op jit(solution)/shard_map/reduce_sum | solution.py:501
  1494.6 5.3 fusion.227
  1502.4 5.4 fusion.226
  1524.7 61.4 %all-reduce.29 = (f32[384]{0:T(512)S(1)}, f32[384]{0:T(512)S(1)}, f32[384]{0:T(512)S(1)}, f32[768]{0:T(1024)S(1)}, f32[768]{0:T(1024)S(1)}, /*index=5*/f32[768]{...) all-reduce(f32[384]{0:T(512)S(1)} %reduce_sum.285, ...), channel_id=11, replica_groups=mesh['fsdp'=16,'tp'=2] {'fsdp'}, use_global_device_ids=true, to_apply=%region_34.35.clone | all-reduce | flops 7296 | bytes 58368
  1595.1 10.0 reduce-scatter.28.cloned.1.call-done
  1606.6 59.5 %reduce-scatter.26.cloned.1.call-done = f32[48,384]{1,0:T(8,128)} async-done(((f32[768,384]{1,0:T(8,128)}), f32[48,384]{1,0:T(8,128)}) %reduce-scatter.26.cloned.1.call-update) | async-done | bytes 73744 | tf_op jit(solution)/shard_map/reduce_scatter | solution.py:490
  1667.6 76.9 %reduce-scatter.24.cloned.1.call-done = f32[1024,768]{1,0:T(8,128)} async-done(((f32[2048,768]{1,0:T(8,128)}), f32[1024,768]{1,0:T(8,128)}) %reduce-scatter.24.cloned.1.call-update) | async-done | bytes 3145744 | tf_op jit(solution)/shard_map/reduce_scatter | solution.py:484
  (564 shorter events, 477.3 us)
Async XLA Ops:
  8.0 139.1 %copy-start.30 = (bf16[384,48]{0,1:T(8,128)(2,1)S(1)}, bf16[384,48]{0,1:T(8,128)(2,1)}, u32[]{:S(2)}) copy-start(bf16[384,48]{0,1:T(8,128)(2,1)} %param.32) | copy-start | bytes 110596
  8.0 161.0 %all-gather.11.cloned.1.call-start = ((), (), s32[]{:S(2)}) async-start(), calls=%async_computation.13 | async-start | bytes 4718592 | tf_op jit(solution)/shard_map/all_gather | solution.py:293
  8.8 354.1 %reduce-scatter.14.cloned.1.call-start = ((), (), s32[]{:S(2)}) async-start(), calls=%async_computation.14 | async-start | bytes 9437184 | tf_op jit(solution)/shard_map/reduce_scatter | solution.py:315
  85.0 106.8 %copy-start.32 = (f32[4,512]{1,0:T(4,128)}, f32[4,512]{1,0:T(4,128)S(1)}, u32[]{:S(2)}) copy-start(f32[4,512]{1,0:T(4,128)S(1)} %fusion.172) | copy-start | bytes 24580
  85.1 106.7 %copy-start.34 = (f32[4,512]{1,0:T(4,128)}, f32[4,512]{1,0:T(4,128)S(1)}, u32[]{:S(2)}) copy-start(f32[4,512]{1,0:T(4,128)S(1)} %fusion.173) | copy-start | bytes 24580
  288.4 74.6 %copy-start.4 = (bf16[1024,768]{1,0:T(8,128)(2,1)S(1)}, bf16[1024,768]{1,0:T(8,128)(2,1)}, u32[]{:S(2)}) copy-start(bf16[1024,768]{1,0:T(8,128)(2,1)} %param.25) | copy-start | bytes 4718596
  288.4 80.2 %all-gather.15.cloned.1.call-start = ((), (), s32[]{:S(2)}) async-start(), calls=%async_computation.16 | async-start | bytes 2506752 | tf_op jit(solution)/shard_map/all_gather | solution.py:286
  289.0 85.3 %all-gather.17.cloned.1.call-start = ((), (), s32[]{:S(2)}) async-start(), calls=%async_computation.17 | async-start | bytes 2506752 | tf_op jit(solution)/shard_map/all_gather | solution.py:287
  289.5 130.0 %all-gather.13.cloned.1.call-start = ((), (), s32[]{:S(2)}) async-start(), calls=%async_computation.15 | async-start | bytes 4718592 | tf_op jit(solution)/shard_map/all_gather | solution.py:327
  368.5 167.8 %reduce-scatter.16.cloned.1.call-start = ((), (), s32[]{:S(2)}) async-start(), calls=%async_computation.18 | async-start | bytes 9437184 | tf_op jit(solution)/shard_map/reduce_scatter | solution.py:332
  459.2 231.2 %all-gather.19.cloned.1.call-start = ((), (), s32[]{:S(2)}) async-start(), calls=%async_computation.19 | async-start | bytes 4718592 | tf_op jit(solution)/shard_map/all_gather | solution.py:293
  540.6 3.8 copy-start.56
  540.6 65.1 %copy-start.27 = (bf16[48,384]{1,0:T(8,128)(2,1)S(1)}, bf16[48,384]{1,0:T(8,128)(2,1)}, u32[]{:S(2)}) copy-start(bf16[48,384]{1,0:T(8,128)(2,1)} %param.26) | copy-start | bytes 110596
  540.6 85.5 %copy-start.28 = (bf16[48,384]{1,0:T(8,128)(2,1)S(1)}, bf16[48,384]{1,0:T(8,128)(2,1)}, u32[]{:S(2)}) copy-start(bf16[48,384]{1,0:T(8,128)(2,1)} %param.27) | copy-start | bytes 110596
  540.7 107.5 %copy-start.29 = (bf16[48,384]{1,0:T(8,128)(2,1)S(1)}, bf16[48,384]{1,0:T(8,128)(2,1)}, u32[]{:S(2)}) copy-start(bf16[48,384]{1,0:T(8,128)(2,1)} %param.28) | copy-start | bytes 110596
  540.7 127.9 %copy-start.31 = (bf16[384,48]{0,1:T(8,128)(2,1)S(1)}, bf16[384,48]{0,1:T(8,128)(2,1)}, u32[]{:S(2)}) copy-start(bf16[384,48]{0,1:T(8,128)(2,1)} %param.32) | copy-start | bytes 110596
  542.4 353.9 %reduce-scatter.18.cloned.1.call-start = ((), (), s32[]{:S(2)}) async-start(), calls=%async_computation.20 | async-start | bytes 9437184 | tf_op jit(solution)/shard_map/reduce_scatter | solution.py:315
  702.7 5.4 copy-start.14
  702.7 5.4 copy-start.33
  702.7 5.4 copy-start.35
  812.7 4.2 copy-start.2
  812.8 5.4 copy-start.25
  822.7 79.4 %all-gather.23.cloned.1.call-start = ((), (), s32[]{:S(2)}) async-start(), calls=%async_computation.22 | async-start | bytes 2506752 | tf_op jit(solution)/shard_map/all_gather | solution.py:286
  823.4 122.8 %all-gather.21.cloned.1.call-start = ((), (), s32[]{:S(2)}) async-start(), calls=%async_computation.21 | async-start | bytes 4718592 | tf_op jit(solution)/shard_map/all_gather | solution.py:327
  901.4 90.0 %all-gather.25.cloned.1.call-start = ((), (), s32[]{:S(2)}) async-start(), calls=%async_computation.23 | async-start | bytes 2506752 | tf_op jit(solution)/shard_map/all_gather | solution.py:287
  901.9 174.8 %reduce-scatter.20.cloned.1.call-start = ((), (), s32[]{:S(2)}) async-start(), calls=%async_computation.24 | async-start | bytes 9437184 | tf_op jit(solution)/shard_map/reduce_scatter | solution.py:332
  1001.0 131.4 %all-gather.27.cloned.1.call-start = ((), (), s32[]{:S(2)}) async-start(), calls=%async_computation.25 | async-start | bytes 4718592 | tf_op jit(solution)/shard_map/all_gather | solution.py:431
  1087.6 149.1 %reduce-scatter.22.cloned.1.call-start = ((), (), s32[]{:S(2)}) async-start(), calls=%async_computation.26 | async-start | bytes 9437184 | tf_op jit(solution)/shard_map/reduce_scatter | solution.py:435
  1132.5 20.2 %copy-start.47 = (bf16[768,1536]{1,0:T(8,128)(2,1)S(1)}, bf16[768,1536]{1,0:T(8,128)(2,1)}, u32[]{:S(2)}) copy-start(bf16[768,1536]{1,0:T(8,128)(2,1)} %all-gather.23.cloned.1.call-done) | copy-start | bytes 7077892
  1159.6 130.2 %all-gather.29.cloned.1.call-start = ((), (), s32[]{:S(2)}) async-start(), calls=%async_computation.27 | async-start | bytes 4718592 | tf_op jit(solution)/shard_map/all_gather | solution.py:446
  1244.7 275.3 %reduce-scatter.38.cloned.1.call-start = ((), (), s32[]{:S(2)}) async-start(), calls=%async_computation.35 | async-start | bytes 5013504 | tf_op jit(solution)/shard_map/reduce_scatter | solution.py:509
  1255.4 266.4 %reduce-scatter.36.cloned.1.call-start = ((), (), s32[]{:S(2)}) async-start(), calls=%async_computation.34 | async-start | bytes 5013504 | tf_op jit(solution)/shard_map/reduce_scatter | solution.py:508
  1267.1 256.4 %reduce-scatter.34.cloned.1.call-start = ((), (), s32[]{:S(2)}) async-start(), calls=%async_computation.33 | async-start | bytes 73728 | tf_op jit(solution)/shard_map/reduce_scatter | solution.py:485
  1271.5 6.1 copy-start.13
  1282.3 309.7 %reduce-scatter.32.cloned.1.call-start = ((), (), s32[]{:S(2)}) async-start(), calls=%async_computation.32 | async-start | bytes 1253376 | tf_op jit(solution)/shard_map/reduce_scatter | solution.py:499
  1302.0 291.6 %reduce-scatter.30.cloned.1.call-start = ((), (), s32[]{:S(2)}) async-start(), calls=%async_computation.31 | async-start | bytes 1253376 | tf_op jit(solution)/shard_map/reduce_scatter | solution.py:496
  1317.4 3.9 copy-start
  1355.0 3.9 copy-start
  1372.1 3.8 copy-start.3
  1393.1 4.0 copy-start
  1431.0 4.0 copy-start
  1448.0 3.8 copy-start.3
  1471.5 133.5 %reduce-scatter.28.cloned.1.call-start = ((), (), s32[]{:S(2)}) async-start(), calls=%async_computation.30 | async-start | bytes 1253376 | tf_op jit(solution)/shard_map/reduce_scatter | solution.py:493
  1499.9 166.1 %reduce-scatter.26.cloned.1.call-start = ((), (), s32[]{:S(2)}) async-start(), calls=%async_computation.29 | async-start | bytes 1253376 | tf_op jit(solution)/shard_map/reduce_scatter | solution.py:490
  1502.4 5.8 copy-start.16
  1507.8 236.7 %reduce-scatter.24.cloned.1.call-start = ((), (), s32[]{:S(2)}) async-start(), calls=%async_computation.28 | async-start | bytes 9437184 | tf_op jit(solution)/shard_map/reduce_scatter | solution.py:484
  1517.8 7.0 copy-start.38
  1517.8 226.8 %copy-start.11 = (f32[1024,768]{1,0:T(8,128)S(1)}, f32[1024,768]{1,0:T(8,128)}, u32[]{:S(2)}) copy-start(f32[1024,768]{1,0:T(8,128)} %copy-done.10) | copy-start | bytes 9437188
  (48 other events, 112.8 us)
Sparse Core Ops, SparseCore 0:
  10.4 47.6 all-gather.10
  288.5 74.3 reduce-scatter.13
  542.5 44.9 all-gather.18
  822.8 73.4 reduce-scatter.17
  1001.2 75.5 reduce-scatter.19
  1244.9 44.9 all-gather.28
Sparse Core Ops, SparseCore 1:
  291.1 39.8 all-gather.14
  333.1 41.0 all-gather.16
  376.3 43.2 all-gather.12
  459.3 76.9 reduce-scatter.15
  826.0 38.9 all-gather.22
  901.4 44.7 all-gather.20
  948.6 42.7 all-gather.24
  1087.7 44.8 all-gather.26
  1159.7 76.9 reduce-scatter.21
  1255.5 75.3 reduce-scatter.37
  1334.6 74.4 reduce-scatter.35
  1411.9 8.9 reduce-scatter.33
  1424.7 58.0 reduce-scatter.31
  1486.8 56.9 reduce-scatter.29
  1547.8 57.1 reduce-scatter.27
  1609.1 56.9 reduce-scatter.25
  1668.5 76.0 reduce-scatter.23
where the time goes:
time: 1770 us; the launch traced here: 1760 us
  waiting for transfers between devices  682 us (39%)
  matrix products  360 us (20%)
  blocking collectives  354 us (20%)
  local copies, waits for them, and re-layouts  198 us (11%)
  other arithmetic  137 us (8%)
  between operations  21.7 us (1%)
    unnamed x3, blocking collectives  185 us
    reduce_scatter x2, waiting for transfers between devices, forward(): lax.psum_scatter(jnp.dot(active, full_down, preferred_element_type=jnp.fl...  151 us
    reduce_scatter x2, waiting for transfers between devices, forward(): lax.psum_scatter(jnp.dot(mixed, full_out, preferred_element_type=jnp.floa...  146 us
    all_gather x2, waiting for transfers between devices, forward(): lifted_input = lax.all_gather(hidden_low, 'tp', axis=0, tiled=True)  89.5 us
    reduce_scatter x1, waiting for transfers between devices, local(): lax.psum_scatter(contract(lifted_low, full_up, 1, 1), 'tp', scatter_dimen...  77 us
    reduce_scatter x1, waiting for transfers between devices, local(): lax.psum_scatter(input_part, 'tp', scatter_dimension=0, tiled=True)  76.9 us
    dot_general x12, matrix products, contract(): lax.dot_general(left, right, (((left_dim,), (right_dim,)), ((), ())), pre...  75.4 us
    reduce_scatter x1, waiting for transfers between devices, local(): lax.psum_scatter(contract(sequence, query_low, 0, 0), 'fsdp', scatter_dim...  59.5 us
  transfers between devices with their start and end apart: 23, of which 14 were waited for; matrix products, arithmetic and copies ran while one was open for 19% of the time, Pallas kernels for 0%

commit v1 on v0

v1 whole, which is shorter than its diff:
```python
import functools
import math

import jax
import jax.numpy as jnp
from jax import lax
from jax.experimental import pallas as pl
from jax.experimental.pallas import tpu as pltpu
from jax.sharding import PartitionSpec as P

HEAD_DIM = 64
PIECE = 256
LANES = 128
EPSILON = 1e-05
F32 = jnp.float32
BF16 = jnp.bfloat16
BOTH = ("fsdp", "tp")


def dot(left, right):
    return lax.dot_general(left, right, (((1,), (0,)), ((), ())), preferred_element_type=F32)


def dot_nt(left, right):
    return lax.dot_general(left, right, (((1,), (1,)), ((), ())), preferred_element_type=F32)


def dot_tn(left, right):
    return lax.dot_general(left, right, (((0,), (0,)), ((), ())), preferred_element_type=F32)


def flat(ref):
    value = ref[...]
    return value.reshape(value.shape[0] * value.shape[1] * value.shape[2], value.shape[3])


def lane_mask(rows, head, dtype=BF16):
    lane = lax.broadcasted_iota(jnp.int32, (rows, LANES), 1)
    return (lane // HEAD_DIM == head).astype(F32).astype(dtype)


def same_head(rows, columns):
    row = lax.broadcasted_iota(jnp.int32, (rows, columns), 0)
    lane = lax.broadcasted_iota(jnp.int32, (rows, columns), 1)
    return (row // HEAD_DIM) % 2 == (lane // HEAD_DIM) % 2


def compact(state):
    left, right = state[:, :LANES], state[:, LANES:]
    row = lax.broadcasted_iota(jnp.int32, left.shape, 0)
    lane = lax.broadcasted_iota(jnp.int32, left.shape, 1)
    first = (row // HEAD_DIM) % 2 == 0
    low = lane < HEAD_DIM
    return jnp.where(
        low,
        jnp.where(first, left, pltpu.roll(left, HEAD_DIM, 1)),
        jnp.where(first, pltpu.roll(right, HEAD_DIM, 1), right),
    )


def expand(packed):
    row = lax.broadcasted_iota(jnp.int32, packed.shape, 0)
    lane = lax.broadcasted_iota(jnp.int32, packed.shape, 1)
    first = (row // HEAD_DIM) % 2 == 0
    low = lane < HEAD_DIM
    turned = pltpu.roll(packed, HEAD_DIM, 1)
    zero = jnp.zeros_like(packed)
    left = jnp.where(first & low, packed, jnp.where(~first & ~low, turned, zero))
    right = jnp.where(first & low, turned, jnp.where(~first & ~low, packed, zero))
    return jnp.concatenate([left, right], axis=1)


def turned_features(values, cosines, sines):
    wide = values.astype(F32)
    return jnp.concatenate([(wide * cosines).astype(BF16), (wide * sines).astype(BF16)], axis=1)


def params(megabytes=56):
    return pltpu.CompilerParams(vmem_limit_bytes=megabytes * 1024 * 1024)


def whole(shape):
    zeros = (0,) * len(shape)
    return pl.BlockSpec(shape, lambda *_: zeros)


def cost(flops, moved, transcendental=0):
    return pl.CostEstimate(
        flops=int(flops), bytes_accessed=int(moved), transcendentals=int(transcendental)
    )


def project_kernel(
    x_ref, w_ref, b_ref, cos_ref, sin_ref,
    sq_ref, sk_ref, v_ref, gq_ref, gk_ref, st_ref, tot_ref,
    *, block, step,
):
    rows = x_ref.shape[0]
    part = sq_ref.shape[1]
    weights = flat(w_ref)

    def body(index, carry):
        here = pl.ds(index * step, step)
        sums = dot(x_ref[here, :], weights)
        for place, (feature_ref, slope_ref) in enumerate(((sq_ref, gq_ref), (sk_ref, gk_ref))):
            value = sums[:, place * part : (place + 1) * part] + b_ref[0, place : place + 1, :]
            positive = jnp.maximum(value, 0.0) + jnp.log1p(jnp.exp(-jnp.abs(value)))
            feature_ref[here, :] = positive.astype(BF16)
            slope_ref[here, :] = jax.nn.sigmoid(value).astype(BF16)
        v_ref[here, :] = (sums[:, 2 * part :] + b_ref[0, 2:3, :]).astype(BF16)
        return carry

    lax.fori_loop(0, rows // step, body, 0)
    keep = same_head(2 * LANES, 2 * LANES)
    ones = jnp.ones((block, LANES), BF16)
    for pair in range(part // LANES):
        lanes = slice(pair * LANES, (pair + 1) * LANES)
        total = jnp.zeros((2 * LANES, 2 * LANES), F32)
        for place in range(rows // block):
            here = slice(place * block, (place + 1) * block)
            features = turned_features(sk_ref[here, lanes], cos_ref[here, :], sin_ref[here, :])
            state = dot_tn(features, jnp.concatenate([v_ref[here, lanes], ones], axis=1))
            state = jnp.where(keep, state, 0.0)
            st_ref[place, pair] = state.astype(BF16)
            total = total + state
        tot_ref[pair] = compact(total).astype(BF16)


def project(x, w, biases, cosines, sines, block):
    rows, width = x.shape
    groups, halves, shard, _ = w.shape
    part = width // halves
    pairs = width // LANES
    half = pairs // halves
    blocks = rows // block
    row_spec = pl.BlockSpec((rows, part), lambda t: (0, t))
    full = jax.ShapeDtypeStruct((rows, width), BF16)
    return pl.pallas_call(
        functools.partial(project_kernel, block=block, step=256),
        grid=(halves,),
        in_specs=[
            whole((rows, width)),
            pl.BlockSpec((groups, 1, shard, 3 * part), lambda t: (0, t, 0, 0)),
            pl.BlockSpec((1, 3, part), lambda t: (t, 0, 0)),
            whole((rows, LANES)),
            whole((rows, LANES)),
        ],
        out_specs=[
            row_spec, row_spec, row_spec, row_spec, row_spec,
            pl.BlockSpec((blocks, half, 2 * LANES, 2 * LANES), lambda t: (0, t, 0, 0)),
            pl.BlockSpec((half, 2 * LANES, LANES), lambda t: (t, 0, 0)),
        ],
        out_shape=[
            full, full, full, full, full,
            jax.ShapeDtypeStruct((blocks, pairs, 2 * LANES, 2 * LANES), BF16),
            jax.ShapeDtypeStruct((pairs, 2 * LANES, LANES), BF16),
        ],
        compiler_params=params(),
        cost_estimate=cost(2 * rows * width * 3 * width, 16e6),
        name="project",
    )(x, w, biases, cosines, sines)


def attend_kernel(sq_ref, sk_ref, v_ref, cm_ref, cos_ref, sin_ref, st_ref, num_ref, den_ref):
    blocks, block, _ = cm_ref.shape
    piece = min(PIECE, block)
    masks = [lane_mask(block, head) for head in range(2)]
    for place in range(blocks):
        start = place * block
        keys = sk_ref[start : start + block, :]
        values = v_ref[start : start + block, :]
        sides = [jnp.concatenate([values * mask, mask], axis=1) for mask in masks]
        for low in range(0, block, piece):
            here = slice(start + low, start + low + piece)
            span = low + piece
            queries = sq_ref[here, :]
            sums = None
            for mask, side in zip(masks, sides):
                scores = dot_nt(queries * mask[:piece], keys[:span])
                weights = (scores * cm_ref[place, low : low + piece, :span]).astype(BF16)
                term = dot(weights, side[:span])
                sums = term if sums is None else sums + term
            for earlier in range(place):
                sums = sums + dot(
                    turned_features(queries, cos_ref[here, :], sin_ref[here, :]), st_ref[earlier, 0]
                )
            num_ref[here, :] = sums[:, :LANES]
            den_ref[here, :] = sums[:, LANES:]


def attend(sq, sk, v, cm, cosines, sines, states):
    rows, width = sq.shape
    pairs = width // LANES
    blocks = cm.shape[0]
    spec = pl.BlockSpec((rows, LANES), lambda p: (0, p))
    full = jax.ShapeDtypeStruct((rows, width), F32)
    return pl.pallas_call(
        attend_kernel,
        grid=(pairs,),
        in_specs=[
            spec, spec, spec,
            whole(cm.shape), whole((rows, LANES)), whole((rows, LANES)),
            pl.BlockSpec((blocks, 1, 2 * LANES, 2 * LANES), lambda p: (0, p, 0, 0)),
        ],
        out_specs=[spec, spec],
        out_shape=[full, full],
        compiler_params=params(),
        cost_estimate=cost(8e9, 14e6),
        name="attend",
    )(sq, sk, v, cm, cosines, sines, states)


def norm_rows(values):
    average = jnp.mean(values, axis=1, keepdims=True)
    centred = values - average
    scale = lax.rsqrt(jnp.mean(centred * centred, axis=1, keepdims=True) + EPSILON)
    return centred * scale, scale


def mix_kernel(
    num_ref, den_ref, sq_ref, in_ref, cos_ref, sin_ref, w_ref, x_ref, vec_ref,
    mixed_ref, rden_ref, normal_ref, scale_ref, low_ref, wide_ref,
):
    pairs = in_ref.shape[0]
    halves = w_ref.shape[1]
    rows, width = x_ref.shape
    part = width // halves

    @pl.when(pl.program_id(0) == 0)
    def _():
        for pair in range(pairs):
            wide_ref[pair] = expand(in_ref[pair].astype(F32)).astype(BF16)

    for pair in range(pairs):
        lanes = slice(pair * LANES, (pair + 1) * LANES)
        sums = dot(turned_features(sq_ref[:, lanes], cos_ref[...], sin_ref[...]), wide_ref[pair])
        inverse = 1.0 / jnp.maximum(den_ref[:, lanes] + sums[:, LANES:], 1.0)
        rden_ref[:, lanes] = inverse
        mixed_ref[:, lanes] = ((num_ref[:, lanes] + sums[:, :LANES]) * inverse).astype(BF16)
    total = x_ref[...].astype(F32) + vec_ref[0:1, :]
    for half in range(halves):
        side = w_ref[:, half]
        side = side.reshape(width, part)
        total = total + dot_nt(mixed_ref[:, half * part : (half + 1) * part], side)
    normal, scale = norm_rows(total)
    normal_ref[...] = normal
    scale_ref[...] = jnp.broadcast_to(scale, scale_ref.shape)
    low_ref[...] = (normal * vec_ref[1:2, :] + vec_ref[2:3, :]).astype(BF16)


def mix(num, den, sq, incoming, cosines, sines, w, x, vectors, step):
    rows, width = x.shape
    groups, halves, shard, _ = w.shape
    part = width // halves
    pairs = incoming.shape[0]
    wide = pl.BlockSpec((step, width), lambda i: (i, 0))
    thin = pl.BlockSpec((step, LANES), lambda i: (i, 0))
    return pl.pallas_call(
        mix_kernel,
        grid=(rows // step,),
        in_specs=[
            wide, wide, wide, whole(incoming.shape), thin, thin,
            pl.BlockSpec((groups, halves, shard, part), lambda i: (0, 0, 0, 3)),
            wide, whole(vectors.shape),
        ],
        out_specs=[wide, wide, wide, thin, wide],
        out_shape=[
            jax.ShapeDtypeStruct((rows, width), BF16),
            jax.ShapeDtypeStruct((rows, width), F32),
            jax.ShapeDtypeStruct((rows, width), F32),
            jax.ShapeDtypeStruct((rows, LANES), F32),
            jax.ShapeDtypeStruct((rows, width), BF16),
        ],
        scratch_shapes=[pltpu.VMEM((pairs, 2 * LANES, 2 * LANES), BF16)],
        compiler_params=params(),
        cost_estimate=cost(2 * rows * width * width * 2, 20e6),
        name="mix",
    )(num, den, sq, incoming, cosines, sines, w, x, vectors)


def norm_back(upstream, normal, scale, gain):
    scaled = upstream * gain
    inner = (
        scaled
        - jnp.mean(scaled, axis=1, keepdims=True)
        - normal * jnp.mean(scaled * normal, axis=1, keepdims=True)
    )
    return inner * scale


def lift_kernel(
    low_ref, up_ref, down_ref, bias_ref, normal_ref, vec_ref, grad_ref,
    act_ref, slope_ref, out_ref, branch_ref, second_ref, sum_ref, total_ref,
    *, step,
):
    rows, width = low_ref.shape
    up, down = flat(up_ref), flat(down_ref)
    index = pl.program_id(0)
    last = pl.num_programs(0) - 1

    def body(place, carry):
        here = pl.ds(place * step, step)
        lifted = dot(low_ref[here, :], up) + bias_ref[0:1, :]
        share = 0.5 + 0.5 * lax.erf(lifted * math.sqrt(0.5))
        bell = jnp.exp(-0.5 * lifted * lifted) * (1.0 / math.sqrt(2.0 * math.pi))
        active = (lifted * share).astype(BF16)
        act_ref[here, :] = active
        slope_ref[here, :] = (share + lifted * bell).astype(BF16)
        term = dot_nt(active, down)

        @pl.when(index == 0)
        def _():
            total_ref[here, :] = term

        @pl.when(index > 0)
        def _():
            total_ref[here, :] = total_ref[here, :] + term

        return carry

    lax.fori_loop(0, rows // step, body, 0)

    @pl.when(index == last)
    def _():
        sum_ref[...] = jnp.zeros_like(sum_ref)

        def finish(place, carry):
            here = pl.ds(place * step, step)
            hidden = normal_ref[here, :] * vec_ref[1:2, :] + vec_ref[2:3, :]
            normal, scale = norm_rows(hidden + total_ref[here, :] + vec_ref[3:4, :])
            gain = vec_ref[4:5, :]
            out_ref[here, :] = (normal * gain + vec_ref[5:6, :]).astype(BF16)
            upstream = grad_ref[here, :].astype(F32)
            second = norm_back(upstream, normal, scale, gain)
            second_ref[here, :] = second
            branch_ref[here, :] = second.astype(BF16)
            sum_ref[0:1, :] += jnp.sum(upstream * normal, axis=0, keepdims=True)
            sum_ref[1:2, :] += jnp.sum(upstream, axis=0, keepdims=True)
            sum_ref[2:3, :] += jnp.sum(second, axis=0, keepdims=True)
            return carry

        lax.fori_loop(0, rows // step, finish, 0)


def lift(low, w, bias, normal, vectors, grad, tile):
    rows, width = low.shape
    groups, halves, shard, columns = w.shape
    units = columns // 2
    tiles = units // tile
    unit_spec = pl.BlockSpec((rows, tile), lambda i: (0, i))
    return pl.pallas_call(
        functools.partial(lift_kernel, step=256),
        grid=(halves * tiles,),
        in_specs=[
            whole((rows, width)),
            pl.BlockSpec((groups, 1, shard, tile), lambda i: (0, i // tiles, 0, i % tiles)),
            pl.BlockSpec((groups, 1, shard, tile), lambda i: (0, i // tiles, 0, tiles + i % tiles)),
            pl.BlockSpec((1, tile), lambda i: (0, i)),
            whole((rows, width)),
            whole(vectors.shape),
            whole((rows, width)),
        ],
        out_specs=[
            unit_spec, unit_spec, whole((rows, width)), whole((rows, width)),
            whole((rows, width)), whole((8, width)),
        ],
        out_shape=[
            jax.ShapeDtypeStruct((rows, halves * units), BF16),
            jax.ShapeDtypeStruct((rows, halves * units), BF16),
            jax.ShapeDtypeStruct((rows, width), BF16),
            jax.ShapeDtypeStruct((rows, width), BF16),
            jax.ShapeDtypeStruct((rows, width), F32),
            jax.ShapeDtypeStruct((8, width), F32),
        ],
        scratch_shapes=[pltpu.VMEM((rows, width), F32)],
        compiler_params=params(),
        cost_estimate=cost(4 * rows * width * halves * units, 40e6),
        name="lift",
    )(low, w, w, bias, normal, vectors, grad)


def lower_kernel(
    branch_ref, low_ref, act_ref, slope_ref, up_ref, down_ref, second_ref, normal_ref, scale_ref,
    vec_ref,
    gdown_ref, gup_ref, gbias_ref, first_ref, firstlow_ref, sum_ref,
    total_ref, turned_branch_ref, turned_low_ref, gl_ref,
    *, step,
):
    rows, width = low_ref.shape
    index = pl.program_id(0)
    last = pl.num_programs(0) - 1
    up, down = flat(up_ref), flat(down_ref)

    @pl.when(index == 0)
    def _():
        turned_branch_ref[...] = branch_ref[...].T
        turned_low_ref[...] = low_ref[...].T

    gdown_ref[...] = dot(turned_branch_ref[...], act_ref[...]).astype(BF16).reshape(gdown_ref.shape)
    gbias_ref[...] = jnp.zeros_like(gbias_ref)

    def body(place, carry):
        here = pl.ds(place * step, step)
        slope = dot(branch_ref[here, :], down) * slope_ref[here, :].astype(F32)
        gbias_ref[0:1, :] += jnp.sum(slope, axis=0, keepdims=True)
        slope = slope.astype(BF16)
        gl_ref[here, :] = slope
        term = dot_nt(slope, up)

        @pl.when(index == 0)
        def _():
            total_ref[here, :] = second_ref[here, :] + term

        @pl.when(index > 0)
        def _():
            total_ref[here, :] = total_ref[here, :] + term

        return carry

    lax.fori_loop(0, rows // step, body, 0)
    gup_ref[...] = dot(turned_low_ref[...], gl_ref[...]).astype(BF16).reshape(gup_ref.shape)

    @pl.when(index == last)
    def _():
        sum_ref[...] = jnp.zeros_like(sum_ref)

        def finish(place, carry):
            here = pl.ds(place * step, step)
            upstream = total_ref[here, :]
            normal = normal_ref[here, :]
            first = norm_back(upstream, normal, scale_ref[here, 0:1], vec_ref[1:2, :])
            first_ref[here, :] = first
            firstlow_ref[here, :] = first.astype(BF16)
            sum_ref[0:1, :] += jnp.sum(upstream * normal, axis=0, keepdims=True)
            sum_ref[1:2, :] += jnp.sum(upstream, axis=0, keepdims=True)
            sum_ref[2:3, :] += jnp.sum(first, axis=0, keepdims=True)
            return carry

        lax.fori_loop(0, rows // step, finish, 0)


def lower(branch, low, act, slope, w, second, normal, scale, vectors, tile):
    rows, width = low.shape
    groups, halves, shard, columns = w.shape
    units = columns // 2
    tiles = units // tile
    unit_spec = pl.BlockSpec((rows, tile), lambda i: (0, i))
    up_spec = pl.BlockSpec((groups, 1, shard, tile), lambda i: (0, i // tiles, 0, i % tiles))
    grad_shape = jax.ShapeDtypeStruct((groups, halves, shard, units), BF16)
    once = functools.partial(pl.BlockSpec, pipeline_mode=pl.Buffered(1))
    row_once = once((rows, width), lambda i: (0, 0))
    return pl.pallas_call(
        functools.partial(lower_kernel, step=256),
        grid=(halves * tiles,),
        in_specs=[
            row_once, row_once, unit_spec, unit_spec, up_spec,
            pl.BlockSpec((groups, 1, shard, tile), lambda i: (0, i // tiles, 0, tiles + i % tiles)),
            row_once, row_once,
            whole((rows, LANES)), whole(vectors.shape),
        ],
        out_specs=[
            up_spec, up_spec, pl.BlockSpec((8, tile), lambda i: (0, i)),
            whole((rows, width)), whole((rows, width)), whole((8, width)),
        ],
        out_shape=[
            grad_shape, grad_shape, jax.ShapeDtypeStruct((8, halves * units), F32),
            jax.ShapeDtypeStruct((rows, width), F32),
            jax.ShapeDtypeStruct((rows, width), BF16),
            jax.ShapeDtypeStruct((8, width), F32),
        ],
        scratch_shapes=[
            pltpu.VMEM((rows, width), F32),
            pltpu.VMEM((width, rows), BF16),
            pltpu.VMEM((width, rows), BF16),
            pltpu.VMEM((rows, tile), BF16),
        ],
        compiler_params=params(),
        cost_estimate=cost(8 * rows * width * halves * units, 50e6),
        name="lower",
    )(branch, low, act, slope, w, w, second, normal, scale, vectors)


def unmix_kernel(
    first_ref, mixed_ref, rden_ref, sq_ref, cos_ref, sin_ref, w_ref,
    gout_ref, gn_ref, gd_ref, st_ref, tot_ref, *, block, step,
):
    rows, width = first_ref.shape
    part = mixed_ref.shape[1]
    side = flat(w_ref)
    group_row = lax.broadcasted_iota(jnp.int32, (LANES, LANES), 0)
    group_lane = lax.broadcasted_iota(jnp.int32, (LANES, LANES), 1)
    group = (group_row // HEAD_DIM == group_lane // HEAD_DIM).astype(F32).astype(BF16)
    lane = lax.broadcasted_iota(jnp.int32, (step, LANES), 1) % HEAD_DIM

    def body(place, carry):
        here = pl.ds(place * step, step)
        grad = dot(first_ref[here, :], side)
        for pair in range(part // LANES):
            lanes = slice(pair * LANES, (pair + 1) * LANES)
            inverse = rden_ref[here, lanes]
            scaled = grad[:, lanes] * inverse
            product = scaled * mixed_ref[here, lanes].astype(F32)
            high = product.astype(BF16)
            rest = (product - high.astype(F32)).astype(BF16)
            inner = dot(high, group) + dot(rest, group)
            slope = jnp.where(inverse < 1.0, -inner, 0.0)
            high = slope.astype(BF16).astype(F32)
            gn_ref[here, lanes] = scaled.astype(BF16)
            gd_ref[here, lanes] = jnp.where(
                lane == 0, high, jnp.where(lane == 1, slope - high, 0.0)
            ).astype(BF16)
        return carry

    lax.fori_loop(0, rows // step, body, 0)
    gout_ref[...] = dot_tn(first_ref[...], mixed_ref[...]).astype(BF16).reshape(gout_ref.shape)
    keep = same_head(2 * LANES, 2 * LANES)
    for pair in range(part // LANES):
        lanes = slice(pair * LANES, (pair + 1) * LANES)
        total = jnp.zeros((2 * LANES, 2 * LANES), F32)
        for place in range(rows // block):
            here = slice(place * block, (place + 1) * block)
            features = turned_features(sq_ref[here, lanes], cos_ref[here, :], sin_ref[here, :])
            state = dot_tn(
                features, jnp.concatenate([gn_ref[here, lanes], gd_ref[here, lanes]], axis=1)
            )
            state = jnp.where(keep, state, 0.0)
            st_ref[place, pair] = state.astype(BF16)
            total = total + state
        tot_ref[pair] = compact(total).astype(BF16)


def unmix(first, mixed, rden, sq, cosines, sines, w, block):
    rows, width = first.shape
    groups, halves, shard, _ = w.shape
    part = width // halves
    pairs = width // LANES
    half = pairs // halves
    blocks = rows // block
    row_spec = pl.BlockSpec((rows, part), lambda t: (0, t))
    full = jax.ShapeDtypeStruct((rows, width), BF16)
    return pl.pallas_call(
        functools.partial(unmix_kernel, block=block, step=256),
        grid=(halves,),
        in_specs=[
            whole((rows, width)), row_spec, row_spec, row_spec,
            whole((rows, LANES)), whole((rows, LANES)),
            pl.BlockSpec((groups, 1, shard, part), lambda t: (0, t, 0, 3)),
        ],
        out_specs=[
            pl.BlockSpec((groups, 1, shard, part), lambda t: (0, t, 0, 0)),
            row_spec, row_spec,
            pl.BlockSpec((blocks, half, 2 * LANES, 2 * LANES), lambda t: (0, t, 0, 0)),
            pl.BlockSpec((half, 2 * LANES, LANES), lambda t: (t, 0, 0)),
        ],
        out_shape=[
            jax.ShapeDtypeStruct((groups, halves, shard, part), BF16),
            full, full,
            jax.ShapeDtypeStruct((blocks, pairs, 2 * LANES, 2 * LANES), BF16),
            jax.ShapeDtypeStruct((pairs, 2 * LANES, LANES), BF16),
        ],
        compiler_params=params(),
        cost_estimate=cost(4 * rows * width * width, 16e6),
        name="unmix",
    )(first, mixed, rden, sq, cosines, sines, w)


def unattend_kernel(
    sq_ref, sk_ref, v_ref, gn_ref, gd_ref, cm_ref, cos_ref, sin_ref, st_ref, in_ref, lt_ref, gq_ref,
    query_ref, dk_ref, dv_ref, sum_ref,
):
    blocks, block, _ = cm_ref.shape
    piece = min(PIECE, block)
    masks = [lane_mask(block, head) for head in range(2)]
    ones = jnp.ones((block, LANES), BF16)
    incoming = expand(in_ref[0].astype(F32))
    sum_ref[...] = jnp.zeros_like(sum_ref)
    for place in range(blocks):
        start = place * block
        all_here = slice(start, start + block)
        keys, values = sk_ref[all_here, :], v_ref[all_here, :]
        sides = jnp.concatenate([values, ones], axis=1)
        key_sides = [keys * mask for mask in masks]
        state = incoming
        for earlier in range(place):
            state = state + st_ref[earlier, 0].astype(F32)
        state = state.astype(BF16)
        grad_keys = [None] * (block // piece)
        grad_values = [None] * (block // piece)
        for low in range(0, block, piece):
            here = slice(start + low, start + low + piece)
            span = low + piece
            queries, grads, slopes = sq_ref[here, :], gn_ref[here, :], gd_ref[here, :]
            grad_queries = None
            for head in range(2):
                mask = masks[head][:piece]
                cm = cm_ref[place, low : low + piece, :span]
                masked_queries, masked_grads = queries * mask, grads * mask
                scores = dot_nt(masked_queries, keys[:span])
                weights = (scores * cm).astype(BF16)
                back = dot_nt(
                    jnp.concatenate([masked_grads, slopes * mask], axis=1), sides[:span]
                )
                back = (back * cm).astype(BF16)
                term = dot(back, key_sides[head][:span])
                grad_queries = term if grad_queries is None else grad_queries + term
                key_term = dot_tn(back, masked_queries)
                value_term = dot_tn(weights, masked_grads)
                for piece_at in range(span // piece):
                    at = slice(piece_at * piece, (piece_at + 1) * piece)
                    old = grad_keys[piece_at]
                    grad_keys[piece_at] = key_term[at] if old is None else old + key_term[at]
                    old = grad_values[piece_at]
                    grad_values[piece_at] = value_term[at] if old is None else old + value_term[at]
            far = dot_nt(jnp.concatenate([grads, slopes], axis=1), state)
            grad_queries = (
                grad_queries
                + far[:, :LANES] * cos_ref[here, :]
                + far[:, LANES:] * sin_ref[here, :]
            ) * gq_ref[here, :].astype(F32)
            query_ref[here, :] = grad_queries.astype(BF16)
            sum_ref[0:1, :] += jnp.sum(grad_queries, axis=0, keepdims=True)
        grad_keys = jnp.concatenate(grad_keys, axis=0)
        grad_values = jnp.concatenate(grad_values, axis=0)
        for later in range(place + 1, blocks):
            far = dot_nt(sides, lt_ref[later, 0])
            grad_keys = (
                grad_keys
                + far[:, :LANES] * cos_ref[all_here, :]
                + far[:, LANES:] * sin_ref[all_here, :]
            )
            features = turned_features(keys, cos_ref[all_here, :], sin_ref[all_here, :])
            grad_values = grad_values + dot(features, lt_ref[later, 0][:, :LANES])
        dk_ref[all_here, :] = grad_keys
        dv_ref[all_here, :] = grad_values


def unattend(sq, sk, v, gn, gd, cm, cosines, sines, states, incoming, later, slope_q):
    rows, width = sq.shape
    pairs = width // LANES
    blocks = cm.shape[0]
    spec = pl.BlockSpec((rows, LANES), lambda p: (0, p))
    state_spec = pl.BlockSpec((blocks, 1, 2 * LANES, 2 * LANES), lambda p: (0, p, 0, 0))
    full = jax.ShapeDtypeStruct((rows, width), F32)
    return pl.pallas_call(
        unattend_kernel,
        grid=(pairs,),
        in_specs=[
            spec, spec, spec, spec, spec,
            whole(cm.shape), whole((rows, LANES)), whole((rows, LANES)),
            state_spec,
            pl.BlockSpec((1, 2 * LANES, LANES), lambda p: (p, 0, 0)),
            state_spec, spec,
        ],
        out_specs=[spec, spec, spec, pl.BlockSpec((8, LANES), lambda p: (0, p))],
        out_shape=[
            jax.ShapeDtypeStruct((rows, width), BF16), full, full,
            jax.ShapeDtypeStruct((8, width), F32),
        ],
        compiler_params=params(),
        cost_estimate=cost(20e9, 20e6),
        name="unattend",
    )(sq, sk, v, gn, gd, cm, cosines, sines, states, incoming, later, slope_q)


def tail_kernel(
    dk_ref, dv_ref, sk_ref, v_ref, gk_ref, cos_ref, sin_ref, in_ref, key_ref, value_ref, sum_ref,
):
    rows = dk_ref.shape[0]
    state = expand(in_ref[0].astype(F32)).astype(BF16)
    ones = jnp.ones((rows, LANES), BF16)
    far = dot_nt(jnp.concatenate([v_ref[...], ones], axis=1), state)
    cosines, sines = cos_ref[...], sin_ref[...]
    keys = (dk_ref[...] + far[:, :LANES] * cosines + far[:, LANES:] * sines) * gk_ref[...].astype(F32)
    values = dv_ref[...] + dot(turned_features(sk_ref[...], cosines, sines), state[:, :LANES])
    key_ref[...] = keys.astype(BF16)
    value_ref[...] = values.astype(BF16)
    sum_ref[...] = jnp.zeros_like(sum_ref)
    sum_ref[0:1, :] = jnp.sum(keys, axis=0, keepdims=True)
    sum_ref[1:2, :] = jnp.sum(values, axis=0, keepdims=True)


def tail(dk, dv, sk, v, slope_k, cosines, sines, incoming):
    rows, width = sk.shape
    pairs = width // LANES
    spec = pl.BlockSpec((rows, LANES), lambda p: (0, p))
    return pl.pallas_call(
        tail_kernel,
        grid=(pairs,),
        in_specs=[
            spec, spec, spec, spec, spec, whole((rows, LANES)), whole((rows, LANES)),
            pl.BlockSpec((1, 2 * LANES, LANES), lambda p: (p, 0, 0)),
        ],
        out_specs=[spec, spec, pl.BlockSpec((8, LANES), lambda p: (0, p))],
        out_shape=[
            jax.ShapeDtypeStruct((rows, width), BF16),
            jax.ShapeDtypeStruct((rows, width), BF16),
            jax.ShapeDtypeStruct((8, width), F32),
        ],
        compiler_params=params(),
        cost_estimate=cost(2e9, 14e6),
        name="tail",
    )(dk, dv, sk, v, slope_k, cosines, sines, incoming)


def weights_kernel(x_ref, q_ref, k_ref, v_ref, g_ref, turned_ref):
    @pl.when(pl.program_id(0) == 0)
    def _():
        turned_ref[...] = x_ref[...].T

    part = q_ref.shape[1]
    for place, ref in enumerate((q_ref, k_ref, v_ref)):
        product = dot(turned_ref[...], ref[...]).astype(BF16)
        g_ref[:, :, :, place * part : (place + 1) * part] = product.reshape(
            g_ref.shape[:3] + (part,)
        )


def weight_gradients(x, q, k, v, groups, halves, shard):
    rows, width = x.shape
    part = width // halves
    spec = pl.BlockSpec((rows, part), lambda t: (0, t))
    return pl.pallas_call(
        weights_kernel,
        grid=(halves,),
        in_specs=[whole((rows, width)), spec, spec, spec],
        out_specs=pl.BlockSpec((groups, 1, shard, 3 * part), lambda t: (0, t, 0, 0)),
        out_shape=jax.ShapeDtypeStruct((groups, halves, shard, 3 * part), BF16),
        scratch_shapes=[pltpu.VMEM((width, rows), BF16)],
        compiler_params=params(),
        cost_estimate=cost(2 * rows * width * 3 * width, 10e6),
        name="weight_gradients",
    )(x, q, k, v)


def inputs_kernel(first_ref, q_ref, k_ref, v_ref, w_ref, out_ref):
    halves = w_ref.shape[1]
    width = first_ref.shape[1]
    part = width // halves
    total = first_ref[...]
    for half in range(halves):
        side = w_ref[:, half].reshape(width, 3 * part)
        at = slice(half * part, (half + 1) * part)
        joined = jnp.concatenate([q_ref[:, at], k_ref[:, at], v_ref[:, at]], axis=1)
        total = total + dot_nt(joined, side)
    out_ref[...] = total.astype(BF16)


def input_gradient(first, q, k, v, w, step):
    rows, width = first.shape
    groups, halves, shard, _ = w.shape
    part = width // halves
    spec = pl.BlockSpec((step, width), lambda i: (i, 0))
    return pl.pallas_call(
        inputs_kernel,
        grid=(rows // step,),
        in_specs=[
            spec, spec, spec, spec,
            pl.BlockSpec((groups, halves, shard, 3 * part), lambda i: (0, 0, 0, 0)),
        ],
        out_specs=spec,
        out_shape=jax.ShapeDtypeStruct((rows, width), BF16),
        compiler_params=params(),
        cost_estimate=cost(2 * rows * width * 3 * width, 14e6),
        name="input_gradient",
    )(first, q, k, v, w)


def local(
    inputs, w_query, w_key, w_value, b_query, b_key, b_value, w_out, b_out, norm_gain, norm_shift,
    w_up, b_up, w_down, b_down, final_gain, final_shift, piece_starts, grad_output,
):
    rows, width = inputs.shape
    halves = lax.axis_size("tp")
    replicas = lax.axis_size("fsdp")
    length = rows * halves
    block = min(512, length)
    blocks = rows // block
    shard = width // replicas
    part = width // halves
    units = w_up.shape[1]
    me = lax.axis_index("tp")
    aligned = shard % 16 == 0
    groups, deep = (replicas, shard) if aligned else (1, width)

    places = me * rows + jnp.arange(rows, dtype=jnp.int32)
    flags = jnp.any(piece_starts[0][:, None] == (places // PIECE * PIECE)[None, :], axis=0)
    angle = 0.5 * jnp.pi / length * places.astype(F32)
    cosines, sines = jnp.cos(angle), jnp.sin(angle)
    at = jnp.arange(block, dtype=jnp.int32)
    allowed = (at[None, None, :] <= at[None, :, None]) | (
        (at[None, None, :] // PIECE == at[None, :, None] // PIECE)
        & flags.reshape(blocks, block)[:, :, None]
    )
    c, s = cosines.reshape(blocks, block), sines.reshape(blocks, block)
    cm = jnp.where(allowed, c[:, :, None] * c[:, None, :] + s[:, :, None] * s[:, None, :], 0.0)
    cosines = jnp.broadcast_to(cosines[:, None], (rows, LANES))
    sines = jnp.broadcast_to(sines[:, None], (rows, LANES))

    thin = jnp.concatenate(
        [b_query, b_key, b_value, b_up, b_out, norm_gain, norm_shift, b_down, final_gain, final_shift]
    )
    slots = thin.shape[0] // shard
    spare = LANES - slots - (1 if thin.shape[0] % shard else 0)
    thin = jnp.pad(thin, (0, (LANES - spare) * shard - thin.shape[0])).reshape(LANES - spare, shard).T
    thin = jnp.pad(thin, ((0, 0), (0, spare)))
    attention_shard = jnp.concatenate([w_query, w_key, w_value, w_out.T, thin], axis=1)
    forward_shard = jnp.concatenate([w_up, w_down.T], axis=1)

    def gather(piece):
        whole_piece = lax.all_gather(piece, BOTH, axis=0, tiled=False)
        whole_piece = whole_piece.reshape(replicas, halves, shard, piece.shape[1])
        if not aligned:
            whole_piece = jnp.moveaxis(whole_piece, 1, 0).reshape(1, halves, width, piece.shape[1])
        return whole_piece

    w_attention = gather(attention_shard)
    w_forward = gather(forward_shard)

    thin = w_attention[..., 4 * part : 4 * part + LANES - spare]
    thin = thin.reshape(replicas, halves, shard, LANES - spare) if aligned else jnp.moveaxis(
        thin.reshape(halves, replicas, shard, LANES - spare), 0, 1
    )
    thin = jnp.moveaxis(thin, 3, 2).reshape(replicas, halves, -1).astype(F32)
    edge = shard // halves
    starts = [0, edge, 2 * edge, 3 * edge]
    biases = jnp.stack(
        [
            jnp.moveaxis(thin[:, :, begin : begin + edge], 0, 1).reshape(halves, part)
            for begin in starts[:3]
        ],
        axis=1,
    )
    begin = 3 * edge
    bias_up = jnp.moveaxis(thin[:, :, begin : begin + units // replicas], 0, 1).reshape(1, halves * units)
    begin += units // replicas
    vectors = jnp.stack(
        [
            thin[:, 0, begin + place * shard : begin + (place + 1) * shard].reshape(width)
            for place in range(6)
        ]
    )
    vectors = jnp.pad(vectors, ((0, 2), (0, 0)))

    sq, sk, v, slope_q, slope_k, states, total = project(
        inputs, w_attention, biases, cosines, sines, block
    )
    incoming = lax.ppermute(total, "tp", [(i, i + 1) for i in range(halves - 1)])
    num, den = attend(sq, sk, v, cm, cosines, sines, states)
    mixed, rden, normal, scale, low = mix(
        num, den, sq, incoming, cosines, sines, w_attention, inputs, vectors, 256
    )
    act, slope, output, branch, second, sums_second = lift(
        low, w_forward, bias_up, normal, vectors, grad_output, 512
    )

    gdown, gup, gbias_up, first, first_low, sums_first = lower(
        branch, low, act, slope, w_forward, second, normal, scale, vectors, 512
    )
    gout, gn, gd, later, later_total = unmix(
        first_low, mixed, rden, sq, cosines, sines, w_attention, block
    )
    later_in = lax.ppermute(later_total, "tp", [(i + 1, i) for i in range(halves - 1)])
    query_low, dk, dv, sum_query = unattend(
        sq, sk, v, gn, gd, cm, cosines, sines, states, incoming, later, slope_q
    )
    key_low, value_low, sum_rest = tail(dk, dv, sk, v, slope_k, cosines, sines, later_in)
    gqkv = weight_gradients(inputs, query_low, key_low, value_low, groups, halves, deep)
    grad_inputs = input_gradient(first, query_low, key_low, value_low, w_attention, 256)

    def split_units(vector):
        return jnp.moveaxis(vector.reshape(halves, replicas, -1), 0, 1)

    def split_width(vector):
        return jnp.broadcast_to(vector.reshape(replicas, 1, shard), (replicas, halves, shard))

    thin = jnp.concatenate(
        [
            split_units(sum_query[0]), split_units(sum_rest[0]), split_units(sum_rest[1]),
            split_units(gbias_up[0]),
            split_width(sums_first[2]), split_width(sums_first[0]), split_width(sums_first[1]),
            split_width(sums_second[2]), split_width(sums_second[0]), split_width(sums_second[1]),
        ],
        axis=2,
    )
    size = thin.shape[2]
    thin = jnp.pad(thin, ((0, 0), (0, 0), (0, (LANES - spare) * shard - size)))
    thin = jnp.moveaxis(thin.reshape(replicas, halves, LANES - spare, shard), 2, 3)
    thin = jnp.pad(thin, ((0, 0), (0, 0), (0, 0), (0, spare))).astype(BF16)

    def spread(grad):
        if not aligned:
            grad = jnp.moveaxis(grad.reshape(halves, replicas, shard, grad.shape[3]), 0, 1)
        return grad

    def scatter(grad):
        grad = grad.reshape(replicas * halves, shard, grad.shape[3])
        return lax.psum_scatter(grad, BOTH, scatter_dimension=0, tiled=False)

    scaling = 1.0 / replicas
    gdown = scatter(spread(gdown)).astype(F32) * scaling
    gup = scatter(spread(gup)).astype(F32) * scaling
    rest = jnp.concatenate([spread(gqkv), spread(gout), thin], axis=3)
    rest = scatter(rest).astype(F32) * scaling
    thin = rest[:, 4 * part : 4 * part + LANES - spare].T.reshape(-1)
    cuts = [0, edge, 2 * edge, 3 * edge, 3 * edge + units // replicas]
    cuts += [cuts[-1] + shard * (place + 1) for place in range(6)]
    pieces = [thin[cuts[place] : cuts[place + 1]] for place in range(10)]
    return (
        output,
        grad_inputs,
        rest[:, :part],
        rest[:, part : 2 * part],
        rest[:, 2 * part : 3 * part],
        pieces[0],
        pieces[1],
        pieces[2],
        rest[:, 3 * part : 4 * part].T,
        pieces[4],
        pieces[5],
        pieces[6],
        gup,
        pieces[3],
        gdown.T,
        pieces[7],
        pieces[8],
        pieces[9],
    )


def solution(mesh):
    row = P(("fsdp", "tp"), None)
    split, turned = P("fsdp", "tp"), P("tp", "fsdp")
    thin, wide = P(("tp", "fsdp")), P("fsdp")
    return jax.shard_map(
        local,
        mesh=mesh,
        in_specs=(
            row, split, split, split, thin, thin, thin, turned, wide, wide, wide,
            split, thin, turned, wide, wide, wide, P("fsdp", None), row,
        ),
        out_specs=(
            row, row, split, split, split, thin, thin, thin, turned, wide, wide, wide,
            split, thin, turned, wide, wide, wide,
        ),
        check_vma=False,
    )
```

time: 1770 us -> 589 us (0.33)
  matrix products: 360 us -> 0 us
  blocking collectives: 354 us -> 0 us
  waiting for transfers between devices: 682 us -> 353 us
  Pallas kernels: 0 us -> 174 us
  local copies, waits for them, and re-layouts: 198 us -> 24.7 us
  other arithmetic: 137 us -> 16.3 us
    dot_general x99 -> x0, matrix products: 360 us -> none  [the longest x12 75.4 us: contract(): lax.dot_general(left, right, (((left_dim,), (right_dim,)), ((), ())), pre...]
    reduce_scatter x13 -> x3, waiting for transfers between devices: 521 us -> 251 us  [scatter(): return lax.psum_scatter(grad, BOTH, scatter_dimension=0, tiled=False)]
    unnamed x3 -> x0, blocking collectives: 185 us -> none
    pallas_call x0 -> x10, Pallas kernels: none -> 174 us  [the longest x1 42.4 us: lower(): pl.pallas_call(functools.partial(lower_kernel, step=256), grid=(halves *...]
    all_gather x8 -> x0, blocking collectives: 169 us -> none  [the longest x2 43.7 us: forward(): lax.all_gather(out_shard, 'fsdp', axis=1, tiled=True)]
    all_gather x10 -> x2, waiting for transfers between devices: 158 us -> 102 us  [gather(): whole_piece = lax.all_gather(piece, BOTH, axis=0, tiled=False)]
    reduce_sum x26 -> x0, other arithmetic: 55.4 us -> none  [the longest x1 18.7 us: local(): jnp.sum(grad_keys, axis=0)]
    unnamed x155 -> x13, local copies, waits for them, and re-layouts: 59.1 us -> 5.36 us
  transfers between devices with their start and end apart: 23 -> 7, of which waited for: 14 -> 5; matrix products, arithmetic and copies ran while one was open for 19% -> 4% of each run, Pallas kernels for 0% -> 17%
where the time goes in v1:
time: 589 us; the launch traced here: 588 us
  waiting for transfers between devices  353 us (60%)
  Pallas kernels  174 us (30%)
  local copies, waits for them, and re-layouts  24.7 us (4%)
  other arithmetic  16.3 us (3%)
  between operations  14.1 us (2%)
    reduce_scatter x3, waiting for transfers between devices, scatter(): return lax.psum_scatter(grad, BOTH, scatter_dimension=0, tiled=False)  251 us
    all_gather x2, waiting for transfers between devices, gather(): whole_piece = lax.all_gather(piece, BOTH, axis=0, tiled=False)  102 us
    pallas_call x1, Pallas kernels, lower(): pl.pallas_call(functools.partial(lower_kernel, step=256), grid=(halves *...  42.4 us
    pallas_call x1, Pallas kernels, lift(): pl.pallas_call(functools.partial(lift_kernel, step=256), grid=(halves * t...  31.4 us
    pallas_call x1, Pallas kernels, unattend(): pl.pallas_call(unattend_kernel, grid=(pairs,), in_specs=[spec, spec, spec...  23.3 us
    pallas_call x1, Pallas kernels, project(): pl.pallas_call(functools.partial(project_kernel, block=block, step=256),...  13.7 us
    pallas_call x1, Pallas kernels, unmix(): pl.pallas_call(functools.partial(unmix_kernel, block=block, step=256), gr...  12.6 us
    pallas_call x1, Pallas kernels, attend(): pl.pallas_call(attend_kernel, grid=(pairs,), in_specs=[spec, spec, spec,...  12.4 us
  transfers between devices with their start and end apart: 7, of which 5 were waited for; matrix products, arithmetic and copies ran while one was open for 4% of the time, Pallas kernels for 17%

profile of v1, /device:TPU:0, one launch (start us, length us, event | category | flops | bytes accessed | tf_op | source)
XLA Modules:
  0.0 587.7 jit_solution(2003118999520098289)
XLA Ops:
  7.2 6.8 %concatenate.16 = bf16[456]{0:T(512)(128)(2,1)S(1)} concatenate(bf16[24]{0:T(256)(128)(2,1)} %param.23, bf16[24]{0:T(256)(128)(2,1)} %param.24, bf16[24]{0:T(256)(128)(2,1)} %param.25, bf16[96]{0:T(256)(128)(2,1)} %param.31, bf16[48]{0:T(256)(128)(2,1)} %param.27, bf16[48]{0:T(256)(128)(2,1)} %param.28, bf16[48]{0:T(256)(128)(2,1)} %param.29, bf16[48]{0:T(256)(128)(2,1)} %param.33, ...), dimensions={0} | concatenate | bytes 1824 | tf_op jit(solution)/shard_map/concatenate | solution.py:799
  14.2 0.8 constant_dynamic-update-slice_fusion.2
  15.0 0.8 constant_dynamic-update-slice_fusion.1
  15.8 0.8 constant_dynamic-update-slice_fusion
  16.5 0.8 bitcast_dynamic-update-slice_fusion
  17.4 0.7 copy-done.3
  18.1 1.7 pad_maximum_fusion
  19.9 0.7 compare_reduce_fusion
  21.1 1.7 add_select_fusion.cm_ref
  22.8 62.9 %all-gather.5.cloned.1.call-done = bf16[1536,1664]{1,0:T(8,128)(2,1)} async-done(((bf16[48,1664]{1,0:T(8,128)(2,1)}), bf16[1536,1664]{1,0:T(8,128)(2,1)}) %all-gather.5.cloned.1.call-update) | async-done | bytes 5111824 | tf_op jit(solution)/shard_map/all_gather | solution.py:810
  85.7 1.1 convert_bitcast_fusion
  87.3 0.7 reshape.268.bias_ref
  89.0 0.6 pad_maximum_fusion.1.b_ref
  89.6 1.0 broadcast_in_dim.64.sin_ref
  90.6 1.0 broadcast_in_dim.32.cos_ref
  91.6 13.7 %project.1 = (bf16[1024,768]{1,0:T(8,128)(2,1)}, bf16[1024,768]{1,0:T(8,128)(2,1)}, bf16[1024,768]{1,0:T(8,128)(2,1)}, bf16[1024,768]{1,0:T(8,128)(2,1)}, bf16[1...) custom-call(bf16[1024,768]{1,0:T(8,128)(2,1)} %x_ref.5, ...), custom_call_target="tpu_custom_call" | custom-call | flops 3623878656 | bytes 16000000 | tf_op jit(solution)/shard_map/project/pallas_call | solution.py:138
  105.3 3.3 collective-permute-start
  108.7 0.6 pad.24.vec_ref
  109.3 12.4 %attend.1 = (f32[1024,768]{1,0:T(8,128)}, f32[1024,768]{1,0:T(8,128)}) custom-call(bf16[1024,768]{1,0:T(8,128)(2,1)} %get-tuple-element.56.sq_ref, bf16[1024,768]{1,0:T(8,128)(2,1)} %get-tuple-element.57.sk_ref, bf16[1024,768]{1,0:T(8,128)(2,1)} %get-tuple-element.58.v_ref, f32[2,512,512]{2,1,0:T(8,128)} %add_select_fusion.cm_ref, ...), custom_call_target="tpu_custom_call" | custom-call | flops 8000000000 | bytes 14000000 | tf_op jit(solution)/shard_map/attend/pallas_call | solution.py:197
  121.8 0.7 copy-done.2
  122.5 10.3 %mix.1 = (bf16[1024,768]{1,0:T(8,128)(2,1)}, f32[1024,768]{1,0:T(8,128)}, f32[1024,768]{1,0:T(8,128)}, f32[1024,128]{1,0:T(8,128)}, bf16[1024,768]{1,0:T(8,128)(2,1)}) custom-call(f32[1024,768]{1,0:T(8,128)} %get-tuple-element.60.num_ref, f32[1024,768]{1,0:T(8,128)} %get-tuple-element.61.den_ref, bf16[1024,768]{1,0:T(8,128)(2,1)} %get-tuple-element.56.sq_ref, ...), custom_call_target="tpu_custom_call" | custom-call | flops 2415919104 | bytes 20000000 | tf_op jit(solution)/shard_map/mix/pallas_call | solution.py:258
  132.8 39.3 %all-gather.7.cloned.1.call-done = bf16[1536,3072]{1,0:T(8,128)(2,1)} async-done(((bf16[48,3072]{1,0:T(8,128)(2,1)}), bf16[1536,3072]{1,0:T(8,128)(2,1)}) %all-gather.7.cloned.1.call-update) | async-done | bytes 9437200 | tf_op jit(solution)/shard_map/all_gather | solution.py:810
  172.1 31.4 %lift.1 = (bf16[1024,3072]{1,0:T(8,128)(2,1)}, bf16[1024,3072]{1,0:T(8,128)(2,1)}, bf16[1024,768]{1,0:T(8,128)(2,1)}, bf16[1024,768]{1,0:T(8,128)(2,1)}, f32[1024,768]{1,0:T(8,128)}, /*index=5*/f32[8,768]{1,0:T(8,128)}) custom-call(bf16[1024,768]{1,0:T(8,128)(2,1)} %get-tuple-element.63.low_ref, bf16[16,2,48,3072]{3,2,1,0:T(8,128)(2,1)} %bitcast.69, ...), custom_call_target="tpu_custom_call" | custom-call | flops 9663676416 | bytes 40000000 | tf_op jit(solution)/shard_map/lift/pallas_call | solution.py:351
  203.5 42.4 %lower.1 = (bf16[16,2,48,1536]{3,2,1,0:T(8,128)(2,1)}, bf16[16,2,48,1536]{3,2,1,0:T(8,128)(2,1)}, f32[8,3072]{1,0:T(8,128)}, f32[1024,768]{1,0:T(8,128)}, bf16[1024,768]{1,0:T(8,128)(2,1)}, /*index=5*/f32[8,768]{1,0:T(8,128)}) custom-call(bf16[1024,768]{1,0:T(8,128)(2,1)} %get-tuple-element.66.branch_ref, bf16[1024,768]{1,0:T(8,128)(2,1)} %get-tuple-element.63.low_ref, ...), custom_call_target="tpu_custom_call" | custom-call | flops 19327352832 | bytes 50000000 | tf_op jit(solution)/shard_map/lower/pallas_call | solution.py:452
  246.0 0.5 reduce-scatter.6.cloned.1.call-update
  246.7 12.6 %unmix.1 = (bf16[16,2,48,384]{3,2,1,0:T(8,128)(2,1)}, bf16[1024,768]{1,0:T(8,128)(2,1)}, bf16[1024,768]{1,0:T(8,128)(2,1)}, bf16[2,6,256,256]{3,2,1,0:T(8,128)(2,1)}, bf16[6,256,128]{2,1,0:T(8,128)(2,1)}) custom-call(bf16[1024,768]{1,0:T(8,128)(2,1)} %get-tuple-element.72.first_ref, bf16[1024,768]{1,0:T(8,128)(2,1)} %get-tuple-element.73.mixed_ref, ...), custom_call_target="tpu_custom_call" | custom-call | flops 2415919104 | bytes 16000000 | tf_op jit(solution)/shard_map/unmix/pallas_call | solution.py:541
  259.4 1.3 collective-permute-start.1
  260.7 23.3 %unattend.1 = (bf16[1024,768]{1,0:T(8,128)(2,1)}, f32[1024,768]{1,0:T(8,128)}, f32[1024,768]{1,0:T(8,128)}, f32[8,768]{1,0:T(8,128)}) custom-call(bf16[1024,768]{1,0:T(8,128)(2,1)} %get-tuple-element.56.sq_ref, bf16[1024,768]{1,0:T(8,128)(2,1)} %get-tuple-element.57.sk_ref, bf16[1024,768]{1,0:T(8,128)(2,1)} %get-tuple-element.58.v_ref, ...), custom_call_target="tpu_custom_call" | custom-call | flops 20000000000 | bytes 20000000 | tf_op jit(solution)/shard_map/unattend/pallas_call | solution.py:644
  284.0 0.9 fusion.2
  285.0 0.9 convert_reduce_fusion.3
  286.1 0.9 convert_reduce_fusion
  287.3 0.8 fusion.9
  288.2 0.7 copy-done.1
  288.9 9.4 %tail.1 = (bf16[1024,768]{1,0:T(8,128)(2,1)}, bf16[1024,768]{1,0:T(8,128)(2,1)}, f32[8,768]{1,0:T(8,128)}) custom-call(f32[1024,768]{1,0:T(8,128)} %get-tuple-element.80.dk_ref, f32[1024,768]{1,0:T(8,128)} %get-tuple-element.81.dv_ref, bf16[1024,768]{1,0:T(8,128)(2,1)} %get-tuple-element.57.sk_ref, bf16[1024,768]{1,0:T(8,128)(2,1)} %get-tuple-element.58.v_ref, ...), custom_call_target="tpu_custom_call" | custom-call | flops 2000000000 | bytes 14000000 | tf_op jit(solution)/shard_map/tail/pallas_call | solution.py:686
  298.4 0.7 convert.55
  300.0 9.7 %weight_gradients.1 = bf16[16,2,48,1152]{3,2,1,0:T(8,128)(2,1)} custom-call(bf16[1024,768]{1,0:T(8,128)(2,1)} %x_ref.5, bf16[1024,768]{1,0:T(8,128)(2,1)} %get-tuple-element.79.q_ref, bf16[1024,768]{1,0:T(8,128)(2,1)} %get-tuple-element.84.k_ref, bf16[1024,768]{1,0:T(8,128)(2,1)} %get-tuple-element.85.v_ref), custom_call_target="tpu_custom_call" | custom-call | flops 3623878656 | bytes 10000000 | tf_op jit(solution)/shard_map/weight_gradients/pallas_call | solution.py:722
  309.7 5.1 fusion.1
  314.8 8.8 %input_gradient.1 = bf16[1024,768]{1,0:T(8,128)(2,1)} custom-call(f32[1024,768]{1,0:T(8,128)} %get-tuple-element.71.first_ref, bf16[1024,768]{1,0:T(8,128)(2,1)} %get-tuple-element.79.q_ref, bf16[1024,768]{1,0:T(8,128)(2,1)} %get-tuple-element.84.k_ref, bf16[1024,768]{1,0:T(8,128)(2,1)} %get-tuple-element.85.v_ref, bf16[16,2,48,1664]{3,2,1,0:T(8,128)(2,1)} %bitcast.57), custom_call_target="tpu_custom_call" | custom-call | flops 3623878656 | bytes 14000000 | tf_op jit(solution)/shard_map/input_gradient/pallas_call | solution.py:753
  323.6 28.1 %reduce-scatter.8.cloned.1.call-done = bf16[1,48,1536]{2,1,0:T(8,128)(2,1)} async-done(((bf16[32,48,1536]{2,1,0:T(8,128)(2,1)}), bf16[1,48,1536]{2,1,0:T(8,128)(2,1)}) %reduce-scatter.8.cloned.1.call-update) | async-done | bytes 147472 | tf_op jit(solution)/shard_map/reduce_scatter | solution.py:897
  351.7 1.6 multiply_bitcast_fusion.1
  353.3 110.7 %reduce-scatter.6.cloned.1.call-done = bf16[1,48,1536]{2,1,0:T(8,128)(2,1)} async-done(((bf16[32,48,1536]{2,1,0:T(8,128)(2,1)}), bf16[1,48,1536]{2,1,0:T(8,128)(2,1)}) %reduce-scatter.6.cloned.1.call-update) | async-done | bytes 147472 | tf_op jit(solution)/shard_map/reduce_scatter | solution.py:897
  464.0 1.6 multiply_bitcast_fusion.2
  465.7 111.9 %reduce-scatter.4.cloned.1.call-done = bf16[1,48,1664]{2,1,0:T(8,128)(2,1)} async-done(((bf16[32,48,1664]{2,1,0:T(8,128)(2,1)}), bf16[1,48,1664]{2,1,0:T(8,128)(2,1)}) %reduce-scatter.4.cloned.1.call-update) | async-done | bytes 159760 | tf_op jit(solution)/shard_map/reduce_scatter | solution.py:897
  577.6 0.9 multiply_bitcast_fusion
  578.5 0.7 slice_bitcast_fusion
  579.4 0.6 slice.144
  580.0 0.6 fusion.17
  580.6 0.6 fusion.16
  (65 shorter events, 4.2 us)
Async XLA Ops:
  7.2 78.5 %all-gather.5.cloned.1.call-start = ((), (), s32[]{:S(2)}) async-start(), calls=%async_computation.6 | async-start | bytes 5271552 | tf_op jit(solution)/shard_map/all_gather | solution.py:810
  17.3 0.7 copy-start.3
  18.0 154.1 %all-gather.7.cloned.1.call-start = ((), (), s32[]{:S(2)}) async-start(), calls=%async_computation.7 | async-start | bytes 9732096 | tf_op jit(solution)/shard_map/all_gather | solution.py:810
  19.8 331.9 %reduce-scatter.8.cloned.1.call-start = ((), (), s32[]{:S(2)}) async-start(), calls=%async_computation.5 | async-start | bytes 4866048 | tf_op jit(solution)/shard_map/reduce_scatter | solution.py:897
  105.3 16.5 %collective-permute-start = (bf16[6,256,128]{2,1,0:T(8,128)(2,1)}, bf16[6,256,128]{2,1,0:T(8,128)(2,1)S(1)}, u32[]{:S(2)}, u32[]{:S(2)}) collective-permute-start(bf16[6,256,128]{2,1,0:T(8,128)(2,1)} %get-tuple-element.62), channel_id=1, source_target_pairs={{0,1},{2,3},{4,5},{6,7},{8,9},{10,11},{12,13},{14,15},{16,17},{18,... | collective-permute-start | bytes 1179656 | tf_op jit(solution)/shard_map/ppermute | solution.py:847
  121.8 0.7 copy-start.2
  245.9 218.1 %reduce-scatter.6.cloned.1.call-start = ((), (), s32[]{:S(2)}) async-start(), calls=%async_computation.4 | async-start | bytes 4866048 | tf_op jit(solution)/shard_map/reduce_scatter | solution.py:897
  246.5 331.1 %reduce-scatter.4.cloned.1.call-start = ((), (), s32[]{:S(2)}) async-start(), calls=%async_computation.3 | async-start | bytes 5271552 | tf_op jit(solution)/shard_map/reduce_scatter | solution.py:897
  259.4 28.8 %collective-permute-start.1 = (bf16[6,256,128]{2,1,0:T(8,128)(2,1)}, bf16[6,256,128]{2,1,0:T(8,128)(2,1)S(1)}, u32[]{:S(2)}, u32[]{:S(2)}) collective-permute-start(bf16[6,256,128]{2,1,0:T(8,128)(2,1)} %get-tuple-element.83), channel_id=1, source_target_pairs={{1,0},{3,2},{5,4},{7,6},{9,8},{11,10},{13,12},{15,14},{17,16},{19,... | collective-permute-start | bytes 1179656 | tf_op jit(solution)/shard_map/ppermute | solution.py:862
  288.2 0.7 copy-start.1
  300.0 9.7 %copy-start = (bf16[16,2,48,384]{3,2,1,0:T(8,128)(2,1)S(1)}, bf16[16,2,48,384]{3,2,1,0:T(8,128)(2,1)}, u32[]{:S(2)}) copy-start(bf16[16,2,48,384]{3,2,1,0:T(8,128)(2,1)} %get-tuple-element.86) | copy-start | bytes 3538948
Sparse Core Ops, SparseCore 0:
  18.2 67.5 all-gather.4
  89.2 82.8 all-gather.6
  246.1 105.5 reduce-scatter.7
  357.9 106.0 reduce-scatter.5
  469.4 108.0 reduce-scatter.3

commit v2 on v1

v2 whole, which is shorter than its diff:
```python
import functools
import math

import jax
import jax.numpy as jnp
from jax import lax
from jax.experimental import pallas as pl
from jax.experimental.pallas import tpu as pltpu
from jax.sharding import PartitionSpec as P

HEAD_DIM = 64
PIECE = 256
LANES = 128
EPSILON = 1e-05
F32 = jnp.float32
BF16 = jnp.bfloat16
BOTH = ("fsdp", "tp")


def dot(left, right):
    return lax.dot_general(left, right, (((1,), (0,)), ((), ())), preferred_element_type=F32)


def dot_nt(left, right):
    return lax.dot_general(left, right, (((1,), (1,)), ((), ())), preferred_element_type=F32)


def dot_tn(left, right):
    return lax.dot_general(left, right, (((0,), (0,)), ((), ())), preferred_element_type=F32)


def flat(ref):
    value = ref[...]
    return value.reshape(value.shape[0] * value.shape[1] * value.shape[2], value.shape[3])


def lane_mask(rows, head, dtype=BF16):
    lane = lax.broadcasted_iota(jnp.int32, (rows, LANES), 1)
    return (lane // HEAD_DIM == head).astype(F32).astype(dtype)


def same_head(rows, columns):
    row = lax.broadcasted_iota(jnp.int32, (rows, columns), 0)
    lane = lax.broadcasted_iota(jnp.int32, (rows, columns), 1)
    return (row // HEAD_DIM) % 2 == (lane // HEAD_DIM) % 2


def compact(state):
    left, right = state[:, :LANES], state[:, LANES:]
    row = lax.broadcasted_iota(jnp.int32, left.shape, 0)
    lane = lax.broadcasted_iota(jnp.int32, left.shape, 1)
    first = (row // HEAD_DIM) % 2 == 0
    low = lane < HEAD_DIM
    return jnp.where(
        low,
        jnp.where(first, left, pltpu.roll(left, HEAD_DIM, 1)),
        jnp.where(first, pltpu.roll(right, HEAD_DIM, 1), right),
    )


def expand(packed):
    row = lax.broadcasted_iota(jnp.int32, packed.shape, 0)
    lane = lax.broadcasted_iota(jnp.int32, packed.shape, 1)
    first = (row // HEAD_DIM) % 2 == 0
    low = lane < HEAD_DIM
    turned = pltpu.roll(packed, HEAD_DIM, 1)
    zero = jnp.zeros_like(packed)
    left = jnp.where(first & low, packed, jnp.where(~first & ~low, turned, zero))
    right = jnp.where(first & low, turned, jnp.where(~first & ~low, packed, zero))
    return jnp.concatenate([left, right], axis=1)


def turned_features(values, cosines, sines):
    wide = values.astype(F32)
    return jnp.concatenate([(wide * cosines).astype(BF16), (wide * sines).astype(BF16)], axis=1)


def slot(coords, z, y, c, x):
    across = jnp.where(c == 0, y ^ coords[1], x ^ coords[3])
    beside = jnp.where(c == 0, x ^ coords[1 + 2], y ^ coords[1])
    return across * 8 + beside * 4 + (z ^ coords[0])


def emit(product, half, outs, coords):
    if len(outs) == 1:
        outs[0][half] = product[...]
        return
    core = coords[2]
    shard = outs[0].shape[1]
    for group in range(product.shape[0] // (2 * shard)):
        z, y = group // 2, group % 2
        for out, c in zip(outs, (core, 1 - core)):
            begin = pl.multiple_of((2 * group + c) * shard, 16)
            out[slot(coords, z, y, c, half)] = product[pl.ds(begin, shard), :]


def scalars():
    return pl.BlockSpec(memory_space=pltpu.SMEM)


def params(megabytes=56):
    return pltpu.CompilerParams(vmem_limit_bytes=megabytes * 1024 * 1024)


def whole(shape):
    zeros = (0,) * len(shape)
    return pl.BlockSpec(shape, lambda *_: zeros)


def cost(flops, moved):
    return pl.CostEstimate(flops=int(flops), bytes_accessed=int(moved), transcendentals=0)


def after(value, *others):
    return lax.optimization_barrier((value, others))[0]


def pack_kernel(*refs):
    q_ref, k_ref, v_ref, out_ref, down_ref = refs[:5]
    thins = refs[5:-2]
    first_ref, turned_ref = refs[-2:]
    shard, part = q_ref.shape

    def chosen(columns, start):
        row = lax.broadcasted_iota(jnp.int32, (shard, columns), 0)
        column = lax.broadcasted_iota(jnp.int32, (shard, columns), 1)
        return (row + start == column).astype(F32).astype(BF16)

    for place, ref in enumerate((q_ref, k_ref, v_ref)):
        first_ref[:, place * part : (place + 1) * part] = ref[...]
    first_ref[:, 3 * part : 4 * part] = dot_nt(chosen(shard, 0), out_ref[...]).astype(BF16)
    turned_ref[...] = dot_nt(chosen(shard, 0), down_ref[...]).astype(BF16)
    columns = jnp.zeros((shard, LANES), F32)
    lane = 0
    for ref in thins:
        size = ref.shape[1]
        for start in range(0, size, shard):
            row = lax.broadcasted_iota(jnp.int32, (LANES, size), 0)
            spread = jnp.where(row == lane, ref[...].astype(F32), 0.0).astype(BF16)
            columns = columns + dot_nt(chosen(size, start), spread)
            lane += 1
    first_ref[:, 4 * part :] = columns.astype(BF16)


def pack(q, k, v, out, down, thins):
    shard, part = q.shape
    return pl.pallas_call(
        pack_kernel,
        out_shape=[
            jax.ShapeDtypeStruct((shard, 4 * part + LANES), BF16),
            jax.ShapeDtypeStruct((shard, down.shape[0]), BF16),
        ],
        compiler_params=params(),
        cost_estimate=cost(1e8, 1e6),
        name="pack",
    )(q, k, v, out, down, *[thin.reshape(1, -1) for thin in thins])


def unpack_kernel(thin_ref, bias_ref, up_ref, vec_ref, *, shard, edge, each):
    halves, width = thin_ref.shape[1], thin_ref.shape[2]
    for half in range(halves):
        thin = thin_ref[0, half]
        part = width // halves
        row = lax.broadcasted_iota(jnp.int32, (width, part), 0)
        column = lax.broadcasted_iota(jnp.int32, (width, part), 1)
        chosen = (row % shard < edge) & (row // shard * edge + row % shard == column)
        bias_ref[half] = dot_tn(thin, chosen.astype(F32).astype(BF16))[:8]
        units = each * width
        row = lax.broadcasted_iota(jnp.int32, (width, units), 0)
        column = lax.broadcasted_iota(jnp.int32, (width, units), 1)
        lane = lax.broadcasted_iota(jnp.int32, (LANES, units), 0)
        rows = jnp.zeros((8, units), F32)
        for turn in range(each):
            chosen = row // shard * (each * shard) + turn * shard + row % shard == column
            picked = dot_tn(thin, chosen.astype(F32).astype(BF16))
            picked = jnp.where(lane == 3 + turn, picked, 0.0)
            rows = rows + jnp.sum(picked, axis=0, keepdims=True)
        up_ref[half] = rows
    row = lax.broadcasted_iota(jnp.int32, (width, width), 0)
    column = lax.broadcasted_iota(jnp.int32, (width, width), 1)
    turned = dot_tn(thin_ref[0, 0], (row == column).astype(F32).astype(BF16))
    vec_ref[...] = turned[3 + each : 11 + each]


def unpack(w, shard, each):
    _, halves, width, columns = w.shape
    return pl.pallas_call(
        functools.partial(unpack_kernel, shard=shard, edge=shard // halves, each=each),
        grid=(1,),
        in_specs=[
            pl.BlockSpec((1, halves, width, LANES), lambda i: (0, 0, 0, columns // LANES - 1))
        ],
        out_specs=[
            whole((halves, 8, width // halves)), whole((halves, 8, each * width)), whole((8, width))
        ],
        out_shape=[
            jax.ShapeDtypeStruct((halves, 8, width // halves), F32),
            jax.ShapeDtypeStruct((halves, 8, each * width), F32),
            jax.ShapeDtypeStruct((8, width), F32),
        ],
        compiler_params=params(),
        cost_estimate=cost(1e8, 1e6),
        name="unpack",
    )(w)


def join_kernel(*refs):
    for place, ref in enumerate(refs[:-1]):
        refs[-1][place] = ref[...]


def join(parts):
    return pl.pallas_call(
        join_kernel,
        out_shape=jax.ShapeDtypeStruct((len(parts),) + parts[0].shape, parts[0].dtype),
        compiler_params=params(),
        cost_estimate=cost(0, 1e6),
        name="join",
    )(*parts)


def project_kernel(
    x_ref, w_ref, b_ref, cos_ref, sin_ref,
    sq_ref, sk_ref, v_ref, gq_ref, gk_ref, st_ref, tot_ref,
    *, block, step,
):
    rows = x_ref.shape[0]
    part = sq_ref.shape[1]
    weights = flat(w_ref)

    def body(index, carry):
        here = pl.ds(index * step, step)
        sums = dot(x_ref[here, :], weights)
        for place, (feature_ref, slope_ref) in enumerate(((sq_ref, gq_ref), (sk_ref, gk_ref))):
            value = sums[:, place * part : (place + 1) * part] + b_ref[0, place : place + 1, :]
            positive = jnp.maximum(value, 0.0) + jnp.log1p(jnp.exp(-jnp.abs(value)))
            feature_ref[here, :] = positive.astype(BF16)
            slope_ref[here, :] = jax.nn.sigmoid(value).astype(BF16)
        v_ref[here, :] = (sums[:, 2 * part :] + b_ref[0, 2:3, :]).astype(BF16)
        return carry

    lax.fori_loop(0, rows // step, body, 0)
    keep = same_head(2 * LANES, 2 * LANES)
    ones = jnp.ones((block, LANES), BF16)
    for pair in range(part // LANES):
        lanes = slice(pair * LANES, (pair + 1) * LANES)
        total = jnp.zeros((2 * LANES, 2 * LANES), F32)
        for place in range(rows // block):
            here = slice(place * block, (place + 1) * block)
            features = turned_features(sk_ref[here, lanes], cos_ref[here, :], sin_ref[here, :])
            state = dot_tn(features, jnp.concatenate([v_ref[here, lanes], ones], axis=1))
            state = jnp.where(keep, state, 0.0)
            st_ref[place, pair] = state.astype(BF16)
            total = total + state
        tot_ref[pair] = compact(total).astype(BF16)


def project(x, w, biases, cosines, sines, block):
    rows, width = x.shape
    groups, halves, shard, _ = w.shape
    part = width // halves
    pairs = width // LANES
    half = pairs // halves
    blocks = rows // block
    row_spec = pl.BlockSpec((rows, part), lambda t: (0, t))
    full = jax.ShapeDtypeStruct((rows, width), BF16)
    return pl.pallas_call(
        functools.partial(project_kernel, block=block, step=256),
        grid=(halves,),
        in_specs=[
            whole((rows, width)),
            pl.BlockSpec((groups, 1, shard, 3 * part), lambda t: (0, t, 0, 0)),
            pl.BlockSpec((1, 8, part), lambda t: (t, 0, 0)),
            whole((rows, LANES)),
            whole((rows, LANES)),
        ],
        out_specs=[
            row_spec, row_spec, row_spec, row_spec, row_spec,
            pl.BlockSpec((blocks, half, 2 * LANES, 2 * LANES), lambda t: (0, t, 0, 0)),
            pl.BlockSpec((half, 2 * LANES, LANES), lambda t: (t, 0, 0)),
        ],
        out_shape=[
            full, full, full, full, full,
            jax.ShapeDtypeStruct((blocks, pairs, 2 * LANES, 2 * LANES), BF16),
            jax.ShapeDtypeStruct((pairs, 2 * LANES, LANES), BF16),
        ],
        compiler_params=params(),
        cost_estimate=cost(2 * rows * width * 3 * width, 16e6),
        name="project",
    )(x, w, biases, cosines, sines)


def attend_kernel(sq_ref, sk_ref, v_ref, cm_ref, cos_ref, sin_ref, st_ref, num_ref, den_ref):
    blocks, block, _ = cm_ref.shape
    piece = min(PIECE, block)
    masks = [lane_mask(block, head) for head in range(2)]
    for place in range(blocks):
        start = place * block
        keys = sk_ref[start : start + block, :]
        values = v_ref[start : start + block, :]
        sides = [jnp.concatenate([values * mask, mask], axis=1) for mask in masks]
        for low in range(0, block, piece):
            here = slice(start + low, start + low + piece)
            span = low + piece
            queries = sq_ref[here, :]
            sums = None
            for mask, side in zip(masks, sides):
                scores = dot_nt(queries * mask[:piece], keys[:span])
                weights = (scores * cm_ref[place, low : low + piece, :span]).astype(BF16)
                term = dot(weights, side[:span])
                sums = term if sums is None else sums + term
            for earlier in range(place):
                sums = sums + dot(
                    turned_features(queries, cos_ref[here, :], sin_ref[here, :]), st_ref[earlier, 0]
                )
            num_ref[here, :] = sums[:, :LANES]
            den_ref[here, :] = sums[:, LANES:]


def attend(sq, sk, v, cm, cosines, sines, states):
    rows, width = sq.shape
    pairs = width // LANES
    blocks = cm.shape[0]
    spec = pl.BlockSpec((rows, LANES), lambda p: (0, p))
    full = jax.ShapeDtypeStruct((rows, width), F32)
    return pl.pallas_call(
        attend_kernel,
        grid=(pairs,),
        in_specs=[
            spec, spec, spec,
            whole(cm.shape), whole((rows, LANES)), whole((rows, LANES)),
            pl.BlockSpec((blocks, 1, 2 * LANES, 2 * LANES), lambda p: (0, p, 0, 0)),
        ],
        out_specs=[spec, spec],
        out_shape=[full, full],
        compiler_params=params(),
        cost_estimate=cost(8e9, 14e6),
        name="attend",
    )(sq, sk, v, cm, cosines, sines, states)


def norm_rows(values):
    average = jnp.mean(values, axis=1, keepdims=True)
    centred = values - average
    scale = lax.rsqrt(jnp.mean(centred * centred, axis=1, keepdims=True) + EPSILON)
    return centred * scale, scale


def mix_kernel(
    num_ref, den_ref, sq_ref, in_ref, cos_ref, sin_ref, w_ref, x_ref, vec_ref,
    mixed_ref, rden_ref, normal_ref, scale_ref, low_ref, wide_ref,
):
    pairs = in_ref.shape[0]
    halves = w_ref.shape[1]
    rows, width = x_ref.shape
    part = width // halves

    @pl.when(pl.program_id(0) == 0)
    def _():
        for pair in range(pairs):
            wide_ref[pair] = expand(in_ref[pair].astype(F32)).astype(BF16)

    for pair in range(pairs):
        lanes = slice(pair * LANES, (pair + 1) * LANES)
        sums = dot(turned_features(sq_ref[:, lanes], cos_ref[...], sin_ref[...]), wide_ref[pair])
        inverse = 1.0 / jnp.maximum(den_ref[:, lanes] + sums[:, LANES:], 1.0)
        rden_ref[:, lanes] = inverse
        mixed_ref[:, lanes] = ((num_ref[:, lanes] + sums[:, :LANES]) * inverse).astype(BF16)
    total = x_ref[...].astype(F32) + vec_ref[0:1, :]
    for half in range(halves):
        side = w_ref[:, half]
        side = side.reshape(width, part)
        total = total + dot_nt(mixed_ref[:, half * part : (half + 1) * part], side)
    normal, scale = norm_rows(total)
    normal_ref[...] = normal
    scale_ref[...] = jnp.broadcast_to(scale, scale_ref.shape)
    low_ref[...] = (normal * vec_ref[1:2, :] + vec_ref[2:3, :]).astype(BF16)


def mix(num, den, sq, incoming, cosines, sines, w, x, vectors, step):
    rows, width = x.shape
    groups, halves, shard, _ = w.shape
    part = width // halves
    pairs = incoming.shape[0]
    wide = pl.BlockSpec((step, width), lambda i: (i, 0))
    thin = pl.BlockSpec((step, LANES), lambda i: (i, 0))
    return pl.pallas_call(
        mix_kernel,
        grid=(rows // step,),
        in_specs=[
            wide, wide, wide, whole(incoming.shape), thin, thin,
            pl.BlockSpec((groups, halves, shard, part), lambda i: (0, 0, 0, 3)),
            wide, whole(vectors.shape),
        ],
        out_specs=[wide, wide, wide, thin, wide],
        out_shape=[
            jax.ShapeDtypeStruct((rows, width), BF16),
            jax.ShapeDtypeStruct((rows, width), F32),
            jax.ShapeDtypeStruct((rows, width), F32),
            jax.ShapeDtypeStruct((rows, LANES), F32),
            jax.ShapeDtypeStruct((rows, width), BF16),
        ],
        scratch_shapes=[pltpu.VMEM((pairs, 2 * LANES, 2 * LANES), BF16)],
        compiler_params=params(),
        cost_estimate=cost(2 * rows * width * width * 2, 20e6),
        name="mix",
    )(num, den, sq, incoming, cosines, sines, w, x, vectors)


def norm_back(upstream, normal, scale, gain):
    scaled = upstream * gain
    inner = (
        scaled
        - jnp.mean(scaled, axis=1, keepdims=True)
        - normal * jnp.mean(scaled * normal, axis=1, keepdims=True)
    )
    return inner * scale


def lift_kernel(low_ref, up_ref, bias_ref, act_ref, slope_ref, *, step):
    up = up_ref[0, 0]

    def body(place, carry):
        here = pl.ds(place * step, step)
        lifted = dot(low_ref[here, :], up) + bias_ref[0, 0:1, :]
        share = 0.5 + 0.5 * lax.erf(lifted * math.sqrt(0.5))
        bell = jnp.exp(-0.5 * lifted * lifted) * (1.0 / math.sqrt(2.0 * math.pi))
        act_ref[here, :] = (lifted * share).astype(BF16)
        slope_ref[here, :] = (share + lifted * bell).astype(BF16)
        return carry

    lax.fori_loop(0, low_ref.shape[0] // step, body, 0, unroll=True)


def lift(low, w, bias, half, units, tile):
    rows, width = low.shape
    tiles = units // tile
    unit_spec = pl.BlockSpec((rows, tile), lambda i: (0, i))
    shape = jax.ShapeDtypeStruct((rows, units), BF16)
    return pl.pallas_call(
        functools.partial(lift_kernel, step=256),
        grid=(tiles,),
        in_specs=[
            whole((rows, width)),
            pl.BlockSpec((1, 1, width, tile), lambda i: (0, half, 0, i)),
            pl.BlockSpec((1, 8, tile), lambda i: (half, 0, i)),
        ],
        out_specs=[unit_spec, unit_spec],
        out_shape=[shape, shape],
        compiler_params=params(),
        cost_estimate=cost(2 * rows * width * units, 10e6),
        name="lift",
    )(low, w, bias)


def drop_kernel(*refs):
    acts = refs[:-8]
    down_ref, normal_ref, vec_ref, grad_ref, out_ref, branch_ref, second_ref, sum_ref = refs[-8:]

    @pl.when(pl.program_id(0) == 0)
    def _():
        sum_ref[...] = jnp.zeros_like(sum_ref)

    total = normal_ref[...] * vec_ref[1:2, :] + vec_ref[2:3, :] + vec_ref[3:4, :]
    for half, act_ref in enumerate(acts):
        total = total + dot_nt(act_ref[...], down_ref[0, half])
    normal, scale = norm_rows(total)
    gain = vec_ref[4:5, :]
    out_ref[...] = (normal * gain + vec_ref[5:6, :]).astype(BF16)
    upstream = grad_ref[...].astype(F32)
    second = norm_back(upstream, normal, scale, gain)
    second_ref[...] = second
    branch_ref[...] = second.astype(BF16)
    sum_ref[0:1, :] += jnp.sum(upstream * normal, axis=0, keepdims=True)
    sum_ref[1:2, :] += jnp.sum(upstream, axis=0, keepdims=True)
    sum_ref[2:3, :] += jnp.sum(second, axis=0, keepdims=True)


def drop(act, w, normal, vectors, grad, units, step):
    rows, width = normal.shape
    halves = w.shape[1]
    wide = pl.BlockSpec((step, width), lambda i: (i, 0))
    return pl.pallas_call(
        drop_kernel,
        grid=(rows // step,),
        in_specs=[pl.BlockSpec((step, units), lambda i: (i, 0))] * halves
        + [whole((1, halves, width, units)), wide, whole(vectors.shape), wide],
        out_specs=[wide, wide, wide, whole((8, width))],
        out_shape=[
            jax.ShapeDtypeStruct((rows, width), BF16),
            jax.ShapeDtypeStruct((rows, width), BF16),
            jax.ShapeDtypeStruct((rows, width), F32),
            jax.ShapeDtypeStruct((8, width), F32),
        ],
        compiler_params=params(),
        cost_estimate=cost(2 * rows * width * halves * units, 20e6),
        name="drop",
    )(*act, w, normal, vectors, grad)


def piece_outputs(layout, tile, index_map):
    replicas, halves, shard, columns, pieces = layout[:5]
    if pieces:
        count = replicas * halves // 2
        spec = pl.BlockSpec((count, shard, tile), lambda *at: (0, 0, index_map(*at)))
        shape = jax.ShapeDtypeStruct((count, shard, columns), BF16)
        return [spec, spec], [shape, shape]
    width = replicas * shard
    spec = pl.BlockSpec((halves, width, tile), lambda *at: (0, 0, index_map(*at)))
    return [spec], [jax.ShapeDtypeStruct((halves, width, columns), BF16)]


def wide_gradient_kernel(coords_ref, left_ref, *refs, halves):
    rights, outs = refs[:halves], refs[halves:-2]
    turned_ref, product_ref = refs[-2:]
    coords = [coords_ref[place] for place in range(4)]

    @pl.when(pl.program_id(0) == 0)
    def _():
        turned_ref[...] = left_ref[...].T

    for half, right_ref in enumerate(rights):
        product_ref[...] = dot(turned_ref[...], right_ref[...]).astype(BF16)
        emit(product_ref, half, outs, coords)


def wide_gradient(coords, left, right, layout, units, tile, name):
    rows, width = left.shape
    halves = layout[1]
    tiles = units // tile
    out_specs, out_shapes = piece_outputs(layout, tile, lambda j: j)
    return pl.pallas_call(
        functools.partial(wide_gradient_kernel, halves=halves),
        grid=(tiles,),
        in_specs=[scalars(), whole((rows, width))]
        + [
            pl.BlockSpec((rows, tile), lambda j: (0, j)) for half in range(halves)
        ],
        out_specs=out_specs,
        out_shape=out_shapes,
        scratch_shapes=[pltpu.VMEM((width, rows), BF16), pltpu.VMEM((width, tile), BF16)],
        compiler_params=params(),
        cost_estimate=cost(2 * rows * width * halves * units, 18e6),
        name=name,
    )(coords, left, *right)


def bend_kernel(branch_ref, down_ref, slope_ref, gl_ref, gbias_ref, *, step):
    down = down_ref[0, 0]
    gbias_ref[...] = jnp.zeros_like(gbias_ref)

    def body(place, carry):
        here = pl.ds(place * step, step)
        slope = dot(branch_ref[here, :], down) * slope_ref[here, :].astype(F32)
        gbias_ref[0:1, :] += jnp.sum(slope, axis=0, keepdims=True)
        gl_ref[here, :] = slope.astype(BF16)
        return carry

    lax.fori_loop(0, branch_ref.shape[0] // step, body, 0, unroll=True)


def bend(branch, w, slope, half, units, tile):
    rows, width = branch.shape
    tiles = units // tile
    unit_spec = pl.BlockSpec((rows, tile), lambda i: (0, i))
    return pl.pallas_call(
        functools.partial(bend_kernel, step=256),
        grid=(tiles,),
        in_specs=[
            whole((rows, width)),
            pl.BlockSpec((1, 1, width, tile), lambda i: (0, half, 0, i)),
            unit_spec,
        ],
        out_specs=[unit_spec, pl.BlockSpec((8, tile), lambda i: (0, i))],
        out_shape=[
            jax.ShapeDtypeStruct((rows, units), BF16),
            jax.ShapeDtypeStruct((8, units), F32),
        ],
        compiler_params=params(),
        cost_estimate=cost(2 * rows * width * units, 10e6),
        name="bend",
    )(branch, w, slope)


def lower_kernel(*refs):
    gls = refs[:-8]
    up_ref, second_ref, normal_ref, scale_ref, vec_ref, first_ref, firstlow_ref, sum_ref = refs[-8:]

    @pl.when(pl.program_id(0) == 0)
    def _():
        sum_ref[...] = jnp.zeros_like(sum_ref)

    upstream = second_ref[...]
    for half, gl_ref in enumerate(gls):
        upstream = upstream + dot_nt(gl_ref[...], up_ref[0, half])
    normal = normal_ref[...]
    first = norm_back(upstream, normal, scale_ref[:, 0:1], vec_ref[1:2, :])
    first_ref[...] = first
    firstlow_ref[...] = first.astype(BF16)
    sum_ref[0:1, :] += jnp.sum(upstream * normal, axis=0, keepdims=True)
    sum_ref[1:2, :] += jnp.sum(upstream, axis=0, keepdims=True)
    sum_ref[2:3, :] += jnp.sum(first, axis=0, keepdims=True)


def lower(gl, w, second, normal, scale, vectors, units, step):
    rows, width = second.shape
    halves = w.shape[1]
    wide = pl.BlockSpec((step, width), lambda i: (i, 0))
    return pl.pallas_call(
        lower_kernel,
        grid=(rows // step,),
        in_specs=[pl.BlockSpec((step, units), lambda i: (i, 0))] * halves
        + [
            whole((1, halves, width, units)), wide, wide,
            pl.BlockSpec((step, LANES), lambda i: (i, 0)), whole(vectors.shape),
        ],
        out_specs=[wide, wide, whole((8, width))],
        out_shape=[
            jax.ShapeDtypeStruct((rows, width), F32),
            jax.ShapeDtypeStruct((rows, width), BF16),
            jax.ShapeDtypeStruct((8, width), F32),
        ],
        compiler_params=params(),
        cost_estimate=cost(2 * rows * width * halves * units, 20e6),
        name="lower",
    )(*gl, w, second, normal, scale, vectors)


def unmix_kernel(
    coords_ref, first_ref, mixed_ref, rden_ref, sq_ref, cos_ref, sin_ref, w_ref,
    sum1_ref, sum2_ref, *refs, block, step, shard, halves
):
    biases = [ref[0:1, :] for ref in refs[:halves]]
    refs = refs[halves:]
    refs = refs[(len(refs) - 5) // 2 :]
    bias = biases[0]
    for half in range(1, halves):
        bias = jnp.where(pl.program_id(0) == half, biases[half], bias)
    bias = jnp.broadcast_to(bias, (8, bias.shape[1]))
    outs = refs[:-5]
    gn_ref, gd_ref, st_ref, tot_ref, product_ref = refs[-5:]
    coords = [coords_ref[place] for place in range(4)]
    rows, width = first_ref.shape
    part = mixed_ref.shape[1]
    side = flat(w_ref)
    group_row = lax.broadcasted_iota(jnp.int32, (LANES, LANES), 0)
    group_lane = lax.broadcasted_iota(jnp.int32, (LANES, LANES), 1)
    group = (group_row // HEAD_DIM == group_lane // HEAD_DIM).astype(F32).astype(BF16)
    lane = lax.broadcasted_iota(jnp.int32, (step, LANES), 1) % HEAD_DIM

    def body(place, carry):
        here = pl.ds(place * step, step)
        grad = dot(first_ref[here, :], side)
        for pair in range(part // LANES):
            lanes = slice(pair * LANES, (pair + 1) * LANES)
            inverse = rden_ref[here, lanes]
            scaled = grad[:, lanes] * inverse
            product = scaled * mixed_ref[here, lanes].astype(F32)
            high = product.astype(BF16)
            rest = (product - high.astype(F32)).astype(BF16)
            inner = dot(high, group) + dot(rest, group)
            slope = jnp.where(inverse < 1.0, -inner, 0.0)
            high = slope.astype(BF16).astype(F32)
            gn_ref[here, lanes] = scaled.astype(BF16)
            gd_ref[here, lanes] = jnp.where(
                lane == 0, high, jnp.where(lane == 1, slope - high, 0.0)
            ).astype(BF16)
        return carry

    lax.fori_loop(0, rows // step, body, 0)
    product_ref[:, :part] = dot_tn(first_ref[...], mixed_ref[...]).astype(BF16)
    side_row = lax.broadcasted_iota(jnp.int32, (8, LANES), 0)
    side_lane = lax.broadcasted_iota(jnp.int32, (8, LANES), 1)

    def pick(first_lane, count):
        chosen = (side_row < count) & (side_row + first_lane == side_lane)
        return chosen.astype(F32).astype(BF16)

    columns = dot_tn(sum1_ref[...].astype(BF16), pick(0, 3))
    columns = columns + dot_tn(sum2_ref[...].astype(BF16), pick(3, 3))
    turned = dot_tn(bias.astype(BF16), (side_row == 0).astype(F32).astype(BF16)).astype(BF16)
    each = bias.shape[1] // width
    row = lax.broadcasted_iota(jnp.int32, (width, each * width), 0)
    column = lax.broadcasted_iota(jnp.int32, (width, each * width), 1)
    for turn in range(each):
        source = row // shard * (each * shard) + turn * shard + row % shard
        chosen = (source == column).astype(F32).astype(BF16)
        lane_at = lax.broadcasted_iota(jnp.int32, (width, LANES), 1)
        columns = jnp.where(lane_at == 6 + turn, dot(chosen, turned), columns)
    product_ref[:, part:] = columns.astype(BF16)
    emit(product_ref, pl.program_id(0), outs, coords)
    keep = same_head(2 * LANES, 2 * LANES)
    for pair in range(part // LANES):
        lanes = slice(pair * LANES, (pair + 1) * LANES)
        total = jnp.zeros((2 * LANES, 2 * LANES), F32)
        for place in range(rows // block):
            here = slice(place * block, (place + 1) * block)
            features = turned_features(sq_ref[here, lanes], cos_ref[here, :], sin_ref[here, :])
            state = dot_tn(
                features, jnp.concatenate([gn_ref[here, lanes], gd_ref[here, lanes]], axis=1)
            )
            state = jnp.where(keep, state, 0.0)
            st_ref[place, pair] = state.astype(BF16)
            total = total + state
        tot_ref[pair] = compact(total).astype(BF16)


def unmix(
    coords, first, mixed, rden, sq, cosines, sines, w, sums1, sums2, gbias, partial, layout, block
):
    rows, width = first.shape
    groups, halves, shard, _ = w.shape
    part = width // halves
    pairs = width // LANES
    half = pairs // halves
    blocks = rows // block
    row_spec = pl.BlockSpec((rows, part), lambda t: (0, t))
    tile = part + LANES
    out_specs, out_shapes = piece_outputs(layout, tile, lambda t: layout[3] // tile - 1)
    units = gbias[0].shape[1]
    full = jax.ShapeDtypeStruct((rows, width), BF16)
    return pl.pallas_call(
        functools.partial(
            unmix_kernel, block=block, step=256, shard=layout[2], halves=halves
        ),
        grid=(halves,),
        in_specs=[
            scalars(), whole((rows, width)), row_spec, row_spec, row_spec,
            whole((rows, LANES)), whole((rows, LANES)),
            pl.BlockSpec((groups, 1, shard, part), lambda t: (0, t, 0, 3)),
            whole((8, width)), whole((8, width)),
        ]
        + [whole((8, units))] * halves
        + [pl.BlockSpec(memory_space=pl.ANY)] * len(partial),
        input_output_aliases={10 + halves + at: at for at in range(len(partial))},
        out_specs=out_specs
        + [
            row_spec, row_spec,
            pl.BlockSpec((blocks, half, 2 * LANES, 2 * LANES), lambda t: (0, t, 0, 0)),
            pl.BlockSpec((half, 2 * LANES, LANES), lambda t: (t, 0, 0)),
        ],
        out_shape=out_shapes
        + [
            full, full,
            jax.ShapeDtypeStruct((blocks, pairs, 2 * LANES, 2 * LANES), BF16),
            jax.ShapeDtypeStruct((pairs, 2 * LANES, LANES), BF16),
        ],
        scratch_shapes=[pltpu.VMEM((width, tile), BF16)],
        compiler_params=params(),
        cost_estimate=cost(4 * rows * width * width, 16e6),
        name="unmix",
    )(coords, first, mixed, rden, sq, cosines, sines, w, sums1, sums2, *gbias, *partial)


def unattend_kernel(
    sq_ref, sk_ref, v_ref, gn_ref, gd_ref, cm_ref, cos_ref, sin_ref, st_ref, in_ref, lt_ref, gq_ref,
    *refs,
):
    query_ref, dk_ref, dv_ref = refs[-3:]
    blocks, block, _ = cm_ref.shape
    piece = min(PIECE, block)
    masks = [lane_mask(block, head) for head in range(2)]
    ones = jnp.ones((block, LANES), BF16)
    incoming = expand(in_ref[0].astype(F32))
    for place in range(blocks):
        start = place * block
        all_here = slice(start, start + block)
        keys, values = sk_ref[all_here, :], v_ref[all_here, :]
        sides = jnp.concatenate([values, ones], axis=1)
        key_sides = [keys * mask for mask in masks]
        state = incoming
        for earlier in range(place):
            state = state + st_ref[earlier, 0].astype(F32)
        state = state.astype(BF16)
        grad_keys = [None] * (block // piece)
        grad_values = [None] * (block // piece)
        for low in range(0, block, piece):
            here = slice(start + low, start + low + piece)
            span = low + piece
            queries, grads, slopes = sq_ref[here, :], gn_ref[here, :], gd_ref[here, :]
            grad_queries = None
            for head in range(2):
                mask = masks[head][:piece]
                cm = cm_ref[place, low : low + piece, :span]
                masked_queries, masked_grads = queries * mask, grads * mask
                scores = dot_nt(masked_queries, keys[:span])
                weights = (scores * cm).astype(BF16)
                back = dot_nt(
                    jnp.concatenate([masked_grads, slopes * mask], axis=1), sides[:span]
                )
                back = (back * cm).astype(BF16)
                term = dot(back, key_sides[head][:span])
                grad_queries = term if grad_queries is None else grad_queries + term
                key_term = dot_tn(back, masked_queries)
                value_term = dot_tn(weights, masked_grads)
                for piece_at in range(span // piece):
                    at = slice(piece_at * piece, (piece_at + 1) * piece)
                    old = grad_keys[piece_at]
                    grad_keys[piece_at] = key_term[at] if old is None else old + key_term[at]
                    old = grad_values[piece_at]
                    grad_values[piece_at] = value_term[at] if old is None else old + value_term[at]
            far = dot_nt(jnp.concatenate([grads, slopes], axis=1), state)
            grad_queries = (
                grad_queries
                + far[:, :LANES] * cos_ref[here, :]
                + far[:, LANES:] * sin_ref[here, :]
            ) * gq_ref[here, :].astype(F32)
            query_ref[here, :] = grad_queries.astype(BF16)
        grad_keys = jnp.concatenate(grad_keys, axis=0)
        grad_values = jnp.concatenate(grad_values, axis=0)
        for later in range(place + 1, blocks):
            far = dot_nt(sides, lt_ref[later, 0])
            grad_keys = (
                grad_keys
                + far[:, :LANES] * cos_ref[all_here, :]
                + far[:, LANES:] * sin_ref[all_here, :]
            )
            features = turned_features(keys, cos_ref[all_here, :], sin_ref[all_here, :])
            grad_values = grad_values + dot(features, lt_ref[later, 0][:, :LANES])
        dk_ref[all_here, :] = grad_keys
        dv_ref[all_here, :] = grad_values


def unattend(
    sq, sk, v, gn, gd, cm, cosines, sines, states, incoming, later, slope_q, start, count, partial
):
    rows, width = sq.shape
    blocks = cm.shape[0]
    spec = pl.BlockSpec((rows, LANES), lambda p: (0, start + p))
    state_spec = pl.BlockSpec((blocks, 1, 2 * LANES, 2 * LANES), lambda p: (0, start + p, 0, 0))
    full = jax.ShapeDtypeStruct((rows, width), F32)
    return pl.pallas_call(
        unattend_kernel,
        grid=(count,),
        in_specs=[
            spec, spec, spec, spec, spec,
            whole(cm.shape), whole((rows, LANES)), whole((rows, LANES)),
            state_spec,
            pl.BlockSpec((1, 2 * LANES, LANES), lambda p: (start + p, 0, 0)),
            state_spec, spec,
        ]
        + [pl.BlockSpec(memory_space=pl.ANY)] * len(partial),
        out_specs=[spec, spec, spec],
        out_shape=[jax.ShapeDtypeStruct((rows, width), BF16), full, full],
        input_output_aliases={12 + at: at for at in range(len(partial))},
        compiler_params=params(),
        cost_estimate=cost(20e9, 20e6),
        name="unattend",
    )(sq, sk, v, gn, gd, cm, cosines, sines, states, incoming, later, slope_q, *partial)


def finish_kernel(
    coords_ref, x_ref, q_ref, dk_ref, dv_ref, sk_ref, v_ref, gk_ref, cos_ref, sin_ref, in_ref,
    *refs, shard
):
    outs = refs[:-4]
    key_ref, value_ref, turned_ref, product_ref = refs[-4:]
    coords = [coords_ref[place] for place in range(4)]
    rows, part = q_ref.shape
    width = x_ref.shape[1]

    @pl.when(pl.program_id(0) == 0)
    def _():
        turned_ref[...] = x_ref[...].T

    product_ref[:, :part] = dot(turned_ref[...], q_ref[...]).astype(BF16)
    ones = jnp.ones((rows, LANES), BF16)
    cosines, sines = cos_ref[...], sin_ref[...]
    for pair in range(part // LANES):
        lanes = slice(pair * LANES, (pair + 1) * LANES)
        state = expand(in_ref[pair].astype(F32)).astype(BF16)
        far = dot_nt(jnp.concatenate([v_ref[:, lanes], ones], axis=1), state)
        keys = dk_ref[:, lanes] + far[:, :LANES] * cosines + far[:, LANES:] * sines
        key_ref[:, lanes] = (keys * gk_ref[:, lanes].astype(F32)).astype(BF16)
        features = turned_features(sk_ref[:, lanes], cosines, sines)
        value_ref[:, lanes] = (dv_ref[:, lanes] + dot(features, state[:, :LANES])).astype(BF16)
    product_ref[:, part : 2 * part] = dot(turned_ref[...], key_ref[...]).astype(BF16)
    product_ref[:, 2 * part : 3 * part] = dot(turned_ref[...], value_ref[...]).astype(BF16)
    lane = lax.broadcasted_iota(jnp.int32, (part, LANES), 1)
    sums = jnp.zeros((part, LANES), F32)
    for place, ref in enumerate((q_ref, key_ref, value_ref)):
        sums = jnp.where(lane == place, dot_tn(ref[...], ones), sums)
    edge = shard * part // width
    row = lax.broadcasted_iota(jnp.int32, (width, part), 0)
    column = lax.broadcasted_iota(jnp.int32, (width, part), 1)
    source = row // shard * edge + row % shard
    chosen = (row % shard < edge) & (source == column)
    product_ref[:, 3 * part :] = dot(chosen.astype(F32).astype(BF16), sums.astype(BF16)).astype(BF16)
    emit(product_ref, pl.program_id(0), outs, coords)


def finish(coords, x, q, dk, dv, sk, v, slope_k, cosines, sines, incoming, layout):
    rows, width = x.shape
    halves, shard = layout[1], layout[2]
    part = width // halves
    half = incoming.shape[0] // halves
    spec = pl.BlockSpec((rows, part), lambda t: (0, t))
    full = jax.ShapeDtypeStruct((rows, width), BF16)
    out_specs, out_shapes = piece_outputs(layout, layout[3], lambda t: 0)
    return pl.pallas_call(
        functools.partial(finish_kernel, shard=shard),
        grid=(halves,),
        in_specs=[
            scalars(), whole((rows, width)), spec, spec, spec, spec, spec, spec,
            whole((rows, LANES)), whole((rows, LANES)),
            pl.BlockSpec((half, 2 * LANES, LANES), lambda t: (t, 0, 0)),
        ],
        out_specs=out_specs + [spec, spec],
        out_shape=out_shapes + [full, full],
        scratch_shapes=[pltpu.VMEM((width, rows), BF16), pltpu.VMEM((width, layout[3]), BF16)],
        compiler_params=params(),
        cost_estimate=cost(2 * rows * width * 3 * width, 10e6),
        name="finish",
    )(coords, x, q, dk, dv, sk, v, slope_k, cosines, sines, incoming)


def inputs_kernel(first_ref, q_ref, k_ref, v_ref, w_ref, out_ref):
    halves = w_ref.shape[1]
    width = first_ref.shape[1]
    part = width // halves
    total = first_ref[...]
    for half in range(halves):
        side = w_ref[:, half].reshape(width, 3 * part)
        at = slice(half * part, (half + 1) * part)
        joined = jnp.concatenate([q_ref[:, at], k_ref[:, at], v_ref[:, at]], axis=1)
        total = total + dot_nt(joined, side)
    out_ref[...] = total.astype(BF16)


def input_gradient(first, q, k, v, w, step):
    rows, width = first.shape
    groups, halves, shard, _ = w.shape
    part = width // halves
    spec = pl.BlockSpec((step, width), lambda i: (i, 0))
    return pl.pallas_call(
        inputs_kernel,
        grid=(rows // step,),
        in_specs=[
            spec, spec, spec, spec,
            pl.BlockSpec((groups, halves, shard, 3 * part), lambda i: (0, 0, 0, 0)),
        ],
        out_specs=spec,
        out_shape=jax.ShapeDtypeStruct((rows, width), BF16),
        compiler_params=params(),
        cost_estimate=cost(2 * rows * width * 3 * width, 14e6),
        name="input_gradient",
    )(first, q, k, v, w)


def assemble_kernel(coords_ref, own_ref, other_ref, out_ref, sems):
    coords = [coords_ref[place] for place in range(4)]
    count, shard, _ = own_ref.shape
    copies = []
    for side, ref in enumerate((own_ref, other_ref)):
        c = coords[2] if side == 0 else 1 - coords[2]
        for index in range(count):
            across, beside, z = index // 8, index // 4 % 2, (index % 4) ^ coords[0]
            y = coords[1] ^ jnp.where(c == 0, across, beside)
            x = coords[3] ^ jnp.where(c == 0, beside, across)
            begin = pl.multiple_of((z * 4 + y * 2 + c) * shard, 16)
            copy = pltpu.make_async_copy(
                ref.at[index],
                out_ref.at[0, x, pl.ds(begin, shard), :],
                sems.at[side * count + index],
            )
            copy.start()
            copies.append(copy)
    for copy in copies:
        copy.wait()


def assemble(coords, own, other):
    count, shard, columns = own.shape
    return pl.pallas_call(
        assemble_kernel,
        in_specs=[
            scalars(), pl.BlockSpec(memory_space=pl.ANY), pl.BlockSpec(memory_space=pl.ANY)
        ],
        out_specs=pl.BlockSpec(memory_space=pltpu.VMEM),
        out_shape=jax.ShapeDtypeStruct((1, 2, count * shard, columns), BF16),
        scratch_shapes=[pltpu.SemaphoreType.DMA((2 * count,))],
        compiler_params=params(),
        cost_estimate=cost(0, 4 * count * shard * columns * 2),
        name="assemble",
    )(coords, own, other)


def moves():
    def table(change):
        pairs = []
        for source in range(32):
            z, y, c, x = source // 8, source // 4 % 2, source // 2 % 2, source % 2
            z, y, c, x = change(z, y, c, x)
            pairs.append((source, ((z * 2 + y) * 2 + c) * 2 + x))
        return pairs

    along = [table(lambda z, y, c, x, k=k: (z ^ k, y, c, x)) for k in range(4)]
    beside = table(lambda z, y, c, x: (z, y ^ c, c, x ^ 1 ^ c))
    across = table(lambda z, y, c, x: (z, y ^ 1 ^ c, c, x ^ c))
    core = table(lambda z, y, c, x: (z, y, c ^ 1, x))
    return along, beside, across, core


def add(left, right):
    return (left.astype(F32) + right.astype(F32)).astype(BF16)


def send(value, table, begin, end, axes=BOTH):
    value = after(value, *begin) if begin else value
    value = lax.ppermute(value, axes, table)
    return after(value, *end) if end else value


class Gather:
    def __init__(self, piece):
        self.tables = moves()
        self.held = piece

    def line(self, begin=(), end=()):
        parts = [send(self.held, self.tables[0][k], begin, end) for k in (1, 2, 3)]
        self.held = join([self.held] + parts)

    def beside(self, begin=(), end=()):
        self.held = jnp.concatenate([self.held, send(self.held, self.tables[1], begin, end)], axis=0)

    def across(self, begin=(), end=()):
        self.held = jnp.concatenate([self.held, send(self.held, self.tables[2], begin, end)], axis=0)

    def core(self, coords, begin=(), end=()):
        return assemble(coords, self.held, send(self.held, self.tables[3], begin, end))


class Sum:
    def __init__(self, own, other):
        self.tables = moves()
        self.kept, self.sent = own, other

    def fold(self, table, begin, end):
        arrived = send(self.sent, table, begin, end)
        size = self.kept.shape[0] // 2
        kept = add(self.kept[:size], arrived[:size])
        self.kept, self.sent = kept, add(self.kept[size:], arrived[size:])

    def both(self):
        return [self.kept, self.sent]

    def core(self, begin=(), end=()):
        self.fold(self.tables[3], begin, end)

    def across(self, begin=(), end=()):
        self.fold(self.tables[2], begin, end)

    def beside(self, begin=(), end=()):
        arrived = send(self.sent, self.tables[1], begin, end)
        self.parts = [add(self.kept[k], arrived[k]) for k in range(4)]

    def line(self, begin=(), end=()):
        parts = [send(self.parts[k], self.tables[0][k], begin, end) for k in (1, 2, 3)]
        total = self.parts[0].astype(F32)
        for part in parts:
            total = total + part.astype(F32)
        return total


def local(
    inputs, w_query, w_key, w_value, b_query, b_key, b_value, w_out, b_out, norm_gain, norm_shift,
    w_up, b_up, w_down, b_down, final_gain, final_shift, piece_starts, grad_output,
):
    rows, width = inputs.shape
    halves = lax.axis_size("tp")
    replicas = lax.axis_size("fsdp")
    length = rows * halves
    block = min(512, length)
    blocks = rows // block
    shard = width // replicas
    part = width // halves
    units = w_up.shape[1]
    me = lax.axis_index("tp")
    pieces = replicas == 16 and halves == 2 and shard % 16 == 0
    place = lax.axis_index("fsdp")
    coords = jnp.stack([place // 4, place // 2 % 2, place % 2, me]).astype(jnp.int32)

    def layout(columns):
        return replicas, halves, shard, columns, pieces

    places = me * rows + jnp.arange(rows, dtype=jnp.int32)
    flags = jnp.any(piece_starts[0][:, None] == (places // PIECE * PIECE)[None, :], axis=0)
    angle = 0.5 * jnp.pi / length * places.astype(F32)
    cosines, sines = jnp.cos(angle), jnp.sin(angle)
    at = jnp.arange(block, dtype=jnp.int32)
    allowed = (at[None, None, :] <= at[None, :, None]) | (
        (at[None, None, :] // PIECE == at[None, :, None] // PIECE)
        & flags.reshape(blocks, block)[:, :, None]
    )
    c, s = cosines.reshape(blocks, block), sines.reshape(blocks, block)
    cm = jnp.where(allowed, c[:, :, None] * c[:, None, :] + s[:, :, None] * s[:, None, :], 0.0)
    cosines = jnp.broadcast_to(cosines[:, None], (rows, LANES))
    sines = jnp.broadcast_to(sines[:, None], (rows, LANES))

    each = units // width
    thins = (
        b_query, b_key, b_value, b_up, b_out, norm_gain, norm_shift, b_down, final_gain, final_shift
    )
    if pieces:
        attention_shard, down_shard = pack(w_query, w_key, w_value, w_out, w_down, thins)
    else:
        columns = []
        for thin in thins:
            thin = jnp.pad(thin, (0, -thin.shape[0] % shard))
            columns.append(thin.reshape(-1, shard).T)
        columns = jnp.concatenate(columns, axis=1)
        columns = jnp.pad(columns, ((0, 0), (0, LANES - columns.shape[1])))
        attention_shard = jnp.concatenate([w_query, w_key, w_value, w_out.T, columns], axis=1)
        down_shard = w_down.T

    def gather_all(piece):
        everything = lax.all_gather(piece, BOTH, axis=0, tiled=False)
        everything = everything.reshape(replicas, halves, shard, piece.shape[1])
        return jnp.moveaxis(everything, 1, 0).reshape(1, halves, width, piece.shape[1])

    if pieces:
        first_chunk, up_chunk, down_chunk = Gather(attention_shard), Gather(w_up), Gather(down_shard)
        first_chunk.line()
        four = first_chunk.held
        first_chunk.beside()
        up_chunk.line([four])
        first_chunk.across([cm, cosines, sines])
        sixteen = first_chunk.held
        w_attention = first_chunk.core(coords)
    else:
        w_attention, w_lift, w_drop = [
            gather_all(piece) for piece in (attention_shard, w_up, down_shard)
        ]

    edge = shard // halves
    biases, bias_up, vectors = unpack(w_attention, shard, each)

    sq, sk, v, slope_q, slope_k, states, total = project(
        inputs, w_attention, biases, cosines, sines, block
    )
    queries, there = sq, []
    if pieces:
        four = up_chunk.held
        up_chunk.beside([sixteen], [sq])
        down_chunk.line([sixteen, four], [sq])
        there = [up_chunk.held, down_chunk.held]
        queries = after(sq, *there)
    num, den = attend(queries, sk, v, cm, cosines, sines, states)
    towards = [(i, i + 1) for i in range(halves - 1)]
    incoming = send(total, towards, there, [num], "tp")
    if pieces:
        up_chunk.across(there, [num])
        down_chunk.beside(there, [num])
        there = [up_chunk.held, down_chunk.held, incoming]
        num = after(num, *there)
    mixed, rden, normal, scale, low = mix(
        num, den, sq, incoming, cosines, sines, w_attention, inputs, vectors, 256
    )
    if pieces:
        sixteen = up_chunk.held
        w_lift = up_chunk.core(coords, [], [low])
    act, slope, now = [], [], low
    for half in range(halves):
        act_half, slope_half = lift(now, w_lift, bias_up, half, units, 512)
        act.append(act_half)
        slope.append(slope_half)
        if pieces and half == 0:
            down_chunk.across(there, [act_half])
            now = after(low, down_chunk.held)
    if pieces:
        w_drop = down_chunk.core(coords, [], [act[1]])
    output, branch, second, sums_second = drop(
        act, w_drop, normal, vectors, grad_output, units, 256
    )

    gdown = wide_gradient(coords, branch, act, layout(units), units, 256, "down_gradient")
    there = gdown
    if pieces:
        down_sum = Sum(*gdown)
    gl, gbias_up = [], []
    for half in range(halves):
        now = after(slope[half], *there)
        gl_half, gbias_half = bend(branch, w_drop, now, half, units, 512)
        gl.append(gl_half)
        gbias_up.append(gbias_half)
        if pieces and half == 0:
            down_sum.core([], [gl_half])
            there = down_sum.both()
    wide = units + part + LANES
    gup = wide_gradient(coords, low, gl, layout(wide), units, 256, "up_gradient")
    there = gup
    if pieces:
        down_sum.across([], gup)
        there = [*gup, *down_sum.both()]
    second = after(second, *there)
    first, first_low, sums_first = lower(gl, w_lift, second, normal, scale, vectors, units, 256)
    if pieces:
        down_sum.beside([], [first])
        first_low = after(first_low, *down_sum.parts)
    *gup, gn, gd, later, later_total = unmix(
        coords, first_low, mixed, rden, sq, cosines, sines, w_attention,
        sums_first, sums_second, gbias_up, gup, layout(wide), block,
    )
    there = []
    if pieces:
        gdown = down_sum.line([], [gn])
        there = [gdown]
        gn = after(gn, gdown)
    pairs = width // LANES
    partial = ()
    for half in range(halves):
        per = pairs // halves
        partial = unattend(
            sq, sk, v, gn, gd, cm, cosines, sines, states, incoming, later, slope_q,
            half * per, per, partial,
        )
        if half == 0:
            towards = [(i + 1, i) for i in range(halves - 1)]
            later_in = send(later_total, towards, there, partial, "tp")
        if pieces and half == 0:
            up_sum = Sum(*gup)
            up_sum.core(there, partial)
            partial = after(tuple(partial), later_in, *up_sum.both())
    query_low, dk, dv = partial
    *gqkv, key_low, value_low = finish(
        coords, inputs, query_low, dk, dv, sk, v, slope_k, cosines, sines, later_in,
        layout(3 * part + LANES),
    )
    if pieces:
        up_sum.across([], [key_low])
        rest_sum = Sum(*gqkv)
        rest_sum.core(up_sum.both())
        up_sum.beside()
        gup = up_sum.line()
        rest_sum.across()
        rest_sum.beside()
        rest = rest_sum.line()
    else:

        def scatter(grad):
            grad = jnp.moveaxis(grad.reshape(halves, replicas, shard, grad.shape[2]), 0, 1)
            grad = grad.reshape(replicas * halves, shard, grad.shape[3])
            return lax.psum_scatter(grad, BOTH, scatter_dimension=0, tiled=False).astype(F32)

        gdown, gup, rest = [scatter(grad[0]) for grad in (gdown, gup, gqkv)]
    grad_inputs = input_gradient(first, query_low, key_low, value_low, w_attention, 256)

    scaling = 1.0 / replicas
    gdown, gup, rest = gdown * scaling, gup * scaling, rest * scaling
    sums = gup[:, units + part :].T
    small = rest[:edge, 3 * part :].T
    return (
        output,
        grad_inputs,
        rest[:, :part],
        rest[:, part : 2 * part],
        rest[:, 2 * part : 3 * part],
        small[0],
        small[1],
        small[2],
        gup[:, units : units + part].T,
        sums[2],
        sums[0],
        sums[1],
        gup[:, :units],
        sums[6 : 6 + units // width].reshape(-1),
        gdown.T,
        sums[5],
        sums[3],
        sums[4],
    )


def solution(mesh):
    row = P(("fsdp", "tp"), None)
    split, turned = P("fsdp", "tp"), P("tp", "fsdp")
    thin, wide = P(("tp", "fsdp")), P("fsdp")
    return jax.shard_map(
        local,
        mesh=mesh,
        in_specs=(
            row, split, split, split, thin, thin, thin, turned, wide, wide, wide,
            split, thin, turned, wide, wide, wide, P("fsdp", None), row,
        ),
        out_specs=(
            row, row, split, split, split, thin, thin, thin, turned, wide, wide, wide,
            split, thin, turned, wide, wide, wide,
        ),
        check_vma=False,
    )
```

time: 589 us -> 391 us (0.66)
  waiting for transfers between devices: 353 us -> 83.7 us
  starting transfers between devices: 5.01 us -> 52.2 us
  Pallas kernels: 174 us -> 221 us
  between operations: 14.1 us -> 1.36 us
  local copies, waits for them, and re-layouts: 24.7 us -> 18.1 us
    reduce_scatter x3 -> x0, waiting for transfers between devices: 251 us -> none  [scatter(): return lax.psum_scatter(grad, BOTH, scatter_dimension=0, tiled=False)]
    all_gather x2 -> x0, waiting for transfers between devices: 102 us -> none  [gather(): whole_piece = lax.all_gather(piece, BOTH, axis=0, tiled=False)]
    ppermute x2 -> x38, waiting for transfers between devices: 0.01 us -> 83.7 us  [send(): value = lax.ppermute(value, axes, table)]
    ppermute x2 -> x38, starting transfers between devices: 4.62 us -> 52.2 us  [send(): value = lax.ppermute(value, axes, table)]
    pallas_call x6 -> x20, Pallas kernels: 129 us -> 176 us  [the longest x2 35.4 us: unattend(): pl.pallas_call(unattend_kernel, grid=(count,), in_specs=[spec, spec, spec...]
    concatenate x3 -> x0, local copies, waits for them, and re-layouts: 6.89 us -> none  [the longest x1 6.77 us: local(): jnp.concatenate([b_query, b_key, b_value, b_up, b_out, norm_gain, norm_sh...]
    unnamed x13 -> x54, local copies, waits for them, and re-layouts: 5.36 us -> 11.8 us
  transfers between devices with their start and end apart: 7 -> 38, of which waited for: 5 -> 16; matrix products, arithmetic and copies ran while one was open for 4% -> 2% of each run, Pallas kernels for 17% -> 48%
where the time goes in v2:
time: 391 us; the launch traced here: 387 us
  Pallas kernels  221 us (57%)
  waiting for transfers between devices  83.7 us (21%)
  starting transfers between devices  52.2 us (13%)
  local copies, waits for them, and re-layouts  18.1 us (5%)
  other arithmetic  11.1 us (3%)
    ppermute x38, waiting for transfers between devices, send(): value = lax.ppermute(value, axes, table)  83.7 us
    ppermute x38, starting transfers between devices, send(): value = lax.ppermute(value, axes, table)  52.2 us
    pallas_call x2, Pallas kernels, unattend(): pl.pallas_call(unattend_kernel, grid=(count,), in_specs=[spec, spec, spec...  35.4 us
    pallas_call x2, Pallas kernels, wide_gradient(): pl.pallas_call(functools.partial(wide_gradient_kernel, halves=halves), gr...  21.5 us
    pallas_call x1, Pallas kernels, finish(): pl.pallas_call(functools.partial(finish_kernel, shard=shard), grid=(halve...  17.5 us
    pallas_call x3, Pallas kernels, assemble(): pl.pallas_call(assemble_kernel, in_specs=[scalars(), pl.BlockSpec(memory_...  17 us
    pallas_call x2, Pallas kernels, lift(): pl.pallas_call(functools.partial(lift_kernel, step=256), grid=(tiles,), i...  16.6 us
    pallas_call x1, Pallas kernels, unmix(): pl.pallas_call(functools.partial(unmix_kernel, block=block, step=256, sha...  16.4 us
  transfers between devices with their start and end apart: 38, of which 16 were waited for; matrix products, arithmetic and copies ran while one was open for 2% of the time, Pallas kernels for 48%

profile of v2, /device:TPU:0, one launch (start us, length us, event | category | flops | bytes accessed | tf_op | source)
XLA Modules:
  0.0 387.4 jit_solution(3352927208465097619)
XLA Ops:
  4.0 2.2 pack.1
  6.2 5.0 %collective-permute-start.2 = (bf16[48,1664]{1,0:T(8,128)(2,1)}, bf16[48,1664]{1,0:T(8,128)(2,1)S(1)}, u32[]{:S(2)}, u32[]{:S(2)}) collective-permute-start(bf16[48,1664]{1,0:T(8,128)(2,1)} %get-tuple-element.113.refs_0_), channel_id=1, source_target_pairs={{0,24},{1,25},{2,26},{3,27},{4,28},{5,29},{6,30},{7,31},{8,16},{9,... | collective-permute-start | bytes 479240 | tf_op jit(solution)/shard_map/ppermute | solution.py:1010
  12.8 3.7 collective-permute-done.2.refs_3_
  16.5 8.5 %collective-permute-done.1.refs_2_ = bf16[48,1664]{1,0:T(8,128)(2,1)S(1)} collective-permute-done((bf16[48,1664]{1,0:T(8,128)(2,1)}, bf16[48,1664]{1,0:T(8,128)(2,1)S(1)}, u32[]{:S(2)}, u32[]{:S(2)}) %collective-permute-start.1) | collective-permute-done | bytes 159776 | tf_op jit(solution)/shard_map/ppermute | solution.py:1010
  26.4 2.0 join.3
  31.9 7.1 %collective-permute-done.3 = bf16[4,48,1664]{2,1,0:T(8,128)(2,1)S(1)} collective-permute-done((bf16[4,48,1664]{2,1,0:T(8,128)(2,1)}, bf16[4,48,1664]{2,1,0:T(8,128)(2,1)S(1)}, u32[]{:S(2)}, u32[]{:S(2)}) %collective-permute-start.3) | collective-permute-done | bytes 639008 | tf_op jit(solution)/shard_map/ppermute | solution.py:1010
  42.7 15.7 %collective-permute-done.4 = bf16[8,48,1664]{2,1,0:T(8,128)(2,1)S(1)} collective-permute-done((bf16[8,48,1664]{2,1,0:T(8,128)(2,1)S(1)}, bf16[8,48,1664]{2,1,0:T(8,128)(2,1)S(1)}, u32[]{:S(2)}, u32[]{:S(2)}) %collective-permute-start.4) | collective-permute-done | bytes 1277984 | tf_op jit(solution)/shard_map/ppermute | solution.py:1010
  58.8 2.5 collective-permute-start.8
  63.3 4.2 %collective-permute-done.8.refs_3_ = bf16[48,1536]{1,0:T(8,128)(2,1)S(1)} collective-permute-done((bf16[48,1536]{1,0:T(8,128)(2,1)S(1)}, bf16[48,1536]{1,0:T(8,128)(2,1)S(1)}, u32[]{:S(2)}, u32[]{:S(2)}) %collective-permute-start.8) | collective-permute-done | bytes 147488 | tf_op jit(solution)/shard_map/ppermute | solution.py:1010
  67.5 6.3 %collective-permute-done.7.refs_2_ = bf16[48,1536]{1,0:T(8,128)(2,1)S(1)} collective-permute-done((bf16[48,1536]{1,0:T(8,128)(2,1)S(1)}, bf16[48,1536]{1,0:T(8,128)(2,1)S(1)}, u32[]{:S(2)}, u32[]{:S(2)}) %collective-permute-start.7) | collective-permute-done | bytes 147488 | tf_op jit(solution)/shard_map/ppermute | solution.py:1010
  81.1 2.4 collective-permute-start.10
  83.5 5.8 %assemble.3.thin_ref.w_ref = bf16[1,2,768,1664]{3,2,1,0:T(8,128)(2,1)} custom-call(s32[4]{0:T(128)} %pad_add_fusion.coords_ref, bf16[16,48,1664]{2,1,0:T(8,128)(2,1)} %copy-done.1, bf16[16,48,1664]{2,1,0:T(8,128)(2,1)} %collective-permute-done.5.other_ref), custom_call_target="tpu_custom_call" | custom-call | bytes 10223616 | tf_op jit(solution)/shard_map/assemble/pallas_call | solution.py:974
  89.3 4.3 %unpack.1 = (f32[2,8,384]{2,1,0:T(8,128)}, f32[2,8,1536]{2,1,0:T(8,128)}, f32[8,768]{1,0:T(8,128)}) custom-call(bf16[1,2,768,1664]{3,2,1,0:T(8,128)(2,1)} %assemble.3.thin_ref.w_ref), custom_call_target="tpu_custom_call" | custom-call | flops 100000000 | bytes 1000000 | tf_op jit(solution)/shard_map/unpack/pallas_call | solution.py:187
  93.7 13.2 %project.1 = (bf16[1024,768]{1,0:T(8,128)(2,1)}, bf16[1024,768]{1,0:T(8,128)(2,1)}, bf16[1024,768]{1,0:T(8,128)(2,1)}, bf16[1024,768]{1,0:T(8,128)(2,1)}, bf16[1...) custom-call(bf16[1024,768]{1,0:T(8,128)(2,1)} %x_ref.5, ...), custom_call_target="tpu_custom_call" | custom-call | flops 3623878656 | bytes 16000000 | tf_op jit(solution)/shard_map/project/pallas_call | solution.py:267
  111.2 12.4 %attend.1 = (f32[1024,768]{1,0:T(8,128)}, f32[1024,768]{1,0:T(8,128)}) custom-call(bf16[1024,768]{1,0:T(8,128)(2,1)} %get-tuple-element.125.sq_ref, bf16[1024,768]{1,0:T(8,128)(2,1)} %get-tuple-element.126.sk_ref, bf16[1024,768]{1,0:T(8,128)(2,1)} %get-tuple-element.127.v_ref, f32[2,512,512]{2,1,0:T(8,128)} %add_select_fusion.cm_ref, ...), custom_call_target="tpu_custom_call" | custom-call | flops 8000000000 | bytes 14000000 | tf_op jit(solution)/shard_map/attend/pallas_call | solution.py:326
  123.6 2.2 collective-permute-done.13
  127.5 3.7 collective-permute-start.15
  131.1 12.8 %collective-permute-done.15.in_ref = bf16[6,256,128]{2,1,0:T(8,128)(2,1)S(1)} collective-permute-done((bf16[6,256,128]{2,1,0:T(8,128)(2,1)S(1)}, bf16[6,256,128]{2,1,0:T(8,128)(2,1)S(1)}, u32[]{:S(2)}, u32[]{:S(2)}) %collective-permute-start.15) | collective-permute-done | bytes 393248 | tf_op jit(solution)/shard_map/ppermute | solution.py:1010
  144.8 2.7 collective-permute-start.17
  147.5 10.3 %mix.1 = (bf16[1024,768]{1,0:T(8,128)(2,1)}, f32[1024,768]{1,0:T(8,128)}, f32[1024,768]{1,0:T(8,128)}, f32[1024,128]{1,0:T(8,128)}, bf16[1024,768]{1,0:T(8,128)(2,1)}) custom-call(f32[1024,768]{1,0:T(8,128)} %get-tuple-element.137.num_ref, f32[1024,768]{1,0:T(8,128)} %get-tuple-element.138.den_ref, bf16[1024,768]{1,0:T(8,128)(2,1)} %get-tuple-element.125.sq_ref, ...), custom_call_target="tpu_custom_call" | custom-call | flops 2415919104 | bytes 20000000 | tf_op jit(solution)/shard_map/mix/pallas_call | solution.py:387
  159.2 5.6 %assemble.4.up_ref.refs_2_ = bf16[1,2,768,1536]{3,2,1,0:T(8,128)(2,1)} custom-call(s32[4]{0:T(128)} %pad_add_fusion.coords_ref, bf16[16,48,1536]{2,1,0:T(8,128)(2,1)} %copy-done.2, bf16[16,48,1536]{2,1,0:T(8,128)(2,1)} %copy-done.8), custom_call_target="tpu_custom_call" | custom-call | bytes 9437184 | tf_op jit(solution)/shard_map/assemble/pallas_call | solution.py:974
  164.8 7.9 %lift.2 = (bf16[1024,1536]{1,0:T(8,128)(2,1)}, bf16[1024,1536]{1,0:T(8,128)(2,1)}) custom-call(bf16[1024,768]{1,0:T(8,128)(2,1)} %get-tuple-element.146.low_ref.left_ref, bf16[1,2,768,1536]{3,2,1,0:T(8,128)(2,1)} %assemble.4.up_ref.refs_2_, f32[2,8,1536]{2,1,0:T(8,128)} %get-tuple-element.142.bias_ref), custom_call_target="tpu_custom_call" | custom-call | flops 2415919104 | bytes 10000000 | tf_op jit(solution)/shard_map/lift/pallas_call | solution.py:440
  173.0 8.7 %lift.3 = (bf16[1024,1536]{1,0:T(8,128)(2,1)}, bf16[1024,1536]{1,0:T(8,128)(2,1)}) custom-call(bf16[1024,768]{1,0:T(8,128)(2,1)} %get-tuple-element.146.low_ref.left_ref, bf16[1,2,768,1536]{3,2,1,0:T(8,128)(2,1)} %assemble.4.up_ref.refs_2_, f32[2,8,1536]{2,1,0:T(8,128)} %get-tuple-element.142.bias_ref), custom_call_target="tpu_custom_call" | custom-call | flops 2415919104 | bytes 10000000 | tf_op jit(solution)/shard_map/lift/pallas_call | solution.py:440
  183.1 5.6 %assemble.5.refs_2_.down_ref = bf16[1,2,768,1536]{3,2,1,0:T(8,128)(2,1)} custom-call(s32[4]{0:T(128)} %pad_add_fusion.coords_ref, bf16[16,48,1536]{2,1,0:T(8,128)(2,1)} %copy-done.3, bf16[16,48,1536]{2,1,0:T(8,128)(2,1)} %copy-done.9), custom_call_target="tpu_custom_call" | custom-call | bytes 9437184 | tf_op jit(solution)/shard_map/assemble/pallas_call | solution.py:974
  188.7 12.7 %drop.1 = (bf16[1024,768]{1,0:T(8,128)(2,1)}, bf16[1024,768]{1,0:T(8,128)(2,1)}, f32[1024,768]{1,0:T(8,128)}, f32[8,768]{1,0:T(8,128)}) custom-call(bf16[1024,1536]{1,0:T(8,128)(2,1)} %get-tuple-element.143.refs_0_, bf16[1024,1536]{1,0:T(8,128)(2,1)} %get-tuple-element.147.refs_1_, bf16[1,2,768,1536]{3,2,1,0:T(8,128)(2,1)} %assemble.5.refs_2_.down_ref, ...), custom_call_target="tpu_custom_call" | custom-call | flops 4831838208 | bytes 20000000 | tf_op jit(solution)/shard_map/drop/pallas_call | solution.py:483
  201.4 10.9 %down_gradient.1 = (bf16[16,48,1536]{2,1,0:T(8,128)(2,1)}, bf16[16,48,1536]{2,1,0:T(8,128)(2,1)}) custom-call(s32[4]{0:T(128)} %pad_add_fusion.coords_ref, bf16[1024,768]{1,0:T(8,128)(2,1)} %get-tuple-element.151.left_ref.branch_ref, bf16[1024,1536]{1,0:T(8,128)(2,1)} %get-tuple-element.143.refs_0_, bf16[1024,1536]{1,0:T(8,128)(2,1)} %get-tuple-element.147.refs_1_), custom_call_target="tpu_custom_call" | custom-call | flops 4831838208 | bytes 18000000 | tf_op jit(solution)/shard_map/down_gradient/pallas_call | solution.py:532
  212.3 7.0 %bend.2 = (bf16[1024,1536]{1,0:T(8,128)(2,1)}, f32[8,1536]{1,0:T(8,128)}) custom-call(bf16[1024,768]{1,0:T(8,128)(2,1)} %get-tuple-element.151.left_ref.branch_ref, bf16[1,2,768,1536]{3,2,1,0:T(8,128)(2,1)} %assemble.5.refs_2_.down_ref, bf16[1024,1536]{1,0:T(8,128)(2,1)} %get-tuple-element.155.slope_ref), custom_call_target="tpu_custom_call" | custom-call | flops 2415919104 | bytes 10000000 | tf_op jit(solution)/shard_map/bend/pallas_call | solution.py:566
  220.1 6.9 %bend.3 = (bf16[1024,1536]{1,0:T(8,128)(2,1)}, f32[8,1536]{1,0:T(8,128)}) custom-call(bf16[1024,768]{1,0:T(8,128)(2,1)} %get-tuple-element.151.left_ref.branch_ref, bf16[1,2,768,1536]{3,2,1,0:T(8,128)(2,1)} %assemble.5.refs_2_.down_ref, bf16[1024,1536]{1,0:T(8,128)(2,1)} %get-tuple-element.159.slope_ref), custom_call_target="tpu_custom_call" | custom-call | flops 2415919104 | bytes 10000000 | tf_op jit(solution)/shard_map/bend/pallas_call | solution.py:566
  226.9 10.7 %up_gradient.1 = (bf16[16,48,2048]{2,1,0:T(8,128)(2,1)}, bf16[16,48,2048]{2,1,0:T(8,128)(2,1)}) custom-call(s32[4]{0:T(128)} %pad_add_fusion.coords_ref, bf16[1024,768]{1,0:T(8,128)(2,1)} %get-tuple-element.146.low_ref.left_ref, bf16[1024,1536]{1,0:T(8,128)(2,1)} %get-tuple-element.156.refs_0_, bf16[1024,1536]{1,0:T(8,128)(2,1)} %get-tuple-element.160.refs_1_), custom_call_target="tpu_custom_call" | custom-call | flops 4831838208 | bytes 18000000 | tf_op jit(solution)/shard_map/up_gradient/pallas_call | solution.py:532
  237.9 2.5 collective-permute-start.21
  240.4 12.7 %lower.1 = (f32[1024,768]{1,0:T(8,128)}, bf16[1024,768]{1,0:T(8,128)(2,1)}, f32[8,768]{1,0:T(8,128)}) custom-call(bf16[1024,1536]{1,0:T(8,128)(2,1)} %get-tuple-element.156.refs_0_, bf16[1024,1536]{1,0:T(8,128)(2,1)} %get-tuple-element.160.refs_1_, bf16[1,2,768,1536]{3,2,1,0:T(8,128)(2,1)} %assemble.4.up_ref.refs_2_, ...), custom_call_target="tpu_custom_call" | custom-call | flops 4831838208 | bytes 20000000 | tf_op jit(solution)/shard_map/lower/pallas_call | solution.py:609
  253.3 2.0 collective-permute-start.24
  255.3 2.4 collective-permute-start.22
  257.7 16.4 %unmix.1 = (bf16[16,48,2048]{2,1,0:T(8,128)(2,1)}, bf16[16,48,2048]{2,1,0:T(8,128)(2,1)}, bf16[1024,768]{1,0:T(8,128)(2,1)}, bf16[1024,768]{1,0:T(8,128)(2,1)}, ...) custom-call(s32[4]{0:T(128)} %pad_add_fusion.coords_ref, ...), custom_call_target="tpu_custom_call", output_to_operand_aliasing={{0}: (12, {}), {1}: (13, {})} | custom-call | flops 2415919104 | bytes 16000000 | tf_op jit(solution)/shard_map/unmix/pallas_call | solution.py:722
  276.3 22.1 %unattend.2 = (bf16[1024,768]{1,0:T(8,128)(2,1)}, f32[1024,768]{1,0:T(8,128)}, f32[1024,768]{1,0:T(8,128)}) custom-call(bf16[1024,768]{1,0:T(8,128)(2,1)} %get-tuple-element.125.sq_ref, bf16[1024,768]{1,0:T(8,128)(2,1)} %get-tuple-element.126.sk_ref, bf16[1024,768]{1,0:T(8,128)(2,1)} %get-tuple-element.127.v_ref, ...), custom_call_target="tpu_custom_call" | custom-call | flops 20000000000 | bytes 20000000 | tf_op jit(solution)/shard_map/unattend/pallas_call | solution.py:832
  298.4 2.7 add_convert_fusion
  303.1 13.3 %unattend.3 = (bf16[1024,768]{1,0:T(8,128)(2,1)}, f32[1024,768]{1,0:T(8,128)}, f32[1024,768]{1,0:T(8,128)}) custom-call(bf16[1024,768]{1,0:T(8,128)(2,1)} %get-tuple-element.125.sq_ref, bf16[1024,768]{1,0:T(8,128)(2,1)} %get-tuple-element.126.sk_ref, ...), custom_call_target="tpu_custom_call", output_to_operand_aliasing={{0}: (12, {}), {1}: (13, {}), {2}: (14, {})} | custom-call | flops 20000000000 | bytes 20000000 | tf_op jit(solution)/shard_map/unattend/pallas_call | solution.py:832
  316.4 17.5 %finish.1 = (bf16[16,48,1280]{2,1,0:T(8,128)(2,1)}, bf16[16,48,1280]{2,1,0:T(8,128)(2,1)}, bf16[1024,768]{1,0:T(8,128)(2,1)}, bf16[1024,768]{1,0:T(8,128)(2,1)}) custom-call(s32[4]{0:T(128)} %pad_add_fusion.coords_ref, bf16[1024,768]{1,0:T(8,128)(2,1)} %x_ref.5, bf16[1024,768]{1,0:T(8,128)(2,1)} %get-tuple-element.198.q_ref, ...), custom_call_target="tpu_custom_call" | custom-call | flops 3623878656 | bytes 10000000 | tf_op jit(solution)/shard_map/finish/pallas_call | solution.py:900
  336.1 2.1 collective-permute-start.34
  340.2 2.0 collective-permute-start.29
  342.3 8.8 %input_gradient.1 = bf16[1024,768]{1,0:T(8,128)(2,1)} custom-call(f32[1024,768]{1,0:T(8,128)} %get-tuple-element.167.first_ref, bf16[1024,768]{1,0:T(8,128)(2,1)} %get-tuple-element.198.q_ref, bf16[1024,768]{1,0:T(8,128)(2,1)} %get-tuple-element.202.k_ref, bf16[1024,768]{1,0:T(8,128)(2,1)} %get-tuple-element.203.v_ref, ...), custom_call_target="tpu_custom_call" | custom-call | flops 3623878656 | bytes 14000000 | tf_op jit(solution)/shard_map/input_gradient/pallas_call | solution.py:935
  352.7 2.0 collective-permute-start.37
  358.1 2.4 collective-permute-start.30
  361.5 3.3 collective-permute-done.37
  364.8 7.4 %collective-permute-done.36 = bf16[48,2048]{1,0:T(8,128)(2,1)S(1)} collective-permute-done((bf16[48,2048]{1,0:T(8,128)(2,1)S(1)}, bf16[48,2048]{1,0:T(8,128)(2,1)S(1)}, u32[]{:S(2)}, u32[]{:S(2)}) %collective-permute-start.36) | collective-permute-done | bytes 196640 | tf_op jit(solution)/shard_map/ppermute | solution.py:1010
  373.2 2.0 collective-permute-start.33
  378.9 2.1 collective-permute-done.33
  381.1 4.6 %collective-permute-done.32 = bf16[48,1280]{1,0:T(8,128)(2,1)S(1)} collective-permute-done((bf16[48,1280]{1,0:T(8,128)(2,1)S(1)}, bf16[48,1280]{1,0:T(8,128)(2,1)S(1)}, u32[]{:S(2)}, u32[]{:S(2)}) %collective-permute-start.32) | collective-permute-done | bytes 122912 | tf_op jit(solution)/shard_map/ppermute | solution.py:1010
  (145 shorter events, 54.4 us)
Async XLA Ops:
  6.2 10.3 %collective-permute-start.2 = (bf16[48,1664]{1,0:T(8,128)(2,1)}, bf16[48,1664]{1,0:T(8,128)(2,1)S(1)}, u32[]{:S(2)}, u32[]{:S(2)}) collective-permute-start(bf16[48,1664]{1,0:T(8,128)(2,1)} %get-tuple-element.113.refs_0_), channel_id=1, source_target_pairs={{0,24},{1,25},{2,26},{3,27},{4,28},{5,29},{6,30},{7,31},{8,16},{9,... | collective-permute-start | bytes 479240 | tf_op jit(solution)/shard_map/ppermute | solution.py:1010
  11.3 13.7 %collective-permute-start.1 = (bf16[48,1664]{1,0:T(8,128)(2,1)}, bf16[48,1664]{1,0:T(8,128)(2,1)S(1)}, u32[]{:S(2)}, u32[]{:S(2)}) collective-permute-start(bf16[48,1664]{1,0:T(8,128)(2,1)} %get-tuple-element.113.refs_0_), channel_id=1, source_target_pairs={{0,16},{1,17},{2,18},{3,19},{4,20},{5,21},{6,22},{7,23},{8,24},{9,... | collective-permute-start | bytes 479240 | tf_op jit(solution)/shard_map/ppermute | solution.py:1010
  11.3 13.7 %collective-permute-start = (bf16[48,1664]{1,0:T(8,128)(2,1)}, bf16[48,1664]{1,0:T(8,128)(2,1)S(1)}, u32[]{:S(2)}, u32[]{:S(2)}) collective-permute-start(bf16[48,1664]{1,0:T(8,128)(2,1)} %get-tuple-element.113.refs_0_), channel_id=1, source_target_pairs={{0,8},{1,9},{2,10},{3,11},{4,12},{5,13},{6,14},{7,15},{8,0},{9,1},... | collective-permute-start | bytes 479240 | tf_op jit(solution)/shard_map/ppermute | solution.py:1010
  16.5 8.5 %copy-start.13 = (bf16[48,1664]{1,0:T(8,128)(2,1)}, bf16[48,1664]{1,0:T(8,128)(2,1)S(1)}, u32[]{:S(2)}) copy-start(bf16[48,1664]{1,0:T(8,128)(2,1)S(1)} %collective-permute-done.2.refs_3_) | copy-start | bytes 479236
  28.4 10.6 %copy-start.4 = (bf16[4,48,1664]{2,1,0:T(8,128)(2,1)S(1)}, bf16[4,48,1664]{2,1,0:T(8,128)(2,1)}, u32[]{:S(2)}) copy-start(bf16[4,48,1664]{2,1,0:T(8,128)(2,1)} %join.3) | copy-start | bytes 1916932
  28.4 10.6 %collective-permute-start.3 = (bf16[4,48,1664]{2,1,0:T(8,128)(2,1)}, bf16[4,48,1664]{2,1,0:T(8,128)(2,1)S(1)}, u32[]{:S(2)}, u32[]{:S(2)}) collective-permute-start(bf16[4,48,1664]{2,1,0:T(8,128)(2,1)} %join.3), channel_id=1, source_target_pairs={{0,1},{1,0},{2,6},{3,7},{4,5},{5,4},{6,2},{7,3},{8,9},{9,8},{10,14... | collective-permute-start | bytes 1916936 | tf_op jit(solution)/shard_map/ppermute | solution.py:1010
  41.2 17.7 %copy-start.16 = (bf16[48,1536]{1,0:T(8,128)(2,1)S(1)}, bf16[48,1536]{1,0:T(8,128)(2,1)}, u32[]{:S(2)}) copy-start(bf16[48,1536]{1,0:T(8,128)(2,1)} %refs_0_.3) | copy-start | bytes 442372
  41.2 38.0 %copy-start.17 = (bf16[48,1536]{1,0:T(8,128)(2,1)S(1)}, bf16[48,1536]{1,0:T(8,128)(2,1)}, u32[]{:S(2)}) copy-start(bf16[48,1536]{1,0:T(8,128)(2,1)} %get-tuple-element.121.refs_0_) | copy-start | bytes 442372
  41.2 17.3 %collective-permute-start.4 = (bf16[8,48,1664]{2,1,0:T(8,128)(2,1)S(1)}, bf16[8,48,1664]{2,1,0:T(8,128)(2,1)S(1)}, u32[]{:S(2)}, u32[]{:S(2)}) collective-permute-start(bf16[8,48,1664]{2,1,0:T(8,128)(2,1)S(1)} %pad_maximum_fusion.3), channel_id=1, source_target_pairs={{0,4},{1,5},{2,3},{3,2},{4,0},{5,1},{6,7},{7,6},{8,12},{9,13},{10,... | collective-permute-start | bytes 3833864 | tf_op jit(solution)/shard_map/ppermute | solution.py:1010
  58.7 24.8 %copy-start.1 = (bf16[16,48,1664]{2,1,0:T(8,128)(2,1)}, bf16[16,48,1664]{2,1,0:T(8,128)(2,1)S(1)}, u32[]{:S(2)}) copy-start(bf16[16,48,1664]{2,1,0:T(8,128)(2,1)S(1)} %pad_maximum_fusion.own_ref) | copy-start | bytes 7667716
  58.7 24.8 %collective-permute-start.5 = (bf16[16,48,1664]{2,1,0:T(8,128)(2,1)S(1)}, bf16[16,48,1664]{2,1,0:T(8,128)(2,1)}, u32[]{:S(2)}, u32[]{:S(2)}) collective-permute-start(bf16[16,48,1664]{2,1,0:T(8,128)(2,1)S(1)} %pad_maximum_fusion.own_ref), channel_id=1, source_target_pairs={{0,2},{1,3},{2,0},{3,1},{4,6},{5,7},{6,4},{7,5},{8,10},{9,11},{10,... | collective-permute-start | bytes 7667720 | tf_op jit(solution)/shard_map/ppermute | solution.py:1010
  58.8 8.7 %collective-permute-start.8 = (bf16[48,1536]{1,0:T(8,128)(2,1)S(1)}, bf16[48,1536]{1,0:T(8,128)(2,1)S(1)}, u32[]{:S(2)}, u32[]{:S(2)}) collective-permute-start(bf16[48,1536]{1,0:T(8,128)(2,1)S(1)} %copy-done.16), channel_id=1, source_target_pairs={{0,24},{1,25},{2,26},{3,27},{4,28},{5,29},{6,30},{7,31},{8,16},{9,... | collective-permute-start | bytes 442376 | tf_op jit(solution)/shard_map/ppermute | solution.py:1010
  61.4 12.4 %collective-permute-start.7 = (bf16[48,1536]{1,0:T(8,128)(2,1)S(1)}, bf16[48,1536]{1,0:T(8,128)(2,1)S(1)}, u32[]{:S(2)}, u32[]{:S(2)}) collective-permute-start(bf16[48,1536]{1,0:T(8,128)(2,1)S(1)} %copy-done.16), channel_id=1, source_target_pairs={{0,16},{1,17},{2,18},{3,19},{4,20},{5,21},{6,22},{7,23},{8,24},{9,... | collective-permute-start | bytes 442376 | tf_op jit(solution)/shard_map/ppermute | solution.py:1010
  61.4 12.4 %collective-permute-start.6 = (bf16[48,1536]{1,0:T(8,128)(2,1)S(1)}, bf16[48,1536]{1,0:T(8,128)(2,1)S(1)}, u32[]{:S(2)}, u32[]{:S(2)}) collective-permute-start(bf16[48,1536]{1,0:T(8,128)(2,1)S(1)} %copy-done.16), channel_id=1, source_target_pairs={{0,8},{1,9},{2,10},{3,11},{4,12},{5,13},{6,14},{7,15},{8,0},{9,1},... | collective-permute-start | bytes 442376 | tf_op jit(solution)/shard_map/ppermute | solution.py:1010
  77.1 29.9 %collective-permute-start.9 = (bf16[4,48,1536]{2,1,0:T(8,128)(2,1)}, bf16[4,48,1536]{2,1,0:T(8,128)(2,1)S(1)}, u32[]{:S(2)}, u32[]{:S(2)}) collective-permute-start(bf16[4,48,1536]{2,1,0:T(8,128)(2,1)} %join.4), channel_id=1, source_target_pairs={{0,1},{1,0},{2,6},{3,7},{4,5},{5,4},{6,2},{7,3},{8,9},{9,8},{10,14... | collective-permute-start | bytes 1769480 | tf_op jit(solution)/shard_map/ppermute | solution.py:1010
  79.1 27.8 %collective-permute-start.12 = (bf16[48,1536]{1,0:T(8,128)(2,1)S(1)}, bf16[48,1536]{1,0:T(8,128)(2,1)S(1)}, u32[]{:S(2)}, u32[]{:S(2)}) collective-permute-start(bf16[48,1536]{1,0:T(8,128)(2,1)S(1)} %copy-done.17), channel_id=1, source_target_pairs={{0,24},{1,25},{2,26},{3,27},{4,28},{5,29},{6,30},{7,31},{8,16},{9,... | collective-permute-start | bytes 442376 | tf_op jit(solution)/shard_map/ppermute | solution.py:1010
  81.1 25.8 %collective-permute-start.11 = (bf16[48,1536]{1,0:T(8,128)(2,1)S(1)}, bf16[48,1536]{1,0:T(8,128)(2,1)S(1)}, u32[]{:S(2)}, u32[]{:S(2)}) collective-permute-start(bf16[48,1536]{1,0:T(8,128)(2,1)S(1)} %copy-done.17), channel_id=1, source_target_pairs={{0,16},{1,17},{2,18},{3,19},{4,20},{5,21},{6,22},{7,23},{8,24},{9,... | collective-permute-start | bytes 442376 | tf_op jit(solution)/shard_map/ppermute | solution.py:1010
  81.1 25.8 %collective-permute-start.10 = (bf16[48,1536]{1,0:T(8,128)(2,1)S(1)}, bf16[48,1536]{1,0:T(8,128)(2,1)S(1)}, u32[]{:S(2)}, u32[]{:S(2)}) collective-permute-start(bf16[48,1536]{1,0:T(8,128)(2,1)S(1)} %copy-done.17), channel_id=1, source_target_pairs={{0,8},{1,9},{2,10},{3,11},{4,12},{5,13},{6,14},{7,15},{8,0},{9,1},... | collective-permute-start | bytes 442376 | tf_op jit(solution)/shard_map/ppermute | solution.py:1010
  93.7 13.3 %copy-start.5 = (bf16[4,48,1536]{2,1,0:T(8,128)(2,1)S(1)}, bf16[4,48,1536]{2,1,0:T(8,128)(2,1)}, u32[]{:S(2)}) copy-start(bf16[4,48,1536]{2,1,0:T(8,128)(2,1)} %join.4) | copy-start | bytes 1769476
  109.7 16.2 %collective-permute-start.13 = (bf16[8,48,1536]{2,1,0:T(8,128)(2,1)S(1)}, bf16[8,48,1536]{2,1,0:T(8,128)(2,1)S(1)}, u32[]{:S(2)}, u32[]{:S(2)}) collective-permute-start(bf16[8,48,1536]{2,1,0:T(8,128)(2,1)S(1)} %pad_maximum_fusion.4), channel_id=1, source_target_pairs={{0,4},{1,5},{2,3},{3,2},{4,0},{5,1},{6,7},{7,6},{8,12},{9,13},{10,... | collective-permute-start | bytes 3538952 | tf_op jit(solution)/shard_map/ppermute | solution.py:1010
  126.1 31.7 %copy-start.2 = (bf16[16,48,1536]{2,1,0:T(8,128)(2,1)}, bf16[16,48,1536]{2,1,0:T(8,128)(2,1)S(1)}, u32[]{:S(2)}) copy-start(bf16[16,48,1536]{2,1,0:T(8,128)(2,1)S(1)} %pad_maximum_fusion.1.own_ref) | copy-start | bytes 7077892
  126.1 31.7 %collective-permute-start.16 = (bf16[16,48,1536]{2,1,0:T(8,128)(2,1)S(1)}, bf16[16,48,1536]{2,1,0:T(8,128)(2,1)S(1)}, u32[]{:S(2)}, u32[]{:S(2)}) collective-permute-start(bf16[16,48,1536]{2,1,0:T(8,128)(2,1)S(1)} %pad_maximum_fusion.1.own_ref), channel_id=1, source_target_pairs={{0,2},{1,3},{2,0},{3,1},{4,6},{5,7},{6,4},{7,5},{8,10},{9,11},{10,... | collective-permute-start | bytes 7077896 | tf_op jit(solution)/shard_map/ppermute | solution.py:1010
  126.9 17.8 %collective-permute-start.14 = (bf16[4,48,1536]{2,1,0:T(8,128)(2,1)S(1)}, bf16[4,48,1536]{2,1,0:T(8,128)(2,1)S(1)}, u32[]{:S(2)}, u32[]{:S(2)}) collective-permute-start(bf16[4,48,1536]{2,1,0:T(8,128)(2,1)S(1)} %copy-done.6), channel_id=1, source_target_pairs={{0,1},{1,0},{2,6},{3,7},{4,5},{5,4},{6,2},{7,3},{8,9},{9,8},{10,14... | collective-permute-start | bytes 1769480 | tf_op jit(solution)/shard_map/ppermute | solution.py:1010
  127.5 16.4 %collective-permute-start.15 = (bf16[6,256,128]{2,1,0:T(8,128)(2,1)S(1)}, bf16[6,256,128]{2,1,0:T(8,128)(2,1)S(1)}, u32[]{:S(2)}, u32[]{:S(2)}) collective-permute-start(bf16[6,256,128]{2,1,0:T(8,128)(2,1)S(1)} %copy-done.25), channel_id=1, source_target_pairs={{0,1},{2,3},{4,5},{6,7},{8,9},{10,11},{12,13},{14,15},{16,17},{18,... | collective-permute-start | bytes 1179656 | tf_op jit(solution)/shard_map/ppermute | solution.py:1010
  144.8 27.9 %collective-permute-start.17 = (bf16[8,48,1536]{2,1,0:T(8,128)(2,1)S(1)}, bf16[8,48,1536]{2,1,0:T(8,128)(2,1)S(1)}, u32[]{:S(2)}, u32[]{:S(2)}) collective-permute-start(bf16[8,48,1536]{2,1,0:T(8,128)(2,1)S(1)} %pad_maximum_fusion.5), channel_id=1, source_target_pairs={{0,4},{1,5},{2,3},{3,2},{4,0},{5,1},{6,7},{7,6},{8,12},{9,13},{10,... | collective-permute-start | bytes 3538952 | tf_op jit(solution)/shard_map/ppermute | solution.py:1010
  173.0 8.8 %copy-start.3 = (bf16[16,48,1536]{2,1,0:T(8,128)(2,1)}, bf16[16,48,1536]{2,1,0:T(8,128)(2,1)S(1)}, u32[]{:S(2)}) copy-start(bf16[16,48,1536]{2,1,0:T(8,128)(2,1)S(1)} %pad_maximum_fusion.2.own_ref) | copy-start | bytes 7077892
  173.0 8.8 %collective-permute-start.18 = (bf16[16,48,1536]{2,1,0:T(8,128)(2,1)S(1)}, bf16[16,48,1536]{2,1,0:T(8,128)(2,1)S(1)}, u32[]{:S(2)}, u32[]{:S(2)}) collective-permute-start(bf16[16,48,1536]{2,1,0:T(8,128)(2,1)S(1)} %pad_maximum_fusion.2.own_ref), channel_id=1, source_target_pairs={{0,2},{1,3},{2,0},{3,1},{4,6},{5,7},{6,4},{7,5},{8,10},{9,11},{10,... | collective-permute-start | bytes 7077896 | tf_op jit(solution)/shard_map/ppermute | solution.py:1010
  212.2 7.0 %collective-permute-start.19 = (bf16[16,48,1536]{2,1,0:T(8,128)(2,1)}, bf16[16,48,1536]{2,1,0:T(8,128)(2,1)S(1)}, u32[]{:S(2)}, u32[]{:S(2)}) collective-permute-start(bf16[16,48,1536]{2,1,0:T(8,128)(2,1)} %get-tuple-element.154), channel_id=1, source_target_pairs={{0,2},{1,3},{2,0},{3,1},{4,6},{5,7},{6,4},{7,5},{8,10},{9,11},{10,... | collective-permute-start | bytes 7077896 | tf_op jit(solution)/shard_map/ppermute | solution.py:1010
  212.2 7.0 %copy-start.7 = (bf16[16,48,1536]{2,1,0:T(8,128)(2,1)S(1)}, bf16[16,48,1536]{2,1,0:T(8,128)(2,1)}, u32[]{:S(2)}) copy-start(bf16[16,48,1536]{2,1,0:T(8,128)(2,1)} %get-tuple-element.153) | copy-start | bytes 7077892
  220.0 17.6 %collective-permute-start.20 = (bf16[8,48,1536]{2,1,0:T(8,128)(2,1)S(1)}, bf16[8,48,1536]{2,1,0:T(8,128)(2,1)S(1)}, u32[]{:S(2)}, u32[]{:S(2)}) collective-permute-start(bf16[8,48,1536]{2,1,0:T(8,128)(2,1)S(1)} %get-tuple-element.221), channel_id=1, source_target_pairs={{0,4},{1,5},{2,3},{3,2},{4,0},{5,1},{6,7},{7,6},{8,12},{9,13},{10,... | collective-permute-start | bytes 3538952 | tf_op jit(solution)/shard_map/ppermute | solution.py:1010
  237.9 15.2 %collective-permute-start.21 = (bf16[4,48,1536]{2,1,0:T(8,128)(2,1)S(1)}, bf16[4,48,1536]{2,1,0:T(8,128)(2,1)S(1)}, u32[]{:S(2)}, u32[]{:S(2)}) collective-permute-start(bf16[4,48,1536]{2,1,0:T(8,128)(2,1)S(1)} %get-tuple-element.227), channel_id=1, source_target_pairs={{0,1},{1,0},{2,6},{3,7},{4,5},{5,4},{6,2},{7,3},{8,9},{9,8},{10,14... | collective-permute-start | bytes 1769480 | tf_op jit(solution)/shard_map/ppermute | solution.py:1010
  253.3 20.8 %collective-permute-start.24 = (bf16[48,1536]{1,0:T(8,128)(2,1)S(1)}, bf16[48,1536]{1,0:T(8,128)(2,1)S(1)}, u32[]{:S(2)}, u32[]{:S(2)}) collective-permute-start(bf16[48,1536]{1,0:T(8,128)(2,1)S(1)} %get-tuple-element.234), channel_id=1, source_target_pairs={{0,24},{1,25},{2,26},{3,27},{4,28},{5,29},{6,30},{7,31},{8,16},{9,... | collective-permute-start | bytes 442376 | tf_op jit(solution)/shard_map/ppermute | solution.py:1010
  255.3 18.8 %collective-permute-start.23 = (bf16[48,1536]{1,0:T(8,128)(2,1)S(1)}, bf16[48,1536]{1,0:T(8,128)(2,1)S(1)}, u32[]{:S(2)}, u32[]{:S(2)}) collective-permute-start(bf16[48,1536]{1,0:T(8,128)(2,1)S(1)} %get-tuple-element.235), channel_id=1, source_target_pairs={{0,16},{1,17},{2,18},{3,19},{4,20},{5,21},{6,22},{7,23},{8,24},{9,... | collective-permute-start | bytes 442376 | tf_op jit(solution)/shard_map/ppermute | solution.py:1010
  255.3 18.8 %collective-permute-start.22 = (bf16[48,1536]{1,0:T(8,128)(2,1)S(1)}, bf16[48,1536]{1,0:T(8,128)(2,1)S(1)}, u32[]{:S(2)}, u32[]{:S(2)}) collective-permute-start(bf16[48,1536]{1,0:T(8,128)(2,1)S(1)} %get-tuple-element.236), channel_id=1, source_target_pairs={{0,8},{1,9},{2,10},{3,11},{4,12},{5,13},{6,14},{7,15},{8,0},{9,1},... | collective-permute-start | bytes 442376 | tf_op jit(solution)/shard_map/ppermute | solution.py:1010
  274.9 23.4 %collective-permute-start.26 = (bf16[16,48,2048]{2,1,0:T(8,128)(2,1)}, bf16[16,48,2048]{2,1,0:T(8,128)(2,1)S(1)}, u32[]{:S(2)}, u32[]{:S(2)}) collective-permute-start(bf16[16,48,2048]{2,1,0:T(8,128)(2,1)} %get-tuple-element.193), channel_id=1, source_target_pairs={{0,2},{1,3},{2,0},{3,1},{4,6},{5,7},{6,4},{7,5},{8,10},{9,11},{10,... | collective-permute-start | bytes 9437192 | tf_op jit(solution)/shard_map/ppermute | solution.py:1010
  275.0 23.4 %collective-permute-start.25 = (bf16[6,256,128]{2,1,0:T(8,128)(2,1)}, bf16[6,256,128]{2,1,0:T(8,128)(2,1)S(1)}, u32[]{:S(2)}, u32[]{:S(2)}) collective-permute-start(bf16[6,256,128]{2,1,0:T(8,128)(2,1)} %get-tuple-element.189), channel_id=1, source_target_pairs={{1,0},{3,2},{5,4},{7,6},{9,8},{11,10},{13,12},{15,14},{17,16},{19,... | collective-permute-start | bytes 1179656 | tf_op jit(solution)/shard_map/ppermute | solution.py:1010
  276.2 22.1 %copy-start = (bf16[16,48,2048]{2,1,0:T(8,128)(2,1)S(1)}, bf16[16,48,2048]{2,1,0:T(8,128)(2,1)}, u32[]{:S(2)}) copy-start(bf16[16,48,2048]{2,1,0:T(8,128)(2,1)} %get-tuple-element.191) | copy-start | bytes 9437188
  301.1 32.8 %collective-permute-start.27 = (bf16[8,48,2048]{2,1,0:T(8,128)(2,1)}, bf16[8,48,2048]{2,1,0:T(8,128)(2,1)S(1)}, u32[]{:S(2)}, u32[]{:S(2)}) collective-permute-start(bf16[8,48,2048]{2,1,0:T(8,128)(2,1)} %get-tuple-element.219), channel_id=1, source_target_pairs={{0,4},{1,5},{2,3},{3,2},{4,0},{5,1},{6,7},{7,6},{8,12},{9,13},{10,... | collective-permute-start | bytes 4718600 | tf_op jit(solution)/shard_map/ppermute | solution.py:1010
  335.5 4.2 %collective-permute-start.28 = (bf16[16,48,1280]{2,1,0:T(8,128)(2,1)S(1)}, bf16[16,48,1280]{2,1,0:T(8,128)(2,1)S(1)}, u32[]{:S(2)}, u32[]{:S(2)}) collective-permute-start(bf16[16,48,1280]{2,1,0:T(8,128)(2,1)S(1)} %copy-done.24), channel_id=1, source_target_pairs={{0,2},{1,3},{2,0},{3,1},{4,6},{5,7},{6,4},{7,5},{8,10},{9,11},{10,... | collective-permute-start | bytes 5898248 | tf_op jit(solution)/shard_map/ppermute | solution.py:1010
  336.1 16.4 %collective-permute-start.34 = (bf16[4,48,2048]{2,1,0:T(8,128)(2,1)S(1)}, bf16[4,48,2048]{2,1,0:T(8,128)(2,1)S(1)}, u32[]{:S(2)}, u32[]{:S(2)}) collective-permute-start(bf16[4,48,2048]{2,1,0:T(8,128)(2,1)S(1)} %get-tuple-element.225), channel_id=1, source_target_pairs={{0,1},{1,0},{2,6},{3,7},{4,5},{5,4},{6,2},{7,3},{8,9},{9,8},{10,14... | collective-permute-start | bytes 2359304 | tf_op jit(solution)/shard_map/ppermute | solution.py:1010
  340.2 17.7 %collective-permute-start.29 = (bf16[8,48,1280]{2,1,0:T(8,128)(2,1)S(1)}, bf16[8,48,1280]{2,1,0:T(8,128)(2,1)S(1)}, u32[]{:S(2)}, u32[]{:S(2)}) collective-permute-start(bf16[8,48,1280]{2,1,0:T(8,128)(2,1)S(1)} %get-tuple-element.224), channel_id=1, source_target_pairs={{0,4},{1,5},{2,3},{3,2},{4,0},{5,1},{6,7},{7,6},{8,12},{9,13},{10,... | collective-permute-start | bytes 2949128 | tf_op jit(solution)/shard_map/ppermute | solution.py:1010
  352.6 8.8 %collective-permute-start.35 = (bf16[48,2048]{1,0:T(8,128)(2,1)S(1)}, bf16[48,2048]{1,0:T(8,128)(2,1)S(1)}, u32[]{:S(2)}, u32[]{:S(2)}) collective-permute-start(bf16[48,2048]{1,0:T(8,128)(2,1)S(1)} %get-tuple-element.231), channel_id=1, source_target_pairs={{0,8},{1,9},{2,10},{3,11},{4,12},{5,13},{6,14},{7,15},{8,0},{9,1},... | collective-permute-start | bytes 589832 | tf_op jit(solution)/shard_map/ppermute | solution.py:1010
  352.7 12.1 %collective-permute-start.37 = (bf16[48,2048]{1,0:T(8,128)(2,1)S(1)}, bf16[48,2048]{1,0:T(8,128)(2,1)S(1)}, u32[]{:S(2)}, u32[]{:S(2)}) collective-permute-start(bf16[48,2048]{1,0:T(8,128)(2,1)S(1)} %get-tuple-element.232), channel_id=1, source_target_pairs={{0,24},{1,25},{2,26},{3,27},{4,28},{5,29},{6,30},{7,31},{8,16},{9,... | collective-permute-start | bytes 589832 | tf_op jit(solution)/shard_map/ppermute | solution.py:1010
  354.7 17.5 %collective-permute-start.36 = (bf16[48,2048]{1,0:T(8,128)(2,1)S(1)}, bf16[48,2048]{1,0:T(8,128)(2,1)S(1)}, u32[]{:S(2)}, u32[]{:S(2)}) collective-permute-start(bf16[48,2048]{1,0:T(8,128)(2,1)S(1)} %get-tuple-element.233), channel_id=1, source_target_pairs={{0,16},{1,17},{2,18},{3,19},{4,20},{5,21},{6,22},{7,23},{8,24},{9,... | collective-permute-start | bytes 589832 | tf_op jit(solution)/shard_map/ppermute | solution.py:1010
  358.1 14.9 %collective-permute-start.30 = (bf16[4,48,1280]{2,1,0:T(8,128)(2,1)S(1)}, bf16[4,48,1280]{2,1,0:T(8,128)(2,1)S(1)}, u32[]{:S(2)}, u32[]{:S(2)}) collective-permute-start(bf16[4,48,1280]{2,1,0:T(8,128)(2,1)S(1)} %get-tuple-element.230), channel_id=1, source_target_pairs={{0,1},{1,0},{2,6},{3,7},{4,5},{5,4},{6,2},{7,3},{8,9},{9,8},{10,14... | collective-permute-start | bytes 1474568 | tf_op jit(solution)/shard_map/ppermute | solution.py:1010
  373.1 5.8 %collective-permute-start.31 = (bf16[48,1280]{1,0:T(8,128)(2,1)S(1)}, bf16[48,1280]{1,0:T(8,128)(2,1)S(1)}, u32[]{:S(2)}, u32[]{:S(2)}) collective-permute-start(bf16[48,1280]{1,0:T(8,128)(2,1)S(1)} %get-tuple-element.238), channel_id=1, source_target_pairs={{0,8},{1,9},{2,10},{3,11},{4,12},{5,13},{6,14},{7,15},{8,0},{9,1},... | collective-permute-start | bytes 368648 | tf_op jit(solution)/shard_map/ppermute | solution.py:1010
  373.2 7.9 %collective-permute-start.33 = (bf16[48,1280]{1,0:T(8,128)(2,1)S(1)}, bf16[48,1280]{1,0:T(8,128)(2,1)S(1)}, u32[]{:S(2)}, u32[]{:S(2)}) collective-permute-start(bf16[48,1280]{1,0:T(8,128)(2,1)S(1)} %get-tuple-element.239), channel_id=1, source_target_pairs={{0,24},{1,25},{2,26},{3,27},{4,28},{5,29},{6,30},{7,31},{8,16},{9,... | collective-permute-start | bytes 368648 | tf_op jit(solution)/shard_map/ppermute | solution.py:1010
  375.2 10.5 %collective-permute-start.32 = (bf16[48,1280]{1,0:T(8,128)(2,1)S(1)}, bf16[48,1280]{1,0:T(8,128)(2,1)S(1)}, u32[]{:S(2)}, u32[]{:S(2)}) collective-permute-start(bf16[48,1280]{1,0:T(8,128)(2,1)S(1)} %get-tuple-element.240), channel_id=1, source_target_pairs={{0,16},{1,17},{2,18},{3,19},{4,20},{5,21},{6,22},{7,23},{8,24},{9,... | collective-permute-start | bytes 368648 | tf_op jit(solution)/shard_map/ppermute | solution.py:1010
  (16 other events, 27.3 us)

commit v3 on v2

--- a/solution.py
+++ b/solution.py
@@ -94,6 +94,66 @@
             out[slot(coords, z, y, c, half)] = product[pl.ds(begin, shard), :]
 
 
+class Weights:
+    def __init__(self, coords_ref, sources, held, out, sems, out_sems, halves):
+        self.coords = [coords_ref[place] for place in range(4)]
+        self.sources, self.held, self.out = sources, held, out
+        self.sems, self.out_sems, self.halves = sems, out_sems, halves
+
+    def copies(self, place):
+        half = self.halves[place]
+        if len(self.sources) == 1:
+            return [
+                pltpu.make_async_copy(
+                    self.sources[0].at[0, half], self.held.at[place], self.sems.at[place, 0]
+                )
+            ]
+        copies = []
+        shard = self.sources[0].shape[1]
+        for side, ref in enumerate(self.sources):
+            c = self.coords[2] if side == 0 else 1 - self.coords[2]
+            for group in range(8):
+                z, y = group // 2, group % 2
+                begin = pl.multiple_of((2 * group + c) * shard, 16)
+                copies.append(
+                    pltpu.make_async_copy(
+                        ref.at[slot(self.coords, z, y, c, half)],
+                        self.held.at[place, pl.ds(begin, shard), :],
+                        self.sems.at[place, side * 8 + group],
+                    )
+                )
+        return copies
+
+    def start(self, place):
+        for copy in self.copies(place):
+            copy.start()
+
+    def ready(self, place):
+        for copy in self.copies(place):
+            copy.wait()
+        self.leaving(place).start()
+
+    def leaving(self, place):
+        return pltpu.make_async_copy(
+            self.held.at[place], self.out.at[0, place], self.out_sems.at[place]
+        )
+
+    def left(self, place):
+        self.leaving(place).wait()
+
+    @staticmethod
+    def scratch(halves, width, columns):
+        return [
+            pltpu.VMEM((halves, width, columns), BF16),
+            pltpu.SemaphoreType.DMA((halves, 16)),
+            pltpu.SemaphoreType.DMA((halves,)),
+        ]
+
+
+def anywhere(count):
+    return [pl.BlockSpec(memory_space=pl.ANY)] * count
+
+
 def scalars():
     return pl.BlockSpec(memory_space=pltpu.SMEM)
 
@@ -116,9 +176,9 @@
 
 
 def pack_kernel(*refs):
-    q_ref, k_ref, v_ref, out_ref, down_ref = refs[:5]
-    thins = refs[5:-2]
-    first_ref, turned_ref = refs[-2:]
+    q_ref, k_ref, v_ref, out_ref = refs[:4]
+    thins = refs[4:-1]
+    first_ref = refs[-1]
     shard, part = q_ref.shape
 
     def chosen(columns, start):
@@ -126,10 +186,8 @@
         column = lax.broadcasted_iota(jnp.int32, (shard, columns), 1)
         return (row + start == column).astype(F32).astype(BF16)
 
-    for place, ref in enumerate((q_ref, k_ref, v_ref)):
+    for place, ref in enumerate((q_ref, k_ref, v_ref, out_ref)):
         first_ref[:, place * part : (place + 1) * part] = ref[...]
-    first_ref[:, 3 * part : 4 * part] = dot_nt(chosen(shard, 0), out_ref[...]).astype(BF16)
-    turned_ref[...] = dot_nt(chosen(shard, 0), down_ref[...]).astype(BF16)
     columns = jnp.zeros((shard, LANES), F32)
     lane = 0
     for ref in thins:
@@ -142,66 +200,90 @@
     first_ref[:, 4 * part :] = columns.astype(BF16)
 
 
-def pack(q, k, v, out, down, thins):
+def pack(q, k, v, out, thins):
     shard, part = q.shape
     return pl.pallas_call(
         pack_kernel,
-        out_shape=[
-            jax.ShapeDtypeStruct((shard, 4 * part + LANES), BF16),
-            jax.ShapeDtypeStruct((shard, down.shape[0]), BF16),
-        ],
+        out_shape=jax.ShapeDtypeStruct((shard, 4 * part + LANES), BF16),
         compiler_params=params(),
         cost_estimate=cost(1e8, 1e6),
         name="pack",
-    )(q, k, v, out, down, *[thin.reshape(1, -1) for thin in thins])
-
-
-def unpack_kernel(thin_ref, bias_ref, up_ref, vec_ref, *, shard, edge, each):
-    halves, width = thin_ref.shape[1], thin_ref.shape[2]
+    )(q, k, v, out, *[thin.reshape(1, -1) for thin in thins])
+
+
+def deal(columns, shard, size, turns):
+    count = columns.shape[0] // shard
+    runs = []
+    for place in range(count):
+        piece = columns[place * shard : place * shard + size]
+        for turn in range(turns):
+            runs.append(pltpu.roll(piece, LANES - turn, 1) if turn else piece)
+    return jnp.concatenate(runs, axis=0)
+
+
+def selectors_kernel(edge_ref, turn_ref, *, shard, edge, each):
+    width, part = edge_ref.shape
+    row = lax.broadcasted_iota(jnp.int32, (width, part), 0)
+    column = lax.broadcasted_iota(jnp.int32, (width, part), 1)
+    chosen = (row % shard < edge) & (row // shard * edge + row % shard == column)
+    edge_ref[...] = chosen.astype(F32).astype(BF16)
+    row = lax.broadcasted_iota(jnp.int32, (width, LANES), 0)
+    source = row // shard * (each * shard) + row % shard
+    lane = lax.broadcasted_iota(jnp.int32, (width, LANES), 1)
+    for turn in range(each):
+        for begin in range(0, each * width, LANES):
+            chosen = source + (turn * shard - begin) == lane
+            turn_ref[turn, :, begin : begin + LANES] = chosen.astype(F32).astype(BF16)
+
+
+def selectors(width, part, shard, edge, each):
+    return pl.pallas_call(
+        functools.partial(selectors_kernel, shard=shard, edge=edge, each=each),
+        out_shape=[
+            jax.ShapeDtypeStruct((width, part), BF16),
+            jax.ShapeDtypeStruct((each, width, each * width), BF16),
+        ],
+        compiler_params=params(),
+        cost_estimate=cost(1e8, 1e6),
+        name="selectors",
+    )()
+
+
+def unpack_kernel(thin_ref, turn_ref, up_ref, vec_ref, *, shard, each):
+    halves = thin_ref.shape[1]
     for half in range(halves):
         thin = thin_ref[0, half]
-        part = width // halves
-        row = lax.broadcasted_iota(jnp.int32, (width, part), 0)
-        column = lax.broadcasted_iota(jnp.int32, (width, part), 1)
-        chosen = (row % shard < edge) & (row // shard * edge + row % shard == column)
-        bias_ref[half] = dot_tn(thin, chosen.astype(F32).astype(BF16))[:8]
-        units = each * width
-        row = lax.broadcasted_iota(jnp.int32, (width, units), 0)
-        column = lax.broadcasted_iota(jnp.int32, (width, units), 1)
-        lane = lax.broadcasted_iota(jnp.int32, (LANES, units), 0)
-        rows = jnp.zeros((8, units), F32)
+        if shard % 16 == 0:
+            turned = deal(thin.astype(F32), shard, shard, each).T
+            up_ref[half] = turned[0:8]
+            continue
+        rows = jnp.zeros((8, turn_ref.shape[2]), F32)
         for turn in range(each):
-            chosen = row // shard * (each * shard) + turn * shard + row % shard == column
-            picked = dot_tn(thin, chosen.astype(F32).astype(BF16))
-            picked = jnp.where(lane == 3 + turn, picked, 0.0)
-            rows = rows + jnp.sum(picked, axis=0, keepdims=True)
+            picked = dot_tn(thin, turn_ref[turn])
+            rows = rows + picked[3 + turn : 4 + turn]
         up_ref[half] = rows
-    row = lax.broadcasted_iota(jnp.int32, (width, width), 0)
-    column = lax.broadcasted_iota(jnp.int32, (width, width), 1)
-    turned = dot_tn(thin_ref[0, 0], (row == column).astype(F32).astype(BF16))
+    turned = thin_ref[0, 0].astype(F32).T
     vec_ref[...] = turned[3 + each : 11 + each]
 
 
-def unpack(w, shard, each):
+def unpack(w, turns, shard, each):
     _, halves, width, columns = w.shape
     return pl.pallas_call(
-        functools.partial(unpack_kernel, shard=shard, edge=shard // halves, each=each),
+        functools.partial(unpack_kernel, shard=shard, each=each),
         grid=(1,),
         in_specs=[
-            pl.BlockSpec((1, halves, width, LANES), lambda i: (0, 0, 0, columns // LANES - 1))
-        ],
-        out_specs=[
-            whole((halves, 8, width // halves)), whole((halves, 8, each * width)), whole((8, width))
-        ],
+            pl.BlockSpec((1, halves, width, LANES), lambda i: (0, 0, 0, columns // LANES - 1)),
+            whole(turns.shape),
+        ],
+        out_specs=[whole((halves, 8, each * width)), whole((8, width))],
         out_shape=[
-            jax.ShapeDtypeStruct((halves, 8, width // halves), F32),
             jax.ShapeDtypeStruct((halves, 8, each * width), F32),
             jax.ShapeDtypeStruct((8, width), F32),
         ],
         compiler_params=params(),
         cost_estimate=cost(1e8, 1e6),
         name="unpack",
-    )(w)
+    )(w, turns)
 
 
 def join_kernel(*refs):
@@ -220,23 +302,44 @@
 
 
 def project_kernel(
-    x_ref, w_ref, b_ref, cos_ref, sin_ref,
-    sq_ref, sk_ref, v_ref, gq_ref, gk_ref, st_ref, tot_ref,
-    *, block, step,
+    coords_ref, *refs, block, step, shard, halves
 ):
+    sources, refs = refs[: len(refs) - 14], refs[len(refs) - 14 :]
+    x_ref, edge_ref, cos_ref, sin_ref, sq_ref, sk_ref, v_ref, gq_ref, gk_ref, st_ref, tot_ref = refs[:11]
+    sources, out_ref = sources[:-1], sources[-1]
+    held_ref, sems, out_sems = refs[11:]
     rows = x_ref.shape[0]
     part = sq_ref.shape[1]
-    weights = flat(w_ref)
+    now = pl.program_id(0)
+    weights = Weights(coords_ref, sources, held_ref, out_ref, sems, out_sems, range(halves))
+
+    @pl.when(now == 0)
+    def _():
+        for half in range(halves):
+            weights.start(half)
+
+    for half in range(halves):
+
+        @pl.when(now == half)
+        def _():
+            weights.ready(half)
+
+    columns = held_ref.shape[2]
+    thin = held_ref[now, :, columns - LANES :]
+    if shard % 16 == 0:
+        biases = deal(thin.astype(F32), shard, shard * part // x_ref.shape[1], 1).T
+    else:
+        biases = dot_tn(thin, edge_ref[...])
 
     def body(index, carry):
         here = pl.ds(index * step, step)
-        sums = dot(x_ref[here, :], weights)
+        sums = dot(x_ref[here, :], held_ref[now, :, : 3 * part])
         for place, (feature_ref, slope_ref) in enumerate(((sq_ref, gq_ref), (sk_ref, gk_ref))):
-            value = sums[:, place * part : (place + 1) * part] + b_ref[0, place : place + 1, :]
+            value = sums[:, place * part : (place + 1) * part] + biases[place : place + 1]
             positive = jnp.maximum(value, 0.0) + jnp.log1p(jnp.exp(-jnp.abs(value)))
             feature_ref[here, :] = positive.astype(BF16)
             slope_ref[here, :] = jax.nn.sigmoid(value).astype(BF16)
-        v_ref[here, :] = (sums[:, 2 * part :] + b_ref[0, 2:3, :]).astype(BF16)
+        v_ref[here, :] = (sums[:, 2 * part :] + biases[2:3]).astype(BF16)
         return carry
 
     lax.fori_loop(0, rows // step, body, 0)
@@ -254,40 +357,54 @@
             total = total + state
         tot_ref[pair] = compact(total).astype(BF16)
 
-
-def project(x, w, biases, cosines, sines, block):
+    @pl.when(now == halves - 1)
+    def _():
+        for half in range(halves):
+            weights.left(half)
+
+
+def project(coords, x, sources, columns, edges, cosines, sines, block, shard, halves):
     rows, width = x.shape
-    groups, halves, shard, _ = w.shape
     part = width // halves
     pairs = width // LANES
     half = pairs // halves
     blocks = rows // block
     row_spec = pl.BlockSpec((rows, part), lambda t: (0, t))
     full = jax.ShapeDtypeStruct((rows, width), BF16)
-    return pl.pallas_call(
-        functools.partial(project_kernel, block=block, step=256),
+
+    def kernel(coords_ref, *refs):
+        count = len(sources)
+        others, outs, scratch = refs[count : count + 4], refs[count + 4 : -3], refs[-3:]
+        project_kernel(
+            coords_ref, *refs[:count], outs[-1], *others, *outs[:-1], *scratch,
+            block=block, step=rows, shard=shard, halves=halves,
+        )
+
+    return pl.pallas_call(
+        kernel,
         grid=(halves,),
-        in_specs=[
-            whole((rows, width)),
-            pl.BlockSpec((groups, 1, shard, 3 * part), lambda t: (0, t, 0, 0)),
-            pl.BlockSpec((1, 8, part), lambda t: (t, 0, 0)),
-            whole((rows, LANES)),
-            whole((rows, LANES)),
+        in_specs=[scalars()]
+        + anywhere(len(sources))
+        + [
+            whole((rows, width)), whole(edges.shape), whole((rows, LANES)), whole((rows, LANES)),
         ],
         out_specs=[
             row_spec, row_spec, row_spec, row_spec, row_spec,
             pl.BlockSpec((blocks, half, 2 * LANES, 2 * LANES), lambda t: (0, t, 0, 0)),
             pl.BlockSpec((half, 2 * LANES, LANES), lambda t: (t, 0, 0)),
-        ],
+        ]
+        + anywhere(1),
         out_shape=[
             full, full, full, full, full,
             jax.ShapeDtypeStruct((blocks, pairs, 2 * LANES, 2 * LANES), BF16),
             jax.ShapeDtypeStruct((pairs, 2 * LANES, LANES), BF16),
-        ],
+            jax.ShapeDtypeStruct((1, halves, width, columns), BF16),
+        ],
+        scratch_shapes=Weights.scratch(halves, width, columns),
         compiler_params=params(),
         cost_estimate=cost(2 * rows * width * 3 * width, 16e6),
         name="project",
-    )(x, w, biases, cosines, sines)
+    )(coords, *sources, x, edges, cosines, sines)
 
 
 def attend_kernel(sq_ref, sk_ref, v_ref, cm_ref, cos_ref, sin_ref, st_ref, num_ref, den_ref):
@@ -417,12 +534,23 @@
     return inner * scale
 
 
-def lift_kernel(low_ref, up_ref, bias_ref, act_ref, slope_ref, *, step):
-    up = up_ref[0, 0]
+def lift_kernel(coords_ref, *refs, step, row, half):
+    sources, refs = refs[:-8], refs[-8:]
+    low_ref, bias_ref, act_ref, slope_ref, out_ref, held_ref, sems, out_sems = refs
+    tile = act_ref.shape[1]
+    now = pl.program_id(0)
+    weights = Weights(coords_ref, sources, held_ref, out_ref, sems, out_sems, [half])
+
+    @pl.when(now == 0)
+    def _():
+        weights.start(0)
+        weights.ready(0)
+
+    up = held_ref[0, :, pl.ds(pl.multiple_of(now * tile, tile), tile)]
 
     def body(place, carry):
         here = pl.ds(place * step, step)
-        lifted = dot(low_ref[here, :], up) + bias_ref[0, 0:1, :]
+        lifted = dot(low_ref[here, :], up) + bias_ref[0, row : row + 1, :]
         share = 0.5 + 0.5 * lax.erf(lifted * math.sqrt(0.5))
         bell = jnp.exp(-0.5 * lifted * lifted) * (1.0 / math.sqrt(2.0 * math.pi))
         act_ref[here, :] = (lifted * share).astype(BF16)
@@ -431,39 +559,47 @@
 
     lax.fori_loop(0, low_ref.shape[0] // step, body, 0, unroll=True)
 
-
-def lift(low, w, bias, half, units, tile):
+    @pl.when(now == pl.num_programs(0) - 1)
+    def _():
+        weights.left(0)
+
+
+def lift(coords, low, sources, bias, half, units, tile, row):
     rows, width = low.shape
-    tiles = units // tile
     unit_spec = pl.BlockSpec((rows, tile), lambda i: (0, i))
     shape = jax.ShapeDtypeStruct((rows, units), BF16)
     return pl.pallas_call(
-        functools.partial(lift_kernel, step=256),
-        grid=(tiles,),
-        in_specs=[
-            whole((rows, width)),
-            pl.BlockSpec((1, 1, width, tile), lambda i: (0, half, 0, i)),
-            pl.BlockSpec((1, 8, tile), lambda i: (half, 0, i)),
-        ],
-        out_specs=[unit_spec, unit_spec],
-        out_shape=[shape, shape],
+        functools.partial(lift_kernel, step=256, row=row, half=half),
+        grid=(units // tile,),
+        in_specs=[scalars()]
+        + anywhere(len(sources))
+        + [whole((rows, width)), pl.BlockSpec((1, 8, tile), lambda i: (half, 0, i))],
+        out_specs=[unit_spec, unit_spec] + anywhere(1),
+        out_shape=[shape, shape, jax.ShapeDtypeStruct((1, 1, width, units), BF16)],
+        scratch_shapes=Weights.scratch(1, width, units),
         compiler_params=params(),
         cost_estimate=cost(2 * rows * width * units, 10e6),
         name="lift",
-    )(low, w, bias)
-
-
-def drop_kernel(*refs):
-    acts = refs[:-8]
-    down_ref, normal_ref, vec_ref, grad_ref, out_ref, branch_ref, second_ref, sum_ref = refs[-8:]
+    )(coords, *sources, low, bias)
+
+
+def drop_kernel(coords_ref, *refs, halves):
+    sources, acts, refs = refs[: -11 - halves], refs[-11 - halves : -11], refs[-11:]
+    normal_ref, vec_ref, grad_ref, out_ref, branch_ref, second_ref, sum_ref = refs[:7]
+    whole_ref, held_ref, sems, out_sems = refs[7:]
+    weights = Weights(coords_ref, sources, held_ref, whole_ref, sems, out_sems, range(halves))
 
     @pl.when(pl.program_id(0) == 0)
     def _():
         sum_ref[...] = jnp.zeros_like(sum_ref)
+        for half in range(halves):
+            weights.start(half)
+        for half in range(halves):
+            weights.ready(half)
 
     total = normal_ref[...] * vec_ref[1:2, :] + vec_ref[2:3, :] + vec_ref[3:4, :]
     for half, act_ref in enumerate(acts):
-        total = total + dot_nt(act_ref[...], down_ref[0, half])
+        total = total + dot_nt(act_ref[...], held_ref[half])
     normal, scale = norm_rows(total)
     gain = vec_ref[4:5, :]
     out_ref[...] = (normal * gain + vec_ref[5:6, :]).astype(BF16)
@@ -475,27 +611,36 @@
     sum_ref[1:2, :] += jnp.sum(upstream, axis=0, keepdims=True)
     sum_ref[2:3, :] += jnp.sum(second, axis=0, keepdims=True)
 
-
-def drop(act, w, normal, vectors, grad, units, step):
+    @pl.when(pl.program_id(0) == pl.num_programs(0) - 1)
+    def _():
+        for half in range(halves):
+            weights.left(half)
+
+
+def drop(coords, act, sources, normal, vectors, grad, units, step):
     rows, width = normal.shape
-    halves = w.shape[1]
+    halves = len(act)
     wide = pl.BlockSpec((step, width), lambda i: (i, 0))
     return pl.pallas_call(
-        drop_kernel,
+        functools.partial(drop_kernel, halves=halves),
         grid=(rows // step,),
-        in_specs=[pl.BlockSpec((step, units), lambda i: (i, 0))] * halves
-        + [whole((1, halves, width, units)), wide, whole(vectors.shape), wide],
-        out_specs=[wide, wide, wide, whole((8, width))],
+        in_specs=[scalars()]
+        + anywhere(len(sources))
+        + [pl.BlockSpec((step, units), lambda i: (i, 0))] * halves
+        + [wide, whole(vectors.shape), wide],
+        out_specs=[wide, wide, wide, whole((8, width))] + anywhere(1),
         out_shape=[
             jax.ShapeDtypeStruct((rows, width), BF16),
             jax.ShapeDtypeStruct((rows, width), BF16),
             jax.ShapeDtypeStruct((rows, width), F32),
             jax.ShapeDtypeStruct((8, width), F32),
-        ],
+            jax.ShapeDtypeStruct((1, halves, width, units), BF16),
+        ],
+        scratch_shapes=Weights.scratch(halves, width, units),
         compiler_params=params(),
         cost_estimate=cost(2 * rows * width * halves * units, 20e6),
         name="drop",
-    )(*act, w, normal, vectors, grad)
+    )(coords, *sources, *act, normal, vectors, grad)
 
 
 def piece_outputs(layout, tile, index_map):
@@ -511,16 +656,10 @@
 
 
 def wide_gradient_kernel(coords_ref, left_ref, *refs, halves):
-    rights, outs = refs[:halves], refs[halves:-2]
-    turned_ref, product_ref = refs[-2:]
+    rights, outs, product_ref = refs[:halves], refs[halves:-1], refs[-1]
     coords = [coords_ref[place] for place in range(4)]
-
-    @pl.when(pl.program_id(0) == 0)
-    def _():
-        turned_ref[...] = left_ref[...].T
-
     for half, right_ref in enumerate(rights):
-        product_ref[...] = dot(turned_ref[...], right_ref[...]).astype(BF16)
+        product_ref[...] = dot_tn(left_ref[...], right_ref[...]).astype(BF16)
         emit(product_ref, half, outs, coords)
 
 
@@ -538,7 +677,7 @@
         ],
         out_specs=out_specs,
         out_shape=out_shapes,
-        scratch_shapes=[pltpu.VMEM((width, rows), BF16), pltpu.VMEM((width, tile), BF16)],
+        scratch_shapes=[pltpu.VMEM((width, tile), BF16)],
         compiler_params=params(),
         cost_estimate=cost(2 * rows * width * halves * units, 18e6),
         name=name,
@@ -583,16 +722,17 @@
 
 
 def lower_kernel(*refs):
-    gls = refs[:-8]
-    up_ref, second_ref, normal_ref, scale_ref, vec_ref, first_ref, firstlow_ref, sum_ref = refs[-8:]
+    count = (len(refs) - 7) // 2
+    gls, ups = refs[:count], refs[count : 2 * count]
+    second_ref, normal_ref, scale_ref, vec_ref, first_ref, firstlow_ref, sum_ref = refs[-7:]
 
     @pl.when(pl.program_id(0) == 0)
     def _():
         sum_ref[...] = jnp.zeros_like(sum_ref)
 
     upstream = second_ref[...]
-    for half, gl_ref in enumerate(gls):
-        upstream = upstream + dot_nt(gl_ref[...], up_ref[0, half])
+    for gl_ref, up_ref in zip(gls, ups):
+        upstream = upstream + dot_nt(gl_ref[...], up_ref[0, 0])
     normal = normal_ref[...]
     first = norm_back(upstream, normal, scale_ref[:, 0:1], vec_ref[1:2, :])
     first_ref[...] = first
@@ -604,14 +744,17 @@
 
 def lower(gl, w, second, normal, scale, vectors, units, step):
     rows, width = second.shape
-    halves = w.shape[1]
+    halves = len(w)
     wide = pl.BlockSpec((step, width), lambda i: (i, 0))
     return pl.pallas_call(
         lower_kernel,
         grid=(rows // step,),
         in_specs=[pl.BlockSpec((step, units), lambda i: (i, 0))] * halves
         + [
-            whole((1, halves, width, units)), wide, wide,
+            whole((1, 1, width, units)) for half in range(halves)
+        ]
+        + [
+            wide, wide,
             pl.BlockSpec((step, LANES), lambda i: (i, 0)), whole(vectors.shape),
         ],
         out_specs=[wide, wide, whole((8, width))],
@@ -623,12 +766,12 @@
         compiler_params=params(),
         cost_estimate=cost(2 * rows * width * halves * units, 20e6),
         name="lower",
-    )(*gl, w, second, normal, scale, vectors)
+    )(*gl, *w, second, normal, scale, vectors)
 
 
 def unmix_kernel(
     coords_ref, first_ref, mixed_ref, rden_ref, sq_ref, cos_ref, sin_ref, w_ref,
-    sum1_ref, sum2_ref, *refs, block, step, shard, halves
+    sum1_ref, sum2_ref, turn_ref, *refs, block, step, shard, halves
 ):
     biases = [ref[0:1, :] for ref in refs[:halves]]
     refs = refs[halves:]
@@ -646,6 +789,8 @@
     group_row = lax.broadcasted_iota(jnp.int32, (LANES, LANES), 0)
     group_lane = lax.broadcasted_iota(jnp.int32, (LANES, LANES), 1)
     group = (group_row // HEAD_DIM == group_lane // HEAD_DIM).astype(F32).astype(BF16)
+    group = jnp.concatenate([group, group], axis=0)
+
     lane = lax.broadcasted_iota(jnp.int32, (step, LANES), 1) % HEAD_DIM
 
     def body(place, carry):
@@ -658,7 +803,7 @@
             product = scaled * mixed_ref[here, lanes].astype(F32)
             high = product.astype(BF16)
             rest = (product - high.astype(F32)).astype(BF16)
-            inner = dot(high, group) + dot(rest, group)
+            inner = dot(jnp.concatenate([high, rest], axis=1), group)
             slope = jnp.where(inverse < 1.0, -inner, 0.0)
             high = slope.astype(BF16).astype(F32)
             gn_ref[here, lanes] = scaled.astype(BF16)
@@ -669,25 +814,30 @@
 
     lax.fori_loop(0, rows // step, body, 0)
     product_ref[:, :part] = dot_tn(first_ref[...], mixed_ref[...]).astype(BF16)
-    side_row = lax.broadcasted_iota(jnp.int32, (8, LANES), 0)
-    side_lane = lax.broadcasted_iota(jnp.int32, (8, LANES), 1)
-
-    def pick(first_lane, count):
-        chosen = (side_row < count) & (side_row + first_lane == side_lane)
-        return chosen.astype(F32).astype(BF16)
-
-    columns = dot_tn(sum1_ref[...].astype(BF16), pick(0, 3))
-    columns = columns + dot_tn(sum2_ref[...].astype(BF16), pick(3, 3))
-    turned = dot_tn(bias.astype(BF16), (side_row == 0).astype(F32).astype(BF16)).astype(BF16)
-    each = bias.shape[1] // width
-    row = lax.broadcasted_iota(jnp.int32, (width, each * width), 0)
-    column = lax.broadcasted_iota(jnp.int32, (width, each * width), 1)
-    for turn in range(each):
-        source = row // shard * (each * shard) + turn * shard + row % shard
-        chosen = (source == column).astype(F32).astype(BF16)
+    row = lax.broadcasted_iota(jnp.int32, (8, width), 0)
+    packed = jnp.where(row < 3, sum1_ref[...], pltpu.roll(sum2_ref[...], 3, 0))
+    packed = jnp.where(row < 6, packed, 0.0)
+    columns = jnp.concatenate([packed, jnp.zeros((LANES - 8, width), F32)], axis=0).T
+    units = bias.shape[1]
+    each = units // width
+    if shard % 16 == 0:
+        at = lax.broadcasted_iota(jnp.int32, (8, units), 0)
+        both = jnp.where(at >= 6, bias, 0.0)
+        turned = jnp.concatenate([both, jnp.zeros((LANES - 8, units), F32)], axis=0).T
+        lane_at = lax.broadcasted_iota(jnp.int32, (shard, LANES), 1)
+        for place in range(width // shard):
+            piece = columns[place * shard : (place + 1) * shard]
+            for turn in range(each):
+                begin = (place * each + turn) * shard
+                piece = jnp.where(lane_at == 6 + turn, turned[begin : begin + shard], piece)
+            product_ref[place * shard : (place + 1) * shard, part:] = piece.astype(BF16)
+    else:
+        side_row = lax.broadcasted_iota(jnp.int32, (8, LANES), 0)
+        turned = dot_tn(bias.astype(BF16), (side_row == 0).astype(F32).astype(BF16)).astype(BF16)
         lane_at = lax.broadcasted_iota(jnp.int32, (width, LANES), 1)
-        columns = jnp.where(lane_at == 6 + turn, dot(chosen, turned), columns)
-    product_ref[:, part:] = columns.astype(BF16)
+        for turn in range(each):
+            columns = jnp.where(lane_at == 6 + turn, dot(turn_ref[turn], turned), columns)
+        product_ref[:, part:] = columns.astype(BF16)
     emit(product_ref, pl.program_id(0), outs, coords)
     keep = same_head(2 * LANES, 2 * LANES)
     for pair in range(part // LANES):
@@ -706,7 +856,7 @@
 
 
 def unmix(
-    coords, first, mixed, rden, sq, cosines, sines, w, sums1, sums2, gbias, partial, layout, block
+    coords, first, mixed, rden, sq, cosines, sines, w, sums1, sums2, turns, gbias, partial, layout, block
 ):
     rows, width = first.shape
     groups, halves, shard, _ = w.shape
@@ -721,18 +871,18 @@
     full = jax.ShapeDtypeStruct((rows, width), BF16)
     return pl.pallas_call(
         functools.partial(
-            unmix_kernel, block=block, step=256, shard=layout[2], halves=halves
+            unmix_kernel, block=block, step=512, shard=layout[2], halves=halves
         ),
         grid=(halves,),
         in_specs=[
             scalars(), whole((rows, width)), row_spec, row_spec, row_spec,
             whole((rows, LANES)), whole((rows, LANES)),
             pl.BlockSpec((groups, 1, shard, part), lambda t: (0, t, 0, 3)),
-            whole((8, width)), whole((8, width)),
+            whole((8, width)), whole((8, width)), whole(turns.shape),
         ]
         + [whole((8, units))] * halves
         + [pl.BlockSpec(memory_space=pl.ANY)] * len(partial),
-        input_output_aliases={10 + halves + at: at for at in range(len(partial))},
+        input_output_aliases={11 + halves + at: at for at in range(len(partial))},
         out_specs=out_specs
         + [
             row_spec, row_spec,
@@ -749,7 +899,7 @@
         compiler_params=params(),
         cost_estimate=cost(4 * rows * width * width, 16e6),
         name="unmix",
-    )(coords, first, mixed, rden, sq, cosines, sines, w, sums1, sums2, *gbias, *partial)
+    )(coords, first, mixed, rden, sq, cosines, sines, w, sums1, sums2, turns, *gbias, *partial)
 
 
 def unattend_kernel(
@@ -849,21 +999,10 @@
     )(sq, sk, v, gn, gd, cm, cosines, sines, states, incoming, later, slope_q, *partial)
 
 
-def finish_kernel(
-    coords_ref, x_ref, q_ref, dk_ref, dv_ref, sk_ref, v_ref, gk_ref, cos_ref, sin_ref, in_ref,
-    *refs, shard
+def tail_kernel(
+    dk_ref, dv_ref, sk_ref, v_ref, gk_ref, cos_ref, sin_ref, in_ref, key_ref, value_ref
 ):
-    outs = refs[:-4]
-    key_ref, value_ref, turned_ref, product_ref = refs[-4:]
-    coords = [coords_ref[place] for place in range(4)]
-    rows, part = q_ref.shape
-    width = x_ref.shape[1]
-
-    @pl.when(pl.program_id(0) == 0)
-    def _():
-        turned_ref[...] = x_ref[...].T
-
-    product_ref[:, :part] = dot(turned_ref[...], q_ref[...]).astype(BF16)
+    rows, part = dk_ref.shape
     ones = jnp.ones((rows, LANES), BF16)
     cosines, sines = cos_ref[...], sin_ref[...]
     for pair in range(part // LANES):
@@ -874,44 +1013,67 @@
         key_ref[:, lanes] = (keys * gk_ref[:, lanes].astype(F32)).astype(BF16)
         features = turned_features(sk_ref[:, lanes], cosines, sines)
         value_ref[:, lanes] = (dv_ref[:, lanes] + dot(features, state[:, :LANES])).astype(BF16)
-    product_ref[:, part : 2 * part] = dot(turned_ref[...], key_ref[...]).astype(BF16)
-    product_ref[:, 2 * part : 3 * part] = dot(turned_ref[...], value_ref[...]).astype(BF16)
+
+
+def tail(dk, dv, sk, v, slope_k, cosines, sines, incoming):
+    rows, width = sk.shape
+    spec = pl.BlockSpec((rows, LANES), lambda p: (0, p))
+    full = jax.ShapeDtypeStruct((rows, width), BF16)
+    return pl.pallas_call(
+        tail_kernel,
+        grid=(width // LANES,),
+        in_specs=[
+            spec, spec, spec, spec, spec, whole((rows, LANES)), whole((rows, LANES)),
+            pl.BlockSpec((1, 2 * LANES, LANES), lambda p: (p, 0, 0)),
+        ],
+        out_specs=[spec, spec],
+        out_shape=[full, full],
+        compiler_params=params(),
+        cost_estimate=cost(2e9, 14e6),
+        name="tail",
+    )(dk, dv, sk, v, slope_k, cosines, sines, incoming)
+
+
+def weights_kernel(coords_ref, x_ref, q_ref, k_ref, v_ref, edge_ref, *refs, shard):
+    outs, product_ref = refs[:-1], refs[-1]
+    coords = [coords_ref[place] for place in range(4)]
+    rows, part = q_ref.shape
+    width = x_ref.shape[1]
+    ones = jnp.ones((rows, LANES), BF16)
     lane = lax.broadcasted_iota(jnp.int32, (part, LANES), 1)
     sums = jnp.zeros((part, LANES), F32)
-    for place, ref in enumerate((q_ref, key_ref, value_ref)):
+    for place, ref in enumerate((q_ref, k_ref, v_ref)):
+        at = slice(place * part, (place + 1) * part)
+        product_ref[:, at] = dot_tn(x_ref[...], ref[...]).astype(BF16)
         sums = jnp.where(lane == place, dot_tn(ref[...], ones), sums)
-    edge = shard * part // width
-    row = lax.broadcasted_iota(jnp.int32, (width, part), 0)
-    column = lax.broadcasted_iota(jnp.int32, (width, part), 1)
-    source = row // shard * edge + row % shard
-    chosen = (row % shard < edge) & (source == column)
-    product_ref[:, 3 * part :] = dot(chosen.astype(F32).astype(BF16), sums.astype(BF16)).astype(BF16)
+    if shard % 16 == 0:
+        edge = shard * part // width
+        for place in range(width // shard):
+            piece = jnp.concatenate(
+                [sums[place * edge : (place + 1) * edge], jnp.zeros((shard - edge, LANES), F32)], axis=0
+            )
+            product_ref[place * shard : (place + 1) * shard, 3 * part :] = piece.astype(BF16)
+    else:
+        product_ref[:, 3 * part :] = dot(edge_ref[...], sums.astype(BF16)).astype(BF16)
     emit(product_ref, pl.program_id(0), outs, coords)
 
 
-def finish(coords, x, q, dk, dv, sk, v, slope_k, cosines, sines, incoming, layout):
+def weight_gradients(coords, x, q, k, v, edges, layout):
     rows, width = x.shape
-    halves, shard = layout[1], layout[2]
-    part = width // halves
-    half = incoming.shape[0] // halves
-    spec = pl.BlockSpec((rows, part), lambda t: (0, t))
-    full = jax.ShapeDtypeStruct((rows, width), BF16)
+    halves = layout[1]
+    spec = pl.BlockSpec((rows, width // halves), lambda t: (0, t))
     out_specs, out_shapes = piece_outputs(layout, layout[3], lambda t: 0)
     return pl.pallas_call(
-        functools.partial(finish_kernel, shard=shard),
+        functools.partial(weights_kernel, shard=layout[2]),
         grid=(halves,),
-        in_specs=[
-            scalars(), whole((rows, width)), spec, spec, spec, spec, spec, spec,
-            whole((rows, LANES)), whole((rows, LANES)),
-            pl.BlockSpec((half, 2 * LANES, LANES), lambda t: (t, 0, 0)),
-        ],
-        out_specs=out_specs + [spec, spec],
-        out_shape=out_shapes + [full, full],
-        scratch_shapes=[pltpu.VMEM((width, rows), BF16), pltpu.VMEM((width, layout[3]), BF16)],
+        in_specs=[scalars(), whole((rows, width)), spec, spec, spec, whole(edges.shape)],
+        out_specs=out_specs,
+        out_shape=out_shapes,
+        scratch_shapes=[pltpu.VMEM((width, layout[3]), BF16)],
         compiler_params=params(),
         cost_estimate=cost(2 * rows * width * 3 * width, 10e6),
-        name="finish",
-    )(coords, x, q, dk, dv, sk, v, slope_k, cosines, sines, incoming)
+        name="weight_gradients",
+    )(coords, x, q, k, v, edges)
 
 
 def inputs_kernel(first_ref, q_ref, k_ref, v_ref, w_ref, out_ref):
@@ -947,44 +1109,6 @@
     )(first, q, k, v, w)
 
 
-def assemble_kernel(coords_ref, own_ref, other_ref, out_ref, sems):
-    coords = [coords_ref[place] for place in range(4)]
-    count, shard, _ = own_ref.shape
-    copies = []
-    for side, ref in enumerate((own_ref, other_ref)):
-        c = coords[2] if side == 0 else 1 - coords[2]
-        for index in range(count):
-            across, beside, z = index // 8, index // 4 % 2, (index % 4) ^ coords[0]
-            y = coords[1] ^ jnp.where(c == 0, across, beside)
-            x = coords[3] ^ jnp.where(c == 0, beside, across)
-            begin = pl.multiple_of((z * 4 + y * 2 + c) * shard, 16)
-            copy = pltpu.make_async_copy(
-                ref.at[index],
-                out_ref.at[0, x, pl.ds(begin, shard), :],
-                sems.at[side * count + index],
-            )
-            copy.start()
-            copies.append(copy)
-    for copy in copies:
-        copy.wait()
-
-
-def assemble(coords, own, other):
-    count, shard, columns = own.shape
-    return pl.pallas_call(
-        assemble_kernel,
-        in_specs=[
-            scalars(), pl.BlockSpec(memory_space=pl.ANY), pl.BlockSpec(memory_space=pl.ANY)
-        ],
-        out_specs=pl.BlockSpec(memory_space=pltpu.VMEM),
-        out_shape=jax.ShapeDtypeStruct((1, 2, count * shard, columns), BF16),
-        scratch_shapes=[pltpu.SemaphoreType.DMA((2 * count,))],
-        compiler_params=params(),
-        cost_estimate=cost(0, 4 * count * shard * columns * 2),
-        name="assemble",
-    )(coords, own, other)
-
-
 def moves():
     def table(change):
         pairs = []
@@ -1020,14 +1144,17 @@
         parts = [send(self.held, self.tables[0][k], begin, end) for k in (1, 2, 3)]
         self.held = join([self.held] + parts)
 
+    def line_parts(self, begin):
+        self.held = self.held, [send(self.held, self.tables[0][k], begin, ()) for k in (1, 2, 3)]
+
     def beside(self, begin=(), end=()):
         self.held = jnp.concatenate([self.held, send(self.held, self.tables[1], begin, end)], axis=0)
 
     def across(self, begin=(), end=()):
         self.held = jnp.concatenate([self.held, send(self.held, self.tables[2], begin, end)], axis=0)
 
-    def core(self, coords, begin=(), end=()):
-        return assemble(coords, self.held, send(self.held, self.tables[3], begin, end))
+    def core(self, begin=(), end=()):
+        return [self.held, send(self.held, self.tables[3], begin, end)]
 
 
 class Sum:
@@ -1097,12 +1224,16 @@
     cosines = jnp.broadcast_to(cosines[:, None], (rows, LANES))
     sines = jnp.broadcast_to(sines[:, None], (rows, LANES))
 
-    each = units // width
+    each, edge = units // width, shard // halves
+    if pieces:
+        edges, turns = jnp.zeros((8, LANES), BF16), jnp.zeros((1, 8, LANES), BF16)
+    else:
+        edges, turns = selectors(width, part, shard, edge, each)
     thins = (
         b_query, b_key, b_value, b_up, b_out, norm_gain, norm_shift, b_down, final_gain, final_shift
     )
     if pieces:
-        attention_shard, down_shard = pack(w_query, w_key, w_value, w_out, w_down, thins)
+        attention_shard = pack(w_query, w_key, w_value, w_out.T, thins)
     else:
         columns = []
         for thin in thins:
@@ -1111,7 +1242,7 @@
         columns = jnp.concatenate(columns, axis=1)
         columns = jnp.pad(columns, ((0, 0), (0, LANES - columns.shape[1])))
         attention_shard = jnp.concatenate([w_query, w_key, w_value, w_out.T, columns], axis=1)
-        down_shard = w_down.T
+    down_shard = w_down.T
 
     def gather_all(piece):
         everything = lax.all_gather(piece, BOTH, axis=0, tiled=False)
@@ -1124,82 +1255,89 @@
         four = first_chunk.held
         first_chunk.beside()
         up_chunk.line([four])
-        first_chunk.across([cm, cosines, sines])
+        first_chunk.across([cm, cosines, sines, coords])
         sixteen = first_chunk.held
-        w_attention = first_chunk.core(coords)
+        four = up_chunk.held
+        w_attention = first_chunk.core([four])
+        up_chunk.beside([sixteen, four], w_attention)
+        eight = up_chunk.held
+        down_chunk.line_parts([sixteen, four])
+        w_attention = [after(w_attention[0], eight), w_attention[1]]
     else:
         w_attention, w_lift, w_drop = [
-            gather_all(piece) for piece in (attention_shard, w_up, down_shard)
+            [gather_all(piece)] for piece in (attention_shard, w_up, down_shard)
         ]
 
-    edge = shard // halves
-    biases, bias_up, vectors = unpack(w_attention, shard, each)
-
-    sq, sk, v, slope_q, slope_k, states, total = project(
-        inputs, w_attention, biases, cosines, sines, block
+
+    columns = 4 * part + LANES
+    sq, sk, v, slope_q, slope_k, states, total, w_attention = project(
+        coords, inputs, w_attention, columns, edges, cosines, sines, block, shard, halves
     )
+    bias_up, vectors = unpack(w_attention, turns, shard, each)
     queries, there = sq, []
     if pieces:
-        four = up_chunk.held
-        up_chunk.beside([sixteen], [sq])
-        down_chunk.line([sixteen, four], [sq])
+        up_chunk.across([], [sq])
+        down_chunk.held = join(
+            [down_chunk.held[0]] + [after(part, sq) for part in down_chunk.held[1]]
+        )
         there = [up_chunk.held, down_chunk.held]
         queries = after(sq, *there)
     num, den = attend(queries, sk, v, cm, cosines, sines, states)
     towards = [(i, i + 1) for i in range(halves - 1)]
     incoming = send(total, towards, there, [num], "tp")
     if pieces:
-        up_chunk.across(there, [num])
+        w_lift = up_chunk.core(there, [num])
         down_chunk.beside(there, [num])
-        there = [up_chunk.held, down_chunk.held, incoming]
+        there = [down_chunk.held, incoming, w_lift[1]]
         num = after(num, *there)
     mixed, rden, normal, scale, low = mix(
-        num, den, sq, incoming, cosines, sines, w_attention, inputs, vectors, 256
+        num, den, sq, incoming, cosines, sines, w_attention, inputs, vectors, 512
     )
     if pieces:
-        sixteen = up_chunk.held
-        w_lift = up_chunk.core(coords, [], [low])
-    act, slope, now = [], [], low
+        down_chunk.across(there, [low])
+        there = [down_chunk.held]
+        low = after(low, *there)
+    act, slope, w_up_halves, now = [], [], [], low
     for half in range(halves):
-        act_half, slope_half = lift(now, w_lift, bias_up, half, units, 512)
+        act_half, slope_half, w_half = lift(
+            coords, now, w_lift, bias_up, half, units, 768, 3 if pieces else 0
+        )
+        w_up_halves.append(w_half)
         act.append(act_half)
         slope.append(slope_half)
-        if pieces and half == 0:
-            down_chunk.across(there, [act_half])
-            now = after(low, down_chunk.held)
     if pieces:
-        w_drop = down_chunk.core(coords, [], [act[1]])
-    output, branch, second, sums_second = drop(
-        act, w_drop, normal, vectors, grad_output, units, 256
+        w_drop = down_chunk.core(there, [act[1]])
+    output, branch, second, sums_second, w_drop = drop(
+        coords, act, w_drop, normal, vectors, grad_output, units, 256
     )
 
-    gdown = wide_gradient(coords, branch, act, layout(units), units, 256, "down_gradient")
+    gdown = wide_gradient(coords, branch, act, layout(units), units, 512, "down_gradient")
     there = gdown
     if pieces:
         down_sum = Sum(*gdown)
     gl, gbias_up = [], []
     for half in range(halves):
         now = after(slope[half], *there)
-        gl_half, gbias_half = bend(branch, w_drop, now, half, units, 512)
+        gl_half, gbias_half = bend(branch, w_drop, now, half, units, 768)
         gl.append(gl_half)
         gbias_up.append(gbias_half)
         if pieces and half == 0:
             down_sum.core([], [gl_half])
             there = down_sum.both()
     wide = units + part + LANES
-    gup = wide_gradient(coords, low, gl, layout(wide), units, 256, "up_gradient")
+    gup = wide_gradient(coords, low, gl, layout(wide), units, 512, "up_gradient")
     there = gup
     if pieces:
         down_sum.across([], gup)
         there = [*gup, *down_sum.both()]
     second = after(second, *there)
-    first, first_low, sums_first = lower(gl, w_lift, second, normal, scale, vectors, units, 256)
+    first, first_low, sums_first = lower(gl, w_up_halves, second, normal, scale, vectors, units, 256)
     if pieces:
         down_sum.beside([], [first])
         first_low = after(first_low, *down_sum.parts)
     *gup, gn, gd, later, later_total = unmix(
         coords, first_low, mixed, rden, sq, cosines, sines, w_attention,
-        sums_first, sums_second, gbias_up, gup, layout(wide), block,
+        sums_first, sums_second, turns, gbias_up, gup, layout(wide), block,
     )
     there = []
     if pieces:
@@ -1222,17 +1360,19 @@
             up_sum.core(there, partial)
             partial = after(tuple(partial), later_in, *up_sum.both())
     query_low, dk, dv = partial
-    *gqkv, key_low, value_low = finish(
-        coords, inputs, query_low, dk, dv, sk, v, slope_k, cosines, sines, later_in,
-        layout(3 * part + LANES),
+    key_low, value_low = tail(dk, dv, sk, v, slope_k, cosines, sines, later_in)
+    if pieces:
+        up_sum.across([], [key_low])
+        query_low = after(query_low, *up_sum.both())
+    gqkv = weight_gradients(
+        coords, inputs, query_low, key_low, value_low, edges, layout(3 * part + LANES)
     )
     if pieces:
-        up_sum.across([], [key_low])
         rest_sum = Sum(*gqkv)
-        rest_sum.core(up_sum.both())
-        up_sum.beside()
-        gup = up_sum.line()
+        up_sum.beside([], gqkv)
+        rest_sum.core(up_sum.parts)
         rest_sum.across()
+        gup = up_sum.line([], rest_sum.both())
         rest_sum.beside()
         rest = rest_sum.line()
     else:

time: 391 us -> 340 us (0.87)
  Pallas kernels: 221 us -> 191 us
  waiting for transfers between devices: 83.7 us -> 71.1 us
  starting transfers between devices: 52.2 us -> 44.4 us
    pallas_call x11 -> x9, Pallas kernels: 99.9 us -> 83.3 us  [the longest x2 18.7 us: lift(): pl.pallas_call(functools.partial(lift_kernel, step=256, row=row, half=hal...]
    ppermute x38, waiting for transfers between devices: 83.7 us -> 71.1 us  [send(): value = lax.ppermute(value, axes, table)]
    pallas_call x2, Pallas kernels: 35.4 us -> 27.4 us  [unattend(): pl.pallas_call(unattend_kernel, grid=(count,), in_specs=[spec, spec, spec...]
    ppermute x38, starting transfers between devices: 52.2 us -> 44.4 us  [send(): value = lax.ppermute(value, axes, table)]
    unnamed x54 -> x48, local copies, waits for them, and re-layouts: 11.8 us -> 6.69 us
  transfers between devices with their start and end apart: 38 -> 38, of which waited for: 16 -> 16; matrix products, arithmetic and copies ran while one was open for 2% -> 2% of each run, Pallas kernels for 48% -> 49%
where the time goes in v3:
time: 340 us; the launch traced here: 334 us
  Pallas kernels  191 us (56%)
  waiting for transfers between devices  71.1 us (21%)
  starting transfers between devices  44.4 us (13%)
  local copies, waits for them, and re-layouts  14.2 us (4%)
  other arithmetic  11.2 us (3%)
    ppermute x38, waiting for transfers between devices, send(): value = lax.ppermute(value, axes, table)  71.1 us
    ppermute x38, starting transfers between devices, send(): value = lax.ppermute(value, axes, table)  44.4 us
    pallas_call x2, Pallas kernels, unattend(): pl.pallas_call(unattend_kernel, grid=(count,), in_specs=[spec, spec, spec...  27.4 us
    pallas_call x2, Pallas kernels, lift(): pl.pallas_call(functools.partial(lift_kernel, step=256, row=row, half=hal...  18.7 us
    pallas_call x2, Pallas kernels, wide_gradient(): pl.pallas_call(functools.partial(wide_gradient_kernel, halves=halves), gr...  18.3 us
    pallas_call x1, Pallas kernels, project(): pl.pallas_call(kernel, grid=(halves,), in_specs=[scalars()] + anywhere(le...  14.7 us
    pallas_call x1, Pallas kernels, drop(): pl.pallas_call(functools.partial(drop_kernel, halves=halves), grid=(rows...  14.4 us
    pallas_call x2, Pallas kernels, bend(): pl.pallas_call(functools.partial(bend_kernel, step=256), grid=(tiles,), i...  13.3 us
  transfers between devices with their start and end apart: 38, of which 16 were waited for; matrix products, arithmetic and copies ran while one was open for 2% of the time, Pallas kernels for 49%

profile of v3, /device:TPU:0, one launch (start us, length us, event | category | flops | bytes accessed | tf_op | source)
XLA Modules:
  0.0 333.7 jit_solution(15614412583764127200)
XLA Ops:
  0.7 1.8 pack.1.refs_0_
  2.4 5.0 %collective-permute-start.2 = (bf16[48,1664]{1,0:T(8,128)(2,1)}, bf16[48,1664]{1,0:T(8,128)(2,1)S(1)}, u32[]{:S(2)}, u32[]{:S(2)}) collective-permute-start(bf16[48,1664]{1,0:T(8,128)(2,1)} %pack.1.refs_0_), channel_id=1, source_target_pairs={{0,24},{1,25},{2,26},{3,27},{4,28},{5,29},{6,30},{7,31},{8,16},{9,... | collective-permute-start | bytes 479240 | tf_op jit(solution)/shard_map/ppermute | solution.py:1134
  9.0 3.7 %collective-permute-done.2.refs_3_ = bf16[48,1664]{1,0:T(8,128)(2,1)S(1)} collective-permute-done((bf16[48,1664]{1,0:T(8,128)(2,1)}, bf16[48,1664]{1,0:T(8,128)(2,1)S(1)}, u32[]{:S(2)}, u32[]{:S(2)}) %collective-permute-start.2) | collective-permute-done | bytes 159776 | tf_op jit(solution)/shard_map/ppermute | solution.py:1134
  12.7 8.5 %collective-permute-done.1.refs_2_ = bf16[48,1664]{1,0:T(8,128)(2,1)S(1)} collective-permute-done((bf16[48,1664]{1,0:T(8,128)(2,1)}, bf16[48,1664]{1,0:T(8,128)(2,1)S(1)}, u32[]{:S(2)}, u32[]{:S(2)}) %collective-permute-start.1) | collective-permute-done | bytes 159776 | tf_op jit(solution)/shard_map/ppermute | solution.py:1134
  22.6 2.0 join.3
  27.0 1.7 add_select_fusion.cm_ref
  28.7 6.5 %collective-permute-done.3 = bf16[4,48,1664]{2,1,0:T(8,128)(2,1)S(1)} collective-permute-done((bf16[4,48,1664]{2,1,0:T(8,128)(2,1)}, bf16[4,48,1664]{2,1,0:T(8,128)(2,1)S(1)}, u32[]{:S(2)}, u32[]{:S(2)}) %collective-permute-start.3) | collective-permute-done | bytes 639008 | tf_op jit(solution)/shard_map/ppermute | solution.py:1134
  38.9 2.5 collective-permute-start.7
  41.4 1.9 collective-permute-start.5
  43.3 4.2 %collective-permute-done.7.refs_3_ = bf16[48,1536]{1,0:T(8,128)(2,1)S(1)} collective-permute-done((bf16[48,1536]{1,0:T(8,128)(2,1)S(1)}, bf16[48,1536]{1,0:T(8,128)(2,1)S(1)}, u32[]{:S(2)}, u32[]{:S(2)}) %collective-permute-start.7) | collective-permute-done | bytes 147488 | tf_op jit(solution)/shard_map/ppermute | solution.py:1134
  47.5 4.9 %collective-permute-done.6.refs_2_ = bf16[48,1536]{1,0:T(8,128)(2,1)S(1)} collective-permute-done((bf16[48,1536]{1,0:T(8,128)(2,1)S(1)}, bf16[48,1536]{1,0:T(8,128)(2,1)S(1)}, u32[]{:S(2)}, u32[]{:S(2)}) %collective-permute-start.6) | collective-permute-done | bytes 147488 | tf_op jit(solution)/shard_map/ppermute | solution.py:1134
  53.7 2.0 join.4
  57.2 9.4 %collective-permute-done.9 = bf16[4,48,1536]{2,1,0:T(8,128)(2,1)S(1)} collective-permute-done((bf16[4,48,1536]{2,1,0:T(8,128)(2,1)S(1)}, bf16[4,48,1536]{2,1,0:T(8,128)(2,1)S(1)}, u32[]{:S(2)}, u32[]{:S(2)}) %collective-permute-start.9) | collective-permute-done | bytes 589856 | tf_op jit(solution)/shard_map/ppermute | solution.py:1134
  69.2 2.9 collective-permute-start.8
  72.6 14.7 %project.1 = (bf16[1024,768]{1,0:T(8,128)(2,1)}, bf16[1024,768]{1,0:T(8,128)(2,1)}, bf16[1024,768]{1,0:T(8,128)(2,1)}, bf16[1024,768]{1,0:T(8,128)(2,1)}, bf16[1...) custom-call(s32[4]{0:T(128)} %pad_add_fusion.coords_ref, ...), custom_call_target="tpu_custom_call" | custom-call | flops 3623878656 | bytes 16000000 | tf_op jit(solution)/shard_map/project/pallas_call | solution.py:383
  88.7 2.0 join.5
  91.7 3.2 collective-permute-start.15
  95.0 12.4 %attend.1 = (f32[1024,768]{1,0:T(8,128)}, f32[1024,768]{1,0:T(8,128)}) custom-call(bf16[1024,768]{1,0:T(8,128)(2,1)} %get-tuple-element.135.sq_ref, bf16[1024,768]{1,0:T(8,128)(2,1)} %get-tuple-element.136.sk_ref, bf16[1024,768]{1,0:T(8,128)(2,1)} %get-tuple-element.137.v_ref, f32[2,512,512]{2,1,0:T(8,128)} %add_select_fusion.cm_ref, ...), custom_call_target="tpu_custom_call" | custom-call | flops 8000000000 | bytes 14000000 | tf_op jit(solution)/shard_map/attend/pallas_call | solution.py:443
  107.5 3.4 %collective-permute-done.14 = bf16[4,48,1536]{2,1,0:T(8,128)(2,1)S(1)} collective-permute-done((bf16[4,48,1536]{2,1,0:T(8,128)(2,1)S(1)}, bf16[4,48,1536]{2,1,0:T(8,128)(2,1)S(1)}, u32[]{:S(2)}, u32[]{:S(2)}) %collective-permute-start.14) | collective-permute-done | bytes 589856 | tf_op jit(solution)/shard_map/ppermute | solution.py:1134
  111.7 2.0 unpack.1
  113.7 9.2 %mix.1 = (bf16[1024,768]{1,0:T(8,128)(2,1)}, f32[1024,768]{1,0:T(8,128)}, f32[1024,768]{1,0:T(8,128)}, f32[1024,128]{1,0:T(8,128)}, bf16[1024,768]{1,0:T(8,128)(2,1)}) custom-call(f32[1024,768]{1,0:T(8,128)} %get-tuple-element.147.num_ref, f32[1024,768]{1,0:T(8,128)} %get-tuple-element.148.den_ref, bf16[1024,768]{1,0:T(8,128)(2,1)} %get-tuple-element.135.sq_ref, ...), custom_call_target="tpu_custom_call" | custom-call | flops 2415919104 | bytes 20000000 | tf_op jit(solution)/shard_map/mix/pallas_call | solution.py:504
  122.9 4.3 %collective-permute-done.17 = bf16[8,48,1536]{2,1,0:T(8,128)(2,1)S(1)} collective-permute-done((bf16[8,48,1536]{2,1,0:T(8,128)(2,1)S(1)}, bf16[8,48,1536]{2,1,0:T(8,128)(2,1)S(1)}, u32[]{:S(2)}, u32[]{:S(2)}) %collective-permute-start.17) | collective-permute-done | bytes 1179680 | tf_op jit(solution)/shard_map/ppermute | solution.py:1134
  127.6 9.7 %lift.3 = (bf16[1024,1536]{1,0:T(8,128)(2,1)}, bf16[1024,1536]{1,0:T(8,128)(2,1)}, bf16[1,1,768,1536]{3,2,1,0:T(8,128)(2,1)}) custom-call(s32[4]{0:T(128)} %pad_add_fusion.coords_ref, bf16[16,48,1536]{2,1,0:T(8,128)(2,1)} %copy-done.6, bf16[16,48,1536]{2,1,0:T(8,128)(2,1)} %collective-permute-done.16.refs_1_, ...), custom_call_target="tpu_custom_call" | custom-call | flops 2415919104 | bytes 10000000 | tf_op jit(solution)/shard_map/lift/pallas_call | solution.py:571
  137.3 9.0 %lift.2 = (bf16[1024,1536]{1,0:T(8,128)(2,1)}, bf16[1024,1536]{1,0:T(8,128)(2,1)}, bf16[1,1,768,1536]{3,2,1,0:T(8,128)(2,1)}) custom-call(s32[4]{0:T(128)} %pad_add_fusion.coords_ref, bf16[16,48,1536]{2,1,0:T(8,128)(2,1)} %copy-done.6, bf16[16,48,1536]{2,1,0:T(8,128)(2,1)} %collective-permute-done.16.refs_1_, ...), custom_call_target="tpu_custom_call" | custom-call | flops 2415919104 | bytes 10000000 | tf_op jit(solution)/shard_map/lift/pallas_call | solution.py:571
  147.7 14.4 %drop.1 = (bf16[1024,768]{1,0:T(8,128)(2,1)}, bf16[1024,768]{1,0:T(8,128)(2,1)}, f32[1024,768]{1,0:T(8,128)}, f32[8,768]{1,0:T(8,128)}, bf16[1,2,768,1536]{3,2,1,0:T(8,128)(2,1)}) custom-call(s32[4]{0:T(128)} %pad_add_fusion.coords_ref, bf16[16,48,1536]{2,1,0:T(8,128)(2,1)} %copy-done.7, bf16[16,48,1536]{2,1,0:T(8,128)(2,1)} %copy-done.22, ...), custom_call_target="tpu_custom_call" | custom-call | flops 4831838208 | bytes 20000000 | tf_op jit(solution)/shard_map/drop/pallas_call | solution.py:624
  162.1 9.1 %down_gradient.1 = (bf16[16,48,1536]{2,1,0:T(8,128)(2,1)}, bf16[16,48,1536]{2,1,0:T(8,128)(2,1)}) custom-call(s32[4]{0:T(128)} %pad_add_fusion.coords_ref, bf16[1024,768]{1,0:T(8,128)(2,1)} %get-tuple-element.161.left_ref.branch_ref, bf16[1024,1536]{1,0:T(8,128)(2,1)} %get-tuple-element.158.refs_2_.refs_0_, bf16[1024,1536]{1,0:T(8,128)(2,1)} %get-tuple-element.156.refs_3_.refs_1_), custom_call_target="tpu_custom_call" | custom-call | flops 4831838208 | bytes 18000000 | tf_op jit(solution)/shard_map/down_gradient/pallas_call | solution.py:671
  171.2 6.6 %bend.2 = (bf16[1024,1536]{1,0:T(8,128)(2,1)}, f32[8,1536]{1,0:T(8,128)}) custom-call(bf16[1024,768]{1,0:T(8,128)(2,1)} %get-tuple-element.161.left_ref.branch_ref, bf16[1,2,768,1536]{3,2,1,0:T(8,128)(2,1)} %get-tuple-element.162.down_ref, bf16[1024,1536]{1,0:T(8,128)(2,1)} %get-tuple-element.166.slope_ref), custom_call_target="tpu_custom_call" | custom-call | flops 2415919104 | bytes 10000000 | tf_op jit(solution)/shard_map/bend/pallas_call | solution.py:705
  178.6 6.7 %bend.3 = (bf16[1024,1536]{1,0:T(8,128)(2,1)}, f32[8,1536]{1,0:T(8,128)}) custom-call(bf16[1024,768]{1,0:T(8,128)(2,1)} %get-tuple-element.161.left_ref.branch_ref, bf16[1,2,768,1536]{3,2,1,0:T(8,128)(2,1)} %get-tuple-element.162.down_ref, bf16[1024,1536]{1,0:T(8,128)(2,1)} %get-tuple-element.170.slope_ref), custom_call_target="tpu_custom_call" | custom-call | flops 2415919104 | bytes 10000000 | tf_op jit(solution)/shard_map/bend/pallas_call | solution.py:705
  185.3 9.1 %up_gradient.1 = (bf16[16,48,2048]{2,1,0:T(8,128)(2,1)}, bf16[16,48,2048]{2,1,0:T(8,128)(2,1)}) custom-call(s32[4]{0:T(128)} %pad_add_fusion.coords_ref, bf16[1024,768]{1,0:T(8,128)(2,1)} %get-tuple-element.154.refs_2_.left_ref, bf16[1024,1536]{1,0:T(8,128)(2,1)} %get-tuple-element.167.refs_0_, bf16[1024,1536]{1,0:T(8,128)(2,1)} %get-tuple-element.171.refs_1_), custom_call_target="tpu_custom_call" | custom-call | flops 4831838208 | bytes 18000000 | tf_op jit(solution)/shard_map/up_gradient/pallas_call | solution.py:671
  195.1 2.5 collective-permute-start.21
  197.6 12.4 %lower.1 = (f32[1024,768]{1,0:T(8,128)}, bf16[1024,768]{1,0:T(8,128)(2,1)}, f32[8,768]{1,0:T(8,128)}) custom-call(bf16[1024,1536]{1,0:T(8,128)(2,1)} %get-tuple-element.167.refs_0_, bf16[1024,1536]{1,0:T(8,128)(2,1)} %get-tuple-element.171.refs_1_, bf16[1,1,768,1536]{3,2,1,0:T(8,128)(2,1)} %get-tuple-element.172.refs_2_, ...), custom_call_target="tpu_custom_call" | custom-call | flops 4831838208 | bytes 20000000 | tf_op jit(solution)/shard_map/lower/pallas_call | solution.py:749
  210.2 2.0 collective-permute-start.24
  212.2 2.5 collective-permute-start.22
  214.7 11.5 %unmix.1 = (bf16[16,48,2048]{2,1,0:T(8,128)(2,1)}, bf16[16,48,2048]{2,1,0:T(8,128)(2,1)}, bf16[1024,768]{1,0:T(8,128)(2,1)}, bf16[1024,768]{1,0:T(8,128)(2,1)}, ...) custom-call(s32[4]{0:T(128)} %pad_add_fusion.coords_ref, ...), custom_call_target="tpu_custom_call", output_to_operand_aliasing={{0}: (13, {}), {1}: (14, {})} | custom-call | flops 2415919104 | bytes 16000000 | tf_op jit(solution)/shard_map/unmix/pallas_call | solution.py:872
  228.4 14.0 %unattend.2 = (bf16[1024,768]{1,0:T(8,128)(2,1)}, f32[1024,768]{1,0:T(8,128)}, f32[1024,768]{1,0:T(8,128)}) custom-call(bf16[1024,768]{1,0:T(8,128)(2,1)} %get-tuple-element.135.sq_ref, bf16[1024,768]{1,0:T(8,128)(2,1)} %get-tuple-element.136.sk_ref, bf16[1024,768]{1,0:T(8,128)(2,1)} %get-tuple-element.137.v_ref, ...), custom_call_target="tpu_custom_call" | custom-call | flops 20000000000 | bytes 20000000 | tf_op jit(solution)/shard_map/unattend/pallas_call | solution.py:982
  242.4 2.7 add_convert_fusion
  246.8 13.4 %unattend.3 = (bf16[1024,768]{1,0:T(8,128)(2,1)}, f32[1024,768]{1,0:T(8,128)}, f32[1024,768]{1,0:T(8,128)}) custom-call(bf16[1024,768]{1,0:T(8,128)(2,1)} %get-tuple-element.135.sq_ref, bf16[1024,768]{1,0:T(8,128)(2,1)} %get-tuple-element.136.sk_ref, ...), custom_call_target="tpu_custom_call", output_to_operand_aliasing={{0}: (12, {}), {1}: (13, {}), {2}: (14, {})} | custom-call | flops 20000000000 | bytes 20000000 | tf_op jit(solution)/shard_map/unattend/pallas_call | solution.py:982
  260.2 9.0 %tail.1 = (bf16[1024,768]{1,0:T(8,128)(2,1)}, bf16[1024,768]{1,0:T(8,128)(2,1)}) custom-call(f32[1024,768]{1,0:T(8,128)} %get-tuple-element.212.dk_ref, f32[1024,768]{1,0:T(8,128)} %get-tuple-element.213.dv_ref, bf16[1024,768]{1,0:T(8,128)(2,1)} %get-tuple-element.136.sk_ref, bf16[1024,768]{1,0:T(8,128)(2,1)} %get-tuple-element.137.v_ref, ...), custom_call_target="tpu_custom_call" | custom-call | flops 2000000000 | bytes 14000000 | tf_op jit(solution)/shard_map/tail/pallas_call | solution.py:1022
  269.9 2.7 collective-permute-start.28
  272.7 11.2 %weight_gradients.1 = (bf16[16,48,1280]{2,1,0:T(8,128)(2,1)}, bf16[16,48,1280]{2,1,0:T(8,128)(2,1)}) custom-call(s32[4]{0:T(128)} %pad_add_fusion.coords_ref, bf16[1024,768]{1,0:T(8,128)(2,1)} %x_ref.3, bf16[1024,768]{1,0:T(8,128)(2,1)} %get-tuple-element.217.q_ref, bf16[1024,768]{1,0:T(8,128)(2,1)} %get-tuple-element.215.k_ref, ...), custom_call_target="tpu_custom_call" | custom-call | flops 3623878656 | bytes 10000000 | tf_op jit(solution)/shard_map/weight_gradients/pallas_call | solution.py:1066
  284.3 4.2 %collective-permute-done.29 = bf16[16,48,1280]{2,1,0:T(8,128)(2,1)S(1)} collective-permute-done((bf16[16,48,1280]{2,1,0:T(8,128)(2,1)}, bf16[16,48,1280]{2,1,0:T(8,128)(2,1)S(1)}, u32[]{:S(2)}, u32[]{:S(2)}) %collective-permute-start.29) | collective-permute-done | bytes 1966112 | tf_op jit(solution)/shard_map/ppermute | solution.py:1134
  289.4 8.8 %input_gradient.1 = bf16[1024,768]{1,0:T(8,128)(2,1)} custom-call(f32[1024,768]{1,0:T(8,128)} %get-tuple-element.180.first_ref, bf16[1024,768]{1,0:T(8,128)(2,1)} %get-tuple-element.217.q_ref, bf16[1024,768]{1,0:T(8,128)(2,1)} %get-tuple-element.215.k_ref, bf16[1024,768]{1,0:T(8,128)(2,1)} %get-tuple-element.218.v_ref, ...), custom_call_target="tpu_custom_call" | custom-call | flops 3623878656 | bytes 14000000 | tf_op jit(solution)/shard_map/input_gradient/pallas_call | solution.py:1097
  298.2 1.9 collective-permute-start.37
  300.1 2.5 collective-permute-start.35
  304.1 3.7 %collective-permute-done.37 = bf16[48,2048]{1,0:T(8,128)(2,1)S(1)} collective-permute-done((bf16[48,2048]{1,0:T(8,128)(2,1)S(1)}, bf16[48,2048]{1,0:T(8,128)(2,1)S(1)}, u32[]{:S(2)}, u32[]{:S(2)}) %collective-permute-start.37) | collective-permute-done | bytes 196640 | tf_op jit(solution)/shard_map/ppermute | solution.py:1134
  307.9 9.5 %collective-permute-done.36 = bf16[48,2048]{1,0:T(8,128)(2,1)S(1)} collective-permute-done((bf16[48,2048]{1,0:T(8,128)(2,1)S(1)}, bf16[48,2048]{1,0:T(8,128)(2,1)S(1)}, u32[]{:S(2)}, u32[]{:S(2)}) %collective-permute-start.36) | collective-permute-done | bytes 196640 | tf_op jit(solution)/shard_map/ppermute | solution.py:1134
  319.8 2.0 collective-permute-start.33
  326.4 5.5 %collective-permute-done.33 = bf16[48,1280]{1,0:T(8,128)(2,1)S(1)} collective-permute-done((bf16[48,1280]{1,0:T(8,128)(2,1)S(1)}, bf16[48,1280]{1,0:T(8,128)(2,1)S(1)}, u32[]{:S(2)}, u32[]{:S(2)}) %collective-permute-start.33) | collective-permute-done | bytes 122912 | tf_op jit(solution)/shard_map/ppermute | solution.py:1134
  (139 shorter events, 37.2 us)
Async XLA Ops:
  2.4 10.3 %collective-permute-start.2 = (bf16[48,1664]{1,0:T(8,128)(2,1)}, bf16[48,1664]{1,0:T(8,128)(2,1)S(1)}, u32[]{:S(2)}, u32[]{:S(2)}) collective-permute-start(bf16[48,1664]{1,0:T(8,128)(2,1)} %pack.1.refs_0_), channel_id=1, source_target_pairs={{0,24},{1,25},{2,26},{3,27},{4,28},{5,29},{6,30},{7,31},{8,16},{9,... | collective-permute-start | bytes 479240 | tf_op jit(solution)/shard_map/ppermute | solution.py:1134
  7.5 13.7 %collective-permute-start.1 = (bf16[48,1664]{1,0:T(8,128)(2,1)}, bf16[48,1664]{1,0:T(8,128)(2,1)S(1)}, u32[]{:S(2)}, u32[]{:S(2)}) collective-permute-start(bf16[48,1664]{1,0:T(8,128)(2,1)} %pack.1.refs_0_), channel_id=1, source_target_pairs={{0,16},{1,17},{2,18},{3,19},{4,20},{5,21},{6,22},{7,23},{8,24},{9,... | collective-permute-start | bytes 479240 | tf_op jit(solution)/shard_map/ppermute | solution.py:1134
  7.5 13.7 %collective-permute-start = (bf16[48,1664]{1,0:T(8,128)(2,1)}, bf16[48,1664]{1,0:T(8,128)(2,1)S(1)}, u32[]{:S(2)}, u32[]{:S(2)}) collective-permute-start(bf16[48,1664]{1,0:T(8,128)(2,1)} %pack.1.refs_0_), channel_id=1, source_target_pairs={{0,8},{1,9},{2,10},{3,11},{4,12},{5,13},{6,14},{7,15},{8,0},{9,1},... | collective-permute-start | bytes 479240 | tf_op jit(solution)/shard_map/ppermute | solution.py:1134
  12.7 8.5 %copy-start.11 = (bf16[48,1664]{1,0:T(8,128)(2,1)}, bf16[48,1664]{1,0:T(8,128)(2,1)S(1)}, u32[]{:S(2)}) copy-start(bf16[48,1664]{1,0:T(8,128)(2,1)S(1)} %collective-permute-done.2.refs_3_) | copy-start | bytes 479236
  24.6 10.6 %copy-start.1 = (bf16[4,48,1664]{2,1,0:T(8,128)(2,1)S(1)}, bf16[4,48,1664]{2,1,0:T(8,128)(2,1)}, u32[]{:S(2)}) copy-start(bf16[4,48,1664]{2,1,0:T(8,128)(2,1)} %join.3) | copy-start | bytes 1916932
  24.6 10.6 %collective-permute-start.3 = (bf16[4,48,1664]{2,1,0:T(8,128)(2,1)}, bf16[4,48,1664]{2,1,0:T(8,128)(2,1)S(1)}, u32[]{:S(2)}, u32[]{:S(2)}) collective-permute-start(bf16[4,48,1664]{2,1,0:T(8,128)(2,1)} %join.3), channel_id=1, source_target_pairs={{0,1},{1,0},{2,6},{3,7},{4,5},{5,4},{6,2},{7,3},{8,9},{9,8},{10,14... | collective-permute-start | bytes 1916936 | tf_op jit(solution)/shard_map/ppermute | solution.py:1134
  28.7 10.2 %copy-start.14 = (bf16[48,1536]{1,0:T(8,128)(2,1)S(1)}, bf16[48,1536]{1,0:T(8,128)(2,1)}, u32[]{:S(2)}) copy-start(bf16[48,1536]{1,0:T(8,128)(2,1)} %refs_0_.3) | copy-start | bytes 442372
  37.4 18.3 %collective-permute-start.4 = (bf16[8,48,1664]{2,1,0:T(8,128)(2,1)S(1)}, bf16[8,48,1664]{2,1,0:T(8,128)(2,1)S(1)}, u32[]{:S(2)}, u32[]{:S(2)}) collective-permute-start(bf16[8,48,1664]{2,1,0:T(8,128)(2,1)S(1)} %pad_maximum_fusion.3), channel_id=1, source_target_pairs={{0,4},{1,5},{2,3},{3,2},{4,0},{5,1},{6,7},{7,6},{8,12},{9,13},{10,... | collective-permute-start | bytes 3833864 | tf_op jit(solution)/shard_map/ppermute | solution.py:1134
  38.9 8.6 %collective-permute-start.7 = (bf16[48,1536]{1,0:T(8,128)(2,1)S(1)}, bf16[48,1536]{1,0:T(8,128)(2,1)S(1)}, u32[]{:S(2)}, u32[]{:S(2)}) collective-permute-start(bf16[48,1536]{1,0:T(8,128)(2,1)S(1)} %copy-done.14), channel_id=1, source_target_pairs={{0,24},{1,25},{2,26},{3,27},{4,28},{5,29},{6,30},{7,31},{8,16},{9,... | collective-permute-start | bytes 442376 | tf_op jit(solution)/shard_map/ppermute | solution.py:1134
  41.4 11.0 %collective-permute-start.6 = (bf16[48,1536]{1,0:T(8,128)(2,1)S(1)}, bf16[48,1536]{1,0:T(8,128)(2,1)S(1)}, u32[]{:S(2)}, u32[]{:S(2)}) collective-permute-start(bf16[48,1536]{1,0:T(8,128)(2,1)S(1)} %copy-done.14), channel_id=1, source_target_pairs={{0,16},{1,17},{2,18},{3,19},{4,20},{5,21},{6,22},{7,23},{8,24},{9,... | collective-permute-start | bytes 442376 | tf_op jit(solution)/shard_map/ppermute | solution.py:1134
  41.4 11.0 %collective-permute-start.5 = (bf16[48,1536]{1,0:T(8,128)(2,1)S(1)}, bf16[48,1536]{1,0:T(8,128)(2,1)S(1)}, u32[]{:S(2)}, u32[]{:S(2)}) collective-permute-start(bf16[48,1536]{1,0:T(8,128)(2,1)S(1)} %copy-done.14), channel_id=1, source_target_pairs={{0,8},{1,9},{2,10},{3,11},{4,12},{5,13},{6,14},{7,15},{8,0},{9,1},... | collective-permute-start | bytes 442376 | tf_op jit(solution)/shard_map/ppermute | solution.py:1134
  56.0 16.7 %copy-start.4 = (bf16[16,48,1664]{2,1,0:T(8,128)(2,1)}, bf16[16,48,1664]{2,1,0:T(8,128)(2,1)S(1)}, u32[]{:S(2)}) copy-start(bf16[16,48,1664]{2,1,0:T(8,128)(2,1)S(1)} %pad_maximum_fusion.refs_0_) | copy-start | bytes 7667716
  56.0 11.7 %copy-start.15 = (bf16[1536,48]{0,1:T(8,128)(2,1)S(1)}, bf16[1536,48]{0,1:T(8,128)(2,1)}, u32[]{:S(2)}) copy-start(bf16[1536,48]{0,1:T(8,128)(2,1)} %param.32) | copy-start | bytes 442372
  56.0 10.6 %collective-permute-start.10 = (bf16[16,48,1664]{2,1,0:T(8,128)(2,1)S(1)}, bf16[16,48,1664]{2,1,0:T(8,128)(2,1)}, u32[]{:S(2)}, u32[]{:S(2)}) collective-permute-start(bf16[16,48,1664]{2,1,0:T(8,128)(2,1)S(1)} %pad_maximum_fusion.refs_0_), channel_id=1, source_target_pairs={{0,2},{1,3},{2,0},{3,1},{4,6},{5,7},{6,4},{7,5},{8,10},{9,11},{10,... | collective-permute-start | bytes 7667720 | tf_op jit(solution)/shard_map/ppermute | solution.py:1134
  56.7 9.9 %collective-permute-start.9 = (bf16[4,48,1536]{2,1,0:T(8,128)(2,1)S(1)}, bf16[4,48,1536]{2,1,0:T(8,128)(2,1)S(1)}, u32[]{:S(2)}, u32[]{:S(2)}) collective-permute-start(bf16[4,48,1536]{2,1,0:T(8,128)(2,1)S(1)} %copy-done.2), channel_id=1, source_target_pairs={{0,1},{1,0},{2,6},{3,7},{4,5},{5,4},{6,2},{7,3},{8,9},{9,8},{10,14... | collective-permute-start | bytes 1769480 | tf_op jit(solution)/shard_map/ppermute | solution.py:1134
  66.7 24.0 %collective-permute-start.13 = (bf16[8,48,1536]{2,1,0:T(8,128)(2,1)S(1)}, bf16[8,48,1536]{2,1,0:T(8,128)(2,1)S(1)}, u32[]{:S(2)}, u32[]{:S(2)}) collective-permute-start(bf16[8,48,1536]{2,1,0:T(8,128)(2,1)S(1)} %pad_maximum_fusion.4), channel_id=1, source_target_pairs={{0,4},{1,5},{2,3},{3,2},{4,0},{5,1},{6,7},{7,6},{8,12},{9,13},{10,... | collective-permute-start | bytes 3538952 | tf_op jit(solution)/shard_map/ppermute | solution.py:1134
  67.7 19.7 %collective-permute-start.12 = (bf16[48,1536]{1,0:T(8,128)(2,1)S(1)}, bf16[48,1536]{1,0:T(8,128)(2,1)S(1)}, u32[]{:S(2)}, u32[]{:S(2)}) collective-permute-start(bf16[48,1536]{1,0:T(8,128)(2,1)S(1)} %bitcast.53), channel_id=1, source_target_pairs={{0,24},{1,25},{2,26},{3,27},{4,28},{5,29},{6,30},{7,31},{8,16},{9,... | collective-permute-start | bytes 442376 | tf_op jit(solution)/shard_map/ppermute | solution.py:1134
  69.2 18.2 %collective-permute-start.11 = (bf16[48,1536]{1,0:T(8,128)(2,1)S(1)}, bf16[48,1536]{1,0:T(8,128)(2,1)S(1)}, u32[]{:S(2)}, u32[]{:S(2)}) collective-permute-start(bf16[48,1536]{1,0:T(8,128)(2,1)S(1)} %bitcast.54), channel_id=1, source_target_pairs={{0,16},{1,17},{2,18},{3,19},{4,20},{5,21},{6,22},{7,23},{8,24},{9,... | collective-permute-start | bytes 442376 | tf_op jit(solution)/shard_map/ppermute | solution.py:1134
  69.2 18.2 %collective-permute-start.8 = (bf16[48,1536]{1,0:T(8,128)(2,1)S(1)}, bf16[48,1536]{1,0:T(8,128)(2,1)S(1)}, u32[]{:S(2)}, u32[]{:S(2)}) collective-permute-start(bf16[48,1536]{1,0:T(8,128)(2,1)S(1)} %bitcast.55), channel_id=1, source_target_pairs={{0,8},{1,9},{2,10},{3,11},{4,12},{5,13},{6,14},{7,15},{8,0},{9,1},... | collective-permute-start | bytes 442376 | tf_op jit(solution)/shard_map/ppermute | solution.py:1134
  90.9 16.5 %copy-start.6 = (bf16[16,48,1536]{2,1,0:T(8,128)(2,1)}, bf16[16,48,1536]{2,1,0:T(8,128)(2,1)S(1)}, u32[]{:S(2)}) copy-start(bf16[16,48,1536]{2,1,0:T(8,128)(2,1)S(1)} %pad_maximum_fusion.1.refs_0_) | copy-start | bytes 7077892
  90.9 20.1 %collective-permute-start.16 = (bf16[16,48,1536]{2,1,0:T(8,128)(2,1)S(1)}, bf16[16,48,1536]{2,1,0:T(8,128)(2,1)}, u32[]{:S(2)}, u32[]{:S(2)}) collective-permute-start(bf16[16,48,1536]{2,1,0:T(8,128)(2,1)S(1)} %pad_maximum_fusion.1.refs_0_), channel_id=1, source_target_pairs={{0,2},{1,3},{2,0},{3,1},{4,6},{5,7},{6,4},{7,5},{8,10},{9,11},{10,... | collective-permute-start | bytes 7077896 | tf_op jit(solution)/shard_map/ppermute | solution.py:1134
  91.7 15.8 %collective-permute-start.15 = (bf16[6,256,128]{2,1,0:T(8,128)(2,1)S(1)}, bf16[6,256,128]{2,1,0:T(8,128)(2,1)S(1)}, u32[]{:S(2)}, u32[]{:S(2)}) collective-permute-start(bf16[6,256,128]{2,1,0:T(8,128)(2,1)S(1)} %copy-done.23), channel_id=1, source_target_pairs={{0,1},{2,3},{4,5},{6,7},{8,9},{10,11},{12,13},{14,15},{16,17},{18,... | collective-permute-start | bytes 1179656 | tf_op jit(solution)/shard_map/ppermute | solution.py:1134
  94.9 16.0 %collective-permute-start.14 = (bf16[4,48,1536]{2,1,0:T(8,128)(2,1)S(1)}, bf16[4,48,1536]{2,1,0:T(8,128)(2,1)S(1)}, u32[]{:S(2)}, u32[]{:S(2)}) collective-permute-start(bf16[4,48,1536]{2,1,0:T(8,128)(2,1)S(1)} %copy-done.3), channel_id=1, source_target_pairs={{0,1},{1,0},{2,6},{3,7},{4,5},{5,4},{6,2},{7,3},{8,9},{9,8},{10,14... | collective-permute-start | bytes 1769480 | tf_op jit(solution)/shard_map/ppermute | solution.py:1134
  107.5 6.3 %copy-start.10 = (bf16[6,256,128]{2,1,0:T(8,128)(2,1)}, bf16[6,256,128]{2,1,0:T(8,128)(2,1)S(1)}, u32[]{:S(2)}) copy-start(bf16[6,256,128]{2,1,0:T(8,128)(2,1)S(1)} %collective-permute-done.15.in_ref) | copy-start | bytes 1179652
  111.0 16.3 %collective-permute-start.17 = (bf16[8,48,1536]{2,1,0:T(8,128)(2,1)S(1)}, bf16[8,48,1536]{2,1,0:T(8,128)(2,1)S(1)}, u32[]{:S(2)}, u32[]{:S(2)}) collective-permute-start(bf16[8,48,1536]{2,1,0:T(8,128)(2,1)S(1)} %pad_maximum_fusion.5), channel_id=1, source_target_pairs={{0,4},{1,5},{2,3},{3,2},{4,0},{5,1},{6,7},{7,6},{8,12},{9,13},{10,... | collective-permute-start | bytes 3538952 | tf_op jit(solution)/shard_map/ppermute | solution.py:1134
  127.5 9.8 %copy-start.7 = (bf16[16,48,1536]{2,1,0:T(8,128)(2,1)}, bf16[16,48,1536]{2,1,0:T(8,128)(2,1)S(1)}, u32[]{:S(2)}) copy-start(bf16[16,48,1536]{2,1,0:T(8,128)(2,1)S(1)} %pad_maximum_fusion.2.refs_0_) | copy-start | bytes 7077892
  127.5 18.8 %collective-permute-start.18 = (bf16[16,48,1536]{2,1,0:T(8,128)(2,1)S(1)}, bf16[16,48,1536]{2,1,0:T(8,128)(2,1)S(1)}, u32[]{:S(2)}, u32[]{:S(2)}) collective-permute-start(bf16[16,48,1536]{2,1,0:T(8,128)(2,1)S(1)} %pad_maximum_fusion.2.refs_0_), channel_id=1, source_target_pairs={{0,2},{1,3},{2,0},{3,1},{4,6},{5,7},{6,4},{7,5},{8,10},{9,11},{10,... | collective-permute-start | bytes 7077896 | tf_op jit(solution)/shard_map/ppermute | solution.py:1134
  171.2 6.6 %collective-permute-start.19 = (bf16[16,48,1536]{2,1,0:T(8,128)(2,1)}, bf16[16,48,1536]{2,1,0:T(8,128)(2,1)S(1)}, u32[]{:S(2)}, u32[]{:S(2)}) collective-permute-start(bf16[16,48,1536]{2,1,0:T(8,128)(2,1)} %get-tuple-element.165), channel_id=1, source_target_pairs={{0,2},{1,3},{2,0},{3,1},{4,6},{5,7},{6,4},{7,5},{8,10},{9,11},{10,... | collective-permute-start | bytes 7077896 | tf_op jit(solution)/shard_map/ppermute | solution.py:1134
  171.2 6.6 %copy-start.5 = (bf16[16,48,1536]{2,1,0:T(8,128)(2,1)S(1)}, bf16[16,48,1536]{2,1,0:T(8,128)(2,1)}, u32[]{:S(2)}) copy-start(bf16[16,48,1536]{2,1,0:T(8,128)(2,1)} %get-tuple-element.164) | copy-start | bytes 7077892
  178.5 16.3 %collective-permute-start.20 = (bf16[8,48,1536]{2,1,0:T(8,128)(2,1)S(1)}, bf16[8,48,1536]{2,1,0:T(8,128)(2,1)S(1)}, u32[]{:S(2)}, u32[]{:S(2)}) collective-permute-start(bf16[8,48,1536]{2,1,0:T(8,128)(2,1)S(1)} %get-tuple-element.239), channel_id=1, source_target_pairs={{0,4},{1,5},{2,3},{3,2},{4,0},{5,1},{6,7},{7,6},{8,12},{9,13},{10,... | collective-permute-start | bytes 3538952 | tf_op jit(solution)/shard_map/ppermute | solution.py:1134
  195.1 15.0 %collective-permute-start.21 = (bf16[4,48,1536]{2,1,0:T(8,128)(2,1)S(1)}, bf16[4,48,1536]{2,1,0:T(8,128)(2,1)S(1)}, u32[]{:S(2)}, u32[]{:S(2)}) collective-permute-start(bf16[4,48,1536]{2,1,0:T(8,128)(2,1)S(1)} %get-tuple-element.245), channel_id=1, source_target_pairs={{0,1},{1,0},{2,6},{3,7},{4,5},{5,4},{6,2},{7,3},{8,9},{9,8},{10,14... | collective-permute-start | bytes 1769480 | tf_op jit(solution)/shard_map/ppermute | solution.py:1134
  210.2 16.0 %collective-permute-start.24 = (bf16[48,1536]{1,0:T(8,128)(2,1)S(1)}, bf16[48,1536]{1,0:T(8,128)(2,1)S(1)}, u32[]{:S(2)}, u32[]{:S(2)}) collective-permute-start(bf16[48,1536]{1,0:T(8,128)(2,1)S(1)} %get-tuple-element.253), channel_id=1, source_target_pairs={{0,24},{1,25},{2,26},{3,27},{4,28},{5,29},{6,30},{7,31},{8,16},{9,... | collective-permute-start | bytes 442376 | tf_op jit(solution)/shard_map/ppermute | solution.py:1134
  212.2 14.0 %collective-permute-start.23 = (bf16[48,1536]{1,0:T(8,128)(2,1)S(1)}, bf16[48,1536]{1,0:T(8,128)(2,1)S(1)}, u32[]{:S(2)}, u32[]{:S(2)}) collective-permute-start(bf16[48,1536]{1,0:T(8,128)(2,1)S(1)} %get-tuple-element.254), channel_id=1, source_target_pairs={{0,16},{1,17},{2,18},{3,19},{4,20},{5,21},{6,22},{7,23},{8,24},{9,... | collective-permute-start | bytes 442376 | tf_op jit(solution)/shard_map/ppermute | solution.py:1134
  212.2 14.0 %collective-permute-start.22 = (bf16[48,1536]{1,0:T(8,128)(2,1)S(1)}, bf16[48,1536]{1,0:T(8,128)(2,1)S(1)}, u32[]{:S(2)}, u32[]{:S(2)}) collective-permute-start(bf16[48,1536]{1,0:T(8,128)(2,1)S(1)} %get-tuple-element.255), channel_id=1, source_target_pairs={{0,8},{1,9},{2,10},{3,11},{4,12},{5,13},{6,14},{7,15},{8,0},{9,1},... | collective-permute-start | bytes 442376 | tf_op jit(solution)/shard_map/ppermute | solution.py:1134
  227.1 15.3 %collective-permute-start.26 = (bf16[16,48,2048]{2,1,0:T(8,128)(2,1)}, bf16[16,48,2048]{2,1,0:T(8,128)(2,1)S(1)}, u32[]{:S(2)}, u32[]{:S(2)}) collective-permute-start(bf16[16,48,2048]{2,1,0:T(8,128)(2,1)} %get-tuple-element.206), channel_id=1, source_target_pairs={{0,2},{1,3},{2,0},{3,1},{4,6},{5,7},{6,4},{7,5},{8,10},{9,11},{10,... | collective-permute-start | bytes 9437192 | tf_op jit(solution)/shard_map/ppermute | solution.py:1134
  227.1 15.3 %collective-permute-start.25 = (bf16[6,256,128]{2,1,0:T(8,128)(2,1)}, bf16[6,256,128]{2,1,0:T(8,128)(2,1)S(1)}, u32[]{:S(2)}, u32[]{:S(2)}) collective-permute-start(bf16[6,256,128]{2,1,0:T(8,128)(2,1)} %get-tuple-element.202), channel_id=1, source_target_pairs={{1,0},{3,2},{5,4},{7,6},{9,8},{11,10},{13,12},{15,14},{17,16},{19,... | collective-permute-start | bytes 1179656 | tf_op jit(solution)/shard_map/ppermute | solution.py:1134
  228.3 14.0 %copy-start = (bf16[16,48,2048]{2,1,0:T(8,128)(2,1)S(1)}, bf16[16,48,2048]{2,1,0:T(8,128)(2,1)}, u32[]{:S(2)}) copy-start(bf16[16,48,2048]{2,1,0:T(8,128)(2,1)} %get-tuple-element.204) | copy-start | bytes 9437188
  245.1 24.1 %collective-permute-start.27 = (bf16[8,48,2048]{2,1,0:T(8,128)(2,1)}, bf16[8,48,2048]{2,1,0:T(8,128)(2,1)S(1)}, u32[]{:S(2)}, u32[]{:S(2)}) collective-permute-start(bf16[8,48,2048]{2,1,0:T(8,128)(2,1)} %get-tuple-element.237), channel_id=1, source_target_pairs={{0,4},{1,5},{2,3},{3,2},{4,0},{5,1},{6,7},{7,6},{8,12},{9,13},{10,... | collective-permute-start | bytes 4718600 | tf_op jit(solution)/shard_map/ppermute | solution.py:1134
  269.9 14.0 %collective-permute-start.28 = (bf16[4,48,2048]{2,1,0:T(8,128)(2,1)S(1)}, bf16[4,48,2048]{2,1,0:T(8,128)(2,1)S(1)}, u32[]{:S(2)}, u32[]{:S(2)}) collective-permute-start(bf16[4,48,2048]{2,1,0:T(8,128)(2,1)S(1)} %get-tuple-element.243), channel_id=1, source_target_pairs={{0,1},{1,0},{2,6},{3,7},{4,5},{5,4},{6,2},{7,3},{8,9},{9,8},{10,14... | collective-permute-start | bytes 2359304 | tf_op jit(solution)/shard_map/ppermute | solution.py:1134
  284.2 4.2 %collective-permute-start.29 = (bf16[16,48,1280]{2,1,0:T(8,128)(2,1)}, bf16[16,48,1280]{2,1,0:T(8,128)(2,1)S(1)}, u32[]{:S(2)}, u32[]{:S(2)}) collective-permute-start(bf16[16,48,1280]{2,1,0:T(8,128)(2,1)} %get-tuple-element.222), channel_id=1, source_target_pairs={{0,2},{1,3},{2,0},{3,1},{4,6},{5,7},{6,4},{7,5},{8,10},{9,11},{10,... | collective-permute-start | bytes 5898248 | tf_op jit(solution)/shard_map/ppermute | solution.py:1134
  289.0 14.2 %collective-permute-start.30 = (bf16[8,48,1280]{2,1,0:T(8,128)(2,1)S(1)}, bf16[8,48,1280]{2,1,0:T(8,128)(2,1)S(1)}, u32[]{:S(2)}, u32[]{:S(2)}) collective-permute-start(bf16[8,48,1280]{2,1,0:T(8,128)(2,1)S(1)} %get-tuple-element.242), channel_id=1, source_target_pairs={{0,4},{1,5},{2,3},{3,2},{4,0},{5,1},{6,7},{7,6},{8,12},{9,13},{10,... | collective-permute-start | bytes 2949128 | tf_op jit(solution)/shard_map/ppermute | solution.py:1134
  298.2 9.7 %collective-permute-start.37 = (bf16[48,2048]{1,0:T(8,128)(2,1)S(1)}, bf16[48,2048]{1,0:T(8,128)(2,1)S(1)}, u32[]{:S(2)}, u32[]{:S(2)}) collective-permute-start(bf16[48,2048]{1,0:T(8,128)(2,1)S(1)} %get-tuple-element.249), channel_id=1, source_target_pairs={{0,24},{1,25},{2,26},{3,27},{4,28},{5,29},{6,30},{7,31},{8,16},{9,... | collective-permute-start | bytes 589832 | tf_op jit(solution)/shard_map/ppermute | solution.py:1134
  300.1 17.2 %collective-permute-start.36 = (bf16[48,2048]{1,0:T(8,128)(2,1)S(1)}, bf16[48,2048]{1,0:T(8,128)(2,1)S(1)}, u32[]{:S(2)}, u32[]{:S(2)}) collective-permute-start(bf16[48,2048]{1,0:T(8,128)(2,1)S(1)} %get-tuple-element.250), channel_id=1, source_target_pairs={{0,16},{1,17},{2,18},{3,19},{4,20},{5,21},{6,22},{7,23},{8,24},{9,... | collective-permute-start | bytes 589832 | tf_op jit(solution)/shard_map/ppermute | solution.py:1134
  300.1 17.2 %collective-permute-start.35 = (bf16[48,2048]{1,0:T(8,128)(2,1)S(1)}, bf16[48,2048]{1,0:T(8,128)(2,1)S(1)}, u32[]{:S(2)}, u32[]{:S(2)}) collective-permute-start(bf16[48,2048]{1,0:T(8,128)(2,1)S(1)} %get-tuple-element.251), channel_id=1, source_target_pairs={{0,8},{1,9},{2,10},{3,11},{4,12},{5,13},{6,14},{7,15},{8,0},{9,1},... | collective-permute-start | bytes 589832 | tf_op jit(solution)/shard_map/ppermute | solution.py:1134
  303.4 14.7 %collective-permute-start.31 = (bf16[4,48,1280]{2,1,0:T(8,128)(2,1)S(1)}, bf16[4,48,1280]{2,1,0:T(8,128)(2,1)S(1)}, u32[]{:S(2)}, u32[]{:S(2)}) collective-permute-start(bf16[4,48,1280]{2,1,0:T(8,128)(2,1)S(1)} %get-tuple-element.248), channel_id=1, source_target_pairs={{0,1},{1,0},{2,6},{3,7},{4,5},{5,4},{6,2},{7,3},{8,9},{9,8},{10,14... | collective-permute-start | bytes 1474568 | tf_op jit(solution)/shard_map/ppermute | solution.py:1134
  318.2 6.9 %collective-permute-start.32 = (bf16[48,1280]{1,0:T(8,128)(2,1)S(1)}, bf16[48,1280]{1,0:T(8,128)(2,1)S(1)}, u32[]{:S(2)}, u32[]{:S(2)}) collective-permute-start(bf16[48,1280]{1,0:T(8,128)(2,1)S(1)} %get-tuple-element.257), channel_id=1, source_target_pairs={{0,8},{1,9},{2,10},{3,11},{4,12},{5,13},{6,14},{7,15},{8,0},{9,1},... | collective-permute-start | bytes 368648 | tf_op jit(solution)/shard_map/ppermute | solution.py:1134
  318.2 8.2 %collective-permute-start.34 = (bf16[48,1280]{1,0:T(8,128)(2,1)S(1)}, bf16[48,1280]{1,0:T(8,128)(2,1)S(1)}, u32[]{:S(2)}, u32[]{:S(2)}) collective-permute-start(bf16[48,1280]{1,0:T(8,128)(2,1)S(1)} %get-tuple-element.258), channel_id=1, source_target_pairs={{0,24},{1,25},{2,26},{3,27},{4,28},{5,29},{6,30},{7,31},{8,16},{9,... | collective-permute-start | bytes 368648 | tf_op jit(solution)/shard_map/ppermute | solution.py:1134
  319.8 12.2 %collective-permute-start.33 = (bf16[48,1280]{1,0:T(8,128)(2,1)S(1)}, bf16[48,1280]{1,0:T(8,128)(2,1)S(1)}, u32[]{:S(2)}, u32[]{:S(2)}) collective-permute-start(bf16[48,1280]{1,0:T(8,128)(2,1)S(1)} %get-tuple-element.259), channel_id=1, source_target_pairs={{0,16},{1,17},{2,18},{3,19},{4,20},{5,21},{6,22},{7,23},{8,24},{9,... | collective-permute-start | bytes 368648 | tf_op jit(solution)/shard_map/ppermute | solution.py:1134
  (14 other events, 24.5 us)

commit v4 on v3

--- a/solution.py
+++ b/solution.py
@@ -158,8 +158,37 @@
     return pl.BlockSpec(memory_space=pltpu.SMEM)
 
 
-def params(megabytes=56):
+def params(megabytes=32):
     return pltpu.CompilerParams(vmem_limit_bytes=megabytes * 1024 * 1024)
+
+
+def call(kernel, *, out_shape, near_in=(), near_out=(), least=65536, **options):
+    shapes = list(out_shape) if isinstance(out_shape, (list, tuple)) else [out_shape]
+
+    def large(value):
+        return math.prod(value.shape) * value.dtype.itemsize > least
+
+    placed = [
+        pltpu.HBM(shape.shape, shape.dtype) if large(shape) and at not in near_out else shape
+        for at, shape in enumerate(shapes)
+    ]
+    function = pl.pallas_call(
+        kernel, out_shape=placed if isinstance(out_shape, (list, tuple)) else placed[0], **options
+    )
+
+    def run(*operands):
+        count = len(operands)
+        near = {at % count for at in near_in}
+        return function(
+            *[
+                pltpu.with_memory_space_constraint(value, pltpu.HBM)
+                if large(value) and at not in near
+                else value
+                for at, value in enumerate(operands)
+            ]
+        )
+
+    return run
 
 
 def whole(shape):
@@ -202,12 +231,13 @@
 
 def pack(q, k, v, out, thins):
     shard, part = q.shape
-    return pl.pallas_call(
+    return call(
         pack_kernel,
         out_shape=jax.ShapeDtypeStruct((shard, 4 * part + LANES), BF16),
         compiler_params=params(),
         cost_estimate=cost(1e8, 1e6),
         name="pack",
+        least=0,
     )(q, k, v, out, *[thin.reshape(1, -1) for thin in thins])
 
 
@@ -237,7 +267,7 @@
 
 
 def selectors(width, part, shard, edge, each):
-    return pl.pallas_call(
+    return call(
         functools.partial(selectors_kernel, shard=shard, edge=edge, each=each),
         out_shape=[
             jax.ShapeDtypeStruct((width, part), BF16),
@@ -268,7 +298,7 @@
 
 def unpack(w, turns, shard, each):
     _, halves, width, columns = w.shape
-    return pl.pallas_call(
+    return call(
         functools.partial(unpack_kernel, shard=shard, each=each),
         grid=(1,),
         in_specs=[
@@ -292,12 +322,13 @@
 
 
 def join(parts):
-    return pl.pallas_call(
+    return call(
         join_kernel,
         out_shape=jax.ShapeDtypeStruct((len(parts),) + parts[0].shape, parts[0].dtype),
         compiler_params=params(),
         cost_estimate=cost(0, 1e6),
         name="join",
+        least=0,
     )(*parts)
 
 
@@ -380,7 +411,7 @@
             block=block, step=rows, shard=shard, halves=halves,
         )
 
-    return pl.pallas_call(
+    return call(
         kernel,
         grid=(halves,),
         in_specs=[scalars()]
@@ -440,7 +471,7 @@
     blocks = cm.shape[0]
     spec = pl.BlockSpec((rows, LANES), lambda p: (0, p))
     full = jax.ShapeDtypeStruct((rows, width), F32)
-    return pl.pallas_call(
+    return call(
         attend_kernel,
         grid=(pairs,),
         in_specs=[
@@ -453,6 +484,7 @@
         compiler_params=params(),
         cost_estimate=cost(8e9, 14e6),
         name="attend",
+        near_out=(0, 1),
     )(sq, sk, v, cm, cosines, sines, states)
 
 
@@ -501,7 +533,7 @@
     pairs = incoming.shape[0]
     wide = pl.BlockSpec((step, width), lambda i: (i, 0))
     thin = pl.BlockSpec((step, LANES), lambda i: (i, 0))
-    return pl.pallas_call(
+    return call(
         mix_kernel,
         grid=(rows // step,),
         in_specs=[
@@ -521,6 +553,8 @@
         compiler_params=params(),
         cost_estimate=cost(2 * rows * width * width * 2, 20e6),
         name="mix",
+        near_in=(0, 1),
+        near_out=(2, 4),
     )(num, den, sq, incoming, cosines, sines, w, x, vectors)
 
 
@@ -534,19 +568,27 @@
     return inner * scale
 
 
-def lift_kernel(coords_ref, *refs, step, row, half):
+def lift_kernel(coords_ref, *refs, step, row, halves):
     sources, refs = refs[:-8], refs[-8:]
     low_ref, bias_ref, act_ref, slope_ref, out_ref, held_ref, sems, out_sems = refs
     tile = act_ref.shape[1]
     now = pl.program_id(0)
-    weights = Weights(coords_ref, sources, held_ref, out_ref, sems, out_sems, [half])
+    tiles = pl.num_programs(0) // halves
+    weights = Weights(coords_ref, sources, held_ref, out_ref, sems, out_sems, range(halves))
 
     @pl.when(now == 0)
     def _():
-        weights.start(0)
-        weights.ready(0)
-
-    up = held_ref[0, :, pl.ds(pl.multiple_of(now * tile, tile), tile)]
+        for half in range(halves):
+            weights.start(half)
+
+    for half in range(halves):
+
+        @pl.when(now == half * tiles)
+        def _():
+            weights.ready(half)
+
+    begin = pl.multiple_of(now % tiles * tile, tile)
+    up = held_ref[now // tiles, :, pl.ds(begin, tile)]
 
     def body(place, carry):
         here = pl.ds(place * step, step)
@@ -561,33 +603,57 @@
 
     @pl.when(now == pl.num_programs(0) - 1)
     def _():
-        weights.left(0)
-
-
-def lift(coords, low, sources, bias, half, units, tile, row):
+        for half in range(halves):
+            weights.left(half)
+
+
+def lift(coords, low, sources, bias, units, tile, row):
     rows, width = low.shape
+    halves = bias.shape[0]
+    tiles = units // tile
     unit_spec = pl.BlockSpec((rows, tile), lambda i: (0, i))
-    shape = jax.ShapeDtypeStruct((rows, units), BF16)
-    return pl.pallas_call(
-        functools.partial(lift_kernel, step=256, row=row, half=half),
-        grid=(units // tile,),
+    shape = jax.ShapeDtypeStruct((rows, halves * units), BF16)
+    return call(
+        functools.partial(lift_kernel, step=256, row=row, halves=halves),
+        grid=(halves * tiles,),
         in_specs=[scalars()]
         + anywhere(len(sources))
-        + [whole((rows, width)), pl.BlockSpec((1, 8, tile), lambda i: (half, 0, i))],
+        + [whole((rows, width)), pl.BlockSpec((1, 8, tile), lambda i: (i // tiles, 0, i % tiles))],
         out_specs=[unit_spec, unit_spec] + anywhere(1),
-        out_shape=[shape, shape, jax.ShapeDtypeStruct((1, 1, width, units), BF16)],
-        scratch_shapes=Weights.scratch(1, width, units),
-        compiler_params=params(),
-        cost_estimate=cost(2 * rows * width * units, 10e6),
+        out_shape=[shape, shape, jax.ShapeDtypeStruct((1, halves, width, units), BF16)],
+        scratch_shapes=Weights.scratch(halves, width, units),
+        compiler_params=params(),
+        cost_estimate=cost(2 * rows * width * halves * units, 20e6),
         name="lift",
+        near_in=(-2,),
+        near_out=(0, 1),
     )(coords, *sources, low, bias)
 
 
+def in_turn(product, finish, total_ref):
+    now = pl.program_id(0)
+    last = pl.num_programs(0) - 1
+
+    @pl.when(now == 0)
+    def _():
+        total_ref[0] = product()
+
+    @pl.when((now > 0) & (now < last))
+    def _():
+        finish(total_ref[(now - 1) % 2])
+        total_ref[now % 2] = product()
+
+    @pl.when(now == last)
+    def _():
+        finish(total_ref[(now - 1) % 2])
+
+
 def drop_kernel(coords_ref, *refs, halves):
-    sources, acts, refs = refs[: -11 - halves], refs[-11 - halves : -11], refs[-11:]
+    sources, act_ref, refs = refs[:-13], refs[-13], refs[-12:]
     normal_ref, vec_ref, grad_ref, out_ref, branch_ref, second_ref, sum_ref = refs[:7]
-    whole_ref, held_ref, sems, out_sems = refs[7:]
+    whole_ref, held_ref, sems, out_sems, total_ref = refs[7:]
     weights = Weights(coords_ref, sources, held_ref, whole_ref, sems, out_sems, range(halves))
+    units = held_ref.shape[2]
 
     @pl.when(pl.program_id(0) == 0)
     def _():
@@ -597,19 +663,27 @@
         for half in range(halves):
             weights.ready(half)
 
-    total = normal_ref[...] * vec_ref[1:2, :] + vec_ref[2:3, :] + vec_ref[3:4, :]
-    for half, act_ref in enumerate(acts):
-        total = total + dot_nt(act_ref[...], held_ref[half])
-    normal, scale = norm_rows(total)
-    gain = vec_ref[4:5, :]
-    out_ref[...] = (normal * gain + vec_ref[5:6, :]).astype(BF16)
-    upstream = grad_ref[...].astype(F32)
-    second = norm_back(upstream, normal, scale, gain)
-    second_ref[...] = second
-    branch_ref[...] = second.astype(BF16)
-    sum_ref[0:1, :] += jnp.sum(upstream * normal, axis=0, keepdims=True)
-    sum_ref[1:2, :] += jnp.sum(upstream, axis=0, keepdims=True)
-    sum_ref[2:3, :] += jnp.sum(second, axis=0, keepdims=True)
+    def product():
+        total = None
+        for half in range(halves):
+            term = dot_nt(act_ref[:, half * units : (half + 1) * units], held_ref[half])
+            total = term if total is None else total + term
+        return total
+
+    def finish(total):
+        total = total + normal_ref[...] * vec_ref[1:2, :] + vec_ref[2:3, :] + vec_ref[3:4, :]
+        normal, scale = norm_rows(total)
+        gain = vec_ref[4:5, :]
+        out_ref[...] = (normal * gain + vec_ref[5:6, :]).astype(BF16)
+        upstream = grad_ref[...].astype(F32)
+        second = norm_back(upstream, normal, scale, gain)
+        second_ref[...] = second
+        branch_ref[...] = second.astype(BF16)
+        sum_ref[0:1, :] += jnp.sum(upstream * normal, axis=0, keepdims=True)
+        sum_ref[1:2, :] += jnp.sum(upstream, axis=0, keepdims=True)
+        sum_ref[2:3, :] += jnp.sum(second, axis=0, keepdims=True)
+
+    in_turn(product, finish, total_ref)
 
     @pl.when(pl.program_id(0) == pl.num_programs(0) - 1)
     def _():
@@ -619,15 +693,18 @@
 
 def drop(coords, act, sources, normal, vectors, grad, units, step):
     rows, width = normal.shape
-    halves = len(act)
-    wide = pl.BlockSpec((step, width), lambda i: (i, 0))
-    return pl.pallas_call(
+    halves = act.shape[1] // units
+    steps = rows // step
+    wide = pl.BlockSpec((step, width), lambda i: (jnp.maximum(i - 1, 0), 0))
+    return call(
         functools.partial(drop_kernel, halves=halves),
-        grid=(rows // step,),
+        grid=(steps + 1,),
         in_specs=[scalars()]
         + anywhere(len(sources))
-        + [pl.BlockSpec((step, units), lambda i: (i, 0))] * halves
-        + [wide, whole(vectors.shape), wide],
+        + [
+            pl.BlockSpec((step, halves * units), lambda i: (jnp.minimum(i, steps - 1), 0)),
+            wide, whole(vectors.shape), wide,
+        ],
         out_specs=[wide, wide, wide, whole((8, width))] + anywhere(1),
         out_shape=[
             jax.ShapeDtypeStruct((rows, width), BF16),
@@ -636,11 +713,13 @@
             jax.ShapeDtypeStruct((8, width), F32),
             jax.ShapeDtypeStruct((1, halves, width, units), BF16),
         ],
-        scratch_shapes=Weights.scratch(halves, width, units),
+        scratch_shapes=Weights.scratch(halves, width, units) + [pltpu.VMEM((2, step, width), F32)],
         compiler_params=params(),
         cost_estimate=cost(2 * rows * width * halves * units, 20e6),
         name="drop",
-    )(coords, *sources, *act, normal, vectors, grad)
+        near_in=(-4, -3),
+        near_out=(1, 2),
+    )(coords, *sources, act, normal, vectors, grad)
 
 
 def piece_outputs(layout, tile, index_map):
@@ -655,33 +734,38 @@
     return [spec], [jax.ShapeDtypeStruct((halves, width, columns), BF16)]
 
 
-def wide_gradient_kernel(coords_ref, left_ref, *refs, halves):
-    rights, outs, product_ref = refs[:halves], refs[halves:-1], refs[-1]
+def wide_gradient_kernel(coords_ref, left_ref, *refs, halves, partial):
+    rights, product_ref = refs[:halves], refs[-1]
+    outs = refs[(len(refs) - 1 + halves) // 2 : -1] if partial else refs[halves:-1]
     coords = [coords_ref[place] for place in range(4)]
     for half, right_ref in enumerate(rights):
         product_ref[...] = dot_tn(left_ref[...], right_ref[...]).astype(BF16)
         emit(product_ref, half, outs, coords)
 
 
-def wide_gradient(coords, left, right, layout, units, tile, name):
+def wide_gradient(coords, left, right, layout, units, tile, name, partial=()):
     rows, width = left.shape
     halves = layout[1]
     tiles = units // tile
     out_specs, out_shapes = piece_outputs(layout, tile, lambda j: j)
-    return pl.pallas_call(
-        functools.partial(wide_gradient_kernel, halves=halves),
+    return call(
+        functools.partial(wide_gradient_kernel, halves=halves, partial=bool(partial)),
         grid=(tiles,),
         in_specs=[scalars(), whole((rows, width))]
         + [
-            pl.BlockSpec((rows, tile), lambda j: (0, j)) for half in range(halves)
-        ],
+            pl.BlockSpec((rows, tile), lambda j, half=half: (0, half * tiles + j))
+            for half in range(halves)
+        ]
+        + anywhere(len(partial)),
         out_specs=out_specs,
         out_shape=out_shapes,
+        input_output_aliases={2 + halves + at: at for at in range(len(partial))},
         scratch_shapes=[pltpu.VMEM((width, tile), BF16)],
         compiler_params=params(),
         cost_estimate=cost(2 * rows * width * halves * units, 18e6),
         name=name,
-    )(coords, left, *right)
+        near_in=(1, 2, 3),
+    )(coords, left, *([right] * halves), *partial)
 
 
 def bend_kernel(branch_ref, down_ref, slope_ref, gl_ref, gbias_ref, *, step):
@@ -698,64 +782,74 @@
     lax.fori_loop(0, branch_ref.shape[0] // step, body, 0, unroll=True)
 
 
-def bend(branch, w, slope, half, units, tile):
+def bend(branch, w, slope, units, tile):
     rows, width = branch.shape
+    halves = w.shape[1]
     tiles = units // tile
     unit_spec = pl.BlockSpec((rows, tile), lambda i: (0, i))
-    return pl.pallas_call(
+    return call(
         functools.partial(bend_kernel, step=256),
-        grid=(tiles,),
+        grid=(halves * tiles,),
         in_specs=[
             whole((rows, width)),
-            pl.BlockSpec((1, 1, width, tile), lambda i: (0, half, 0, i)),
+            pl.BlockSpec((1, 1, width, tile), lambda i: (0, i // tiles, 0, i % tiles)),
             unit_spec,
         ],
         out_specs=[unit_spec, pl.BlockSpec((8, tile), lambda i: (0, i))],
         out_shape=[
-            jax.ShapeDtypeStruct((rows, units), BF16),
-            jax.ShapeDtypeStruct((8, units), F32),
-        ],
-        compiler_params=params(),
-        cost_estimate=cost(2 * rows * width * units, 10e6),
+            jax.ShapeDtypeStruct(slope.shape, BF16),
+            jax.ShapeDtypeStruct((8, halves * units), F32),
+        ],
+        compiler_params=params(),
+        cost_estimate=cost(2 * rows * width * halves * units, 20e6),
         name="bend",
+        near_in=(0, 2),
+        near_out=(0,),
     )(branch, w, slope)
 
 
-def lower_kernel(*refs):
-    count = (len(refs) - 7) // 2
-    gls, ups = refs[:count], refs[count : 2 * count]
-    second_ref, normal_ref, scale_ref, vec_ref, first_ref, firstlow_ref, sum_ref = refs[-7:]
+def lower_kernel(
+    gl_ref, up_ref, second_ref, normal_ref, scale_ref, vec_ref, first_ref, firstlow_ref, sum_ref,
+    total_ref,
+):
+    halves, units = up_ref.shape[1], up_ref.shape[3]
 
     @pl.when(pl.program_id(0) == 0)
     def _():
         sum_ref[...] = jnp.zeros_like(sum_ref)
 
-    upstream = second_ref[...]
-    for gl_ref, up_ref in zip(gls, ups):
-        upstream = upstream + dot_nt(gl_ref[...], up_ref[0, 0])
-    normal = normal_ref[...]
-    first = norm_back(upstream, normal, scale_ref[:, 0:1], vec_ref[1:2, :])
-    first_ref[...] = first
-    firstlow_ref[...] = first.astype(BF16)
-    sum_ref[0:1, :] += jnp.sum(upstream * normal, axis=0, keepdims=True)
-    sum_ref[1:2, :] += jnp.sum(upstream, axis=0, keepdims=True)
-    sum_ref[2:3, :] += jnp.sum(first, axis=0, keepdims=True)
+    def product():
+        total = None
+        for half in range(halves):
+            term = dot_nt(gl_ref[:, half * units : (half + 1) * units], up_ref[0, half])
+            total = term if total is None else total + term
+        return total
+
+    def finish(total):
+        upstream = second_ref[...] + total
+        normal = normal_ref[...]
+        first = norm_back(upstream, normal, scale_ref[:, 0:1], vec_ref[1:2, :])
+        first_ref[...] = first
+        firstlow_ref[...] = first.astype(BF16)
+        sum_ref[0:1, :] += jnp.sum(upstream * normal, axis=0, keepdims=True)
+        sum_ref[1:2, :] += jnp.sum(upstream, axis=0, keepdims=True)
+        sum_ref[2:3, :] += jnp.sum(first, axis=0, keepdims=True)
+
+    in_turn(product, finish, total_ref)
 
 
 def lower(gl, w, second, normal, scale, vectors, units, step):
     rows, width = second.shape
-    halves = len(w)
-    wide = pl.BlockSpec((step, width), lambda i: (i, 0))
-    return pl.pallas_call(
+    steps = rows // step
+    wide = pl.BlockSpec((step, width), lambda i: (jnp.maximum(i - 1, 0), 0))
+    return call(
         lower_kernel,
-        grid=(rows // step,),
-        in_specs=[pl.BlockSpec((step, units), lambda i: (i, 0))] * halves
-        + [
-            whole((1, 1, width, units)) for half in range(halves)
-        ]
-        + [
-            wide, wide,
-            pl.BlockSpec((step, LANES), lambda i: (i, 0)), whole(vectors.shape),
+        grid=(steps + 1,),
+        in_specs=[
+            pl.BlockSpec((step, gl.shape[1]), lambda i: (jnp.minimum(i, steps - 1), 0)),
+            whole(w.shape), wide, wide,
+            pl.BlockSpec((step, LANES), lambda i: (jnp.maximum(i - 1, 0), 0)),
+            whole(vectors.shape),
         ],
         out_specs=[wide, wide, whole((8, width))],
         out_shape=[
@@ -763,23 +857,21 @@
             jax.ShapeDtypeStruct((rows, width), BF16),
             jax.ShapeDtypeStruct((8, width), F32),
         ],
-        compiler_params=params(),
-        cost_estimate=cost(2 * rows * width * halves * units, 20e6),
+        scratch_shapes=[pltpu.VMEM((2, step, width), F32)],
+        compiler_params=params(),
+        cost_estimate=cost(2 * rows * width * gl.shape[1], 20e6),
         name="lower",
-    )(*gl, *w, second, normal, scale, vectors)
+        near_in=(0, 2, 3),
+        near_out=(1,),
+    )(gl, w, second, normal, scale, vectors)
 
 
 def unmix_kernel(
     coords_ref, first_ref, mixed_ref, rden_ref, sq_ref, cos_ref, sin_ref, w_ref,
-    sum1_ref, sum2_ref, turn_ref, *refs, block, step, shard, halves
+    sum1_ref, sum2_ref, turn_ref, *refs, block, step, shard
 ):
-    biases = [ref[0:1, :] for ref in refs[:halves]]
-    refs = refs[halves:]
-    refs = refs[(len(refs) - 5) // 2 :]
-    bias = biases[0]
-    for half in range(1, halves):
-        bias = jnp.where(pl.program_id(0) == half, biases[half], bias)
-    bias = jnp.broadcast_to(bias, (8, bias.shape[1]))
+    bias = jnp.broadcast_to(refs[0][0:1, :], refs[0].shape)
+    refs = refs[1:]
     outs = refs[:-5]
     gn_ref, gd_ref, st_ref, tot_ref, product_ref = refs[-5:]
     coords = [coords_ref[place] for place in range(4)]
@@ -856,7 +948,7 @@
 
 
 def unmix(
-    coords, first, mixed, rden, sq, cosines, sines, w, sums1, sums2, turns, gbias, partial, layout, block
+    coords, first, mixed, rden, sq, cosines, sines, w, sums1, sums2, turns, gbias, layout, block
 ):
     rows, width = first.shape
     groups, halves, shard, _ = w.shape
@@ -867,11 +959,11 @@
     row_spec = pl.BlockSpec((rows, part), lambda t: (0, t))
     tile = part + LANES
     out_specs, out_shapes = piece_outputs(layout, tile, lambda t: layout[3] // tile - 1)
-    units = gbias[0].shape[1]
+    units = gbias.shape[1] // halves
     full = jax.ShapeDtypeStruct((rows, width), BF16)
-    return pl.pallas_call(
+    return call(
         functools.partial(
-            unmix_kernel, block=block, step=512, shard=layout[2], halves=halves
+            unmix_kernel, block=block, step=512, shard=layout[2]
         ),
         grid=(halves,),
         in_specs=[
@@ -880,9 +972,7 @@
             pl.BlockSpec((groups, 1, shard, part), lambda t: (0, t, 0, 3)),
             whole((8, width)), whole((8, width)), whole(turns.shape),
         ]
-        + [whole((8, units))] * halves
-        + [pl.BlockSpec(memory_space=pl.ANY)] * len(partial),
-        input_output_aliases={11 + halves + at: at for at in range(len(partial))},
+        + [pl.BlockSpec((8, units), lambda t: (0, t))],
         out_specs=out_specs
         + [
             row_spec, row_spec,
@@ -899,12 +989,14 @@
         compiler_params=params(),
         cost_estimate=cost(4 * rows * width * width, 16e6),
         name="unmix",
-    )(coords, first, mixed, rden, sq, cosines, sines, w, sums1, sums2, turns, *gbias, *partial)
+        near_in=(1,),
+        near_out=(len(out_shapes), len(out_shapes) + 1),
+    )(coords, first, mixed, rden, sq, cosines, sines, w, sums1, sums2, turns, gbias)
 
 
 def unattend_kernel(
     sq_ref, sk_ref, v_ref, gn_ref, gd_ref, cm_ref, cos_ref, sin_ref, st_ref, in_ref, lt_ref, gq_ref,
-    *refs,
+    gk_ref, later_ref, *refs,
 ):
     query_ref, dk_ref, dv_ref = refs[-3:]
     blocks, block, _ = cm_ref.shape
@@ -912,6 +1004,7 @@
     masks = [lane_mask(block, head) for head in range(2)]
     ones = jnp.ones((block, LANES), BF16)
     incoming = expand(in_ref[0].astype(F32))
+    outgoing = expand(later_ref[0].astype(F32))
     for place in range(blocks):
         start = place * block
         all_here = slice(start, start + block)
@@ -958,28 +1051,32 @@
             query_ref[here, :] = grad_queries.astype(BF16)
         grad_keys = jnp.concatenate(grad_keys, axis=0)
         grad_values = jnp.concatenate(grad_values, axis=0)
+        state = outgoing
         for later in range(place + 1, blocks):
-            far = dot_nt(sides, lt_ref[later, 0])
-            grad_keys = (
-                grad_keys
-                + far[:, :LANES] * cos_ref[all_here, :]
-                + far[:, LANES:] * sin_ref[all_here, :]
-            )
-            features = turned_features(keys, cos_ref[all_here, :], sin_ref[all_here, :])
-            grad_values = grad_values + dot(features, lt_ref[later, 0][:, :LANES])
-        dk_ref[all_here, :] = grad_keys
-        dv_ref[all_here, :] = grad_values
+            state = state + lt_ref[later, 0].astype(F32)
+        state = state.astype(BF16)
+        far = dot_nt(sides, state)
+        grad_keys = (
+            grad_keys
+            + far[:, :LANES] * cos_ref[all_here, :]
+            + far[:, LANES:] * sin_ref[all_here, :]
+        ) * gk_ref[all_here, :].astype(F32)
+        features = turned_features(keys, cos_ref[all_here, :], sin_ref[all_here, :])
+        grad_values = grad_values + dot(features, state[:, :LANES])
+        dk_ref[all_here, :] = grad_keys.astype(BF16)
+        dv_ref[all_here, :] = grad_values.astype(BF16)
 
 
 def unattend(
-    sq, sk, v, gn, gd, cm, cosines, sines, states, incoming, later, slope_q, start, count, partial
+    sq, sk, v, gn, gd, cm, cosines, sines, states, incoming, later, slope_q, slope_k,
+    later_in, start, count, partial
 ):
     rows, width = sq.shape
     blocks = cm.shape[0]
     spec = pl.BlockSpec((rows, LANES), lambda p: (0, start + p))
     state_spec = pl.BlockSpec((blocks, 1, 2 * LANES, 2 * LANES), lambda p: (0, start + p, 0, 0))
-    full = jax.ShapeDtypeStruct((rows, width), F32)
-    return pl.pallas_call(
+    full = jax.ShapeDtypeStruct((rows, width), BF16)
+    return call(
         unattend_kernel,
         grid=(count,),
         in_specs=[
@@ -987,51 +1084,19 @@
             whole(cm.shape), whole((rows, LANES)), whole((rows, LANES)),
             state_spec,
             pl.BlockSpec((1, 2 * LANES, LANES), lambda p: (start + p, 0, 0)),
-            state_spec, spec,
+            state_spec, spec, spec,
+            pl.BlockSpec((1, 2 * LANES, LANES), lambda p: (start + p, 0, 0)),
         ]
         + [pl.BlockSpec(memory_space=pl.ANY)] * len(partial),
         out_specs=[spec, spec, spec],
         out_shape=[jax.ShapeDtypeStruct((rows, width), BF16), full, full],
-        input_output_aliases={12 + at: at for at in range(len(partial))},
+        input_output_aliases={14 + at: at for at in range(len(partial))},
         compiler_params=params(),
         cost_estimate=cost(20e9, 20e6),
         name="unattend",
-    )(sq, sk, v, gn, gd, cm, cosines, sines, states, incoming, later, slope_q, *partial)
-
-
-def tail_kernel(
-    dk_ref, dv_ref, sk_ref, v_ref, gk_ref, cos_ref, sin_ref, in_ref, key_ref, value_ref
-):
-    rows, part = dk_ref.shape
-    ones = jnp.ones((rows, LANES), BF16)
-    cosines, sines = cos_ref[...], sin_ref[...]
-    for pair in range(part // LANES):
-        lanes = slice(pair * LANES, (pair + 1) * LANES)
-        state = expand(in_ref[pair].astype(F32)).astype(BF16)
-        far = dot_nt(jnp.concatenate([v_ref[:, lanes], ones], axis=1), state)
-        keys = dk_ref[:, lanes] + far[:, :LANES] * cosines + far[:, LANES:] * sines
-        key_ref[:, lanes] = (keys * gk_ref[:, lanes].astype(F32)).astype(BF16)
-        features = turned_features(sk_ref[:, lanes], cosines, sines)
-        value_ref[:, lanes] = (dv_ref[:, lanes] + dot(features, state[:, :LANES])).astype(BF16)
-
-
-def tail(dk, dv, sk, v, slope_k, cosines, sines, incoming):
-    rows, width = sk.shape
-    spec = pl.BlockSpec((rows, LANES), lambda p: (0, p))
-    full = jax.ShapeDtypeStruct((rows, width), BF16)
-    return pl.pallas_call(
-        tail_kernel,
-        grid=(width // LANES,),
-        in_specs=[
-            spec, spec, spec, spec, spec, whole((rows, LANES)), whole((rows, LANES)),
-            pl.BlockSpec((1, 2 * LANES, LANES), lambda p: (p, 0, 0)),
-        ],
-        out_specs=[spec, spec],
-        out_shape=[full, full],
-        compiler_params=params(),
-        cost_estimate=cost(2e9, 14e6),
-        name="tail",
-    )(dk, dv, sk, v, slope_k, cosines, sines, incoming)
+        near_in=(3, 4, 14, 15, 16),
+        near_out=(0, 1, 2),
+    )(sq, sk, v, gn, gd, cm, cosines, sines, states, incoming, later, slope_q, slope_k, later_in, *partial)
 
 
 def weights_kernel(coords_ref, x_ref, q_ref, k_ref, v_ref, edge_ref, *refs, shard):
@@ -1063,7 +1128,7 @@
     halves = layout[1]
     spec = pl.BlockSpec((rows, width // halves), lambda t: (0, t))
     out_specs, out_shapes = piece_outputs(layout, layout[3], lambda t: 0)
-    return pl.pallas_call(
+    return call(
         functools.partial(weights_kernel, shard=layout[2]),
         grid=(halves,),
         in_specs=[scalars(), whole((rows, width)), spec, spec, spec, whole(edges.shape)],
@@ -1073,6 +1138,7 @@
         compiler_params=params(),
         cost_estimate=cost(2 * rows * width * 3 * width, 10e6),
         name="weight_gradients",
+        near_in=(2, 3, 4),
     )(coords, x, q, k, v, edges)
 
 
@@ -1094,7 +1160,7 @@
     groups, halves, shard, _ = w.shape
     part = width // halves
     spec = pl.BlockSpec((step, width), lambda i: (i, 0))
-    return pl.pallas_call(
+    return call(
         inputs_kernel,
         grid=(rows // step,),
         in_specs=[
@@ -1106,6 +1172,7 @@
         compiler_params=params(),
         cost_estimate=cost(2 * rows * width * 3 * width, 14e6),
         name="input_gradient",
+        near_in=(1, 2, 3),
     )(first, q, k, v, w)
 
 
@@ -1297,80 +1364,65 @@
         down_chunk.across(there, [low])
         there = [down_chunk.held]
         low = after(low, *there)
-    act, slope, w_up_halves, now = [], [], [], low
-    for half in range(halves):
-        act_half, slope_half, w_half = lift(
-            coords, now, w_lift, bias_up, half, units, 768, 3 if pieces else 0
-        )
-        w_up_halves.append(w_half)
-        act.append(act_half)
-        slope.append(slope_half)
+    act, slope, w_lift = lift(
+        coords, low, w_lift, bias_up, units, 768, 3 if pieces else 0
+    )
     if pieces:
-        w_drop = down_chunk.core(there, [act[1]])
+        w_drop = down_chunk.core(there, [act])
     output, branch, second, sums_second, w_drop = drop(
         coords, act, w_drop, normal, vectors, grad_output, units, 256
     )
 
     gdown = wide_gradient(coords, branch, act, layout(units), units, 512, "down_gradient")
-    there = gdown
+    gl, gbias_up = bend(branch, w_drop, after(slope, *gdown), units, 768)
     if pieces:
         down_sum = Sum(*gdown)
-    gl, gbias_up = [], []
-    for half in range(halves):
-        now = after(slope[half], *there)
-        gl_half, gbias_half = bend(branch, w_drop, now, half, units, 768)
-        gl.append(gl_half)
-        gbias_up.append(gbias_half)
-        if pieces and half == 0:
-            down_sum.core([], [gl_half])
-            there = down_sum.both()
+        down_sum.core([], [gl])
+        second = after(second, *down_sum.both())
+    first, first_low, sums_first = lower(gl, w_lift, second, normal, scale, vectors, units, 256)
     wide = units + part + LANES
-    gup = wide_gradient(coords, low, gl, layout(wide), units, 512, "up_gradient")
-    there = gup
-    if pieces:
-        down_sum.across([], gup)
-        there = [*gup, *down_sum.both()]
-    second = after(second, *there)
-    first, first_low, sums_first = lower(gl, w_up_halves, second, normal, scale, vectors, units, 256)
-    if pieces:
-        down_sum.beside([], [first])
-        first_low = after(first_low, *down_sum.parts)
     *gup, gn, gd, later, later_total = unmix(
         coords, first_low, mixed, rden, sq, cosines, sines, w_attention,
-        sums_first, sums_second, turns, gbias_up, gup, layout(wide), block,
+        sums_first, sums_second, turns, gbias_up, layout(wide), block,
     )
     there = []
     if pieces:
-        gdown = down_sum.line([], [gn])
-        there = [gdown]
-        gn = after(gn, gdown)
+        down_sum.across([], [gn])
+        there = down_sum.both()
+    gup = wide_gradient(
+        coords, after(low, *there, *gup), gl, layout(wide), units, 512, "up_gradient", gup
+    )
+    towards = [(i + 1, i) for i in range(halves - 1)]
+    later_in = send(later_total, towards, there, gup, "tp")
+    there = [later_in, *gup]
+    if pieces:
+        down_sum.beside([], gup)
+        there += down_sum.parts
+        up_sum = Sum(*gup)
+    gn = after(gn, *there)
     pairs = width // LANES
     partial = ()
     for half in range(halves):
         per = pairs // halves
         partial = unattend(
-            sq, sk, v, gn, gd, cm, cosines, sines, states, incoming, later, slope_q,
-            half * per, per, partial,
+            sq, sk, v, gn, gd, cm, cosines, sines, states, incoming, later, slope_q, slope_k,
+            later_in, half * per, per, partial,
         )
-        if half == 0:
-            towards = [(i + 1, i) for i in range(halves - 1)]
-            later_in = send(later_total, towards, there, partial, "tp")
         if pieces and half == 0:
-            up_sum = Sum(*gup)
             up_sum.core(there, partial)
-            partial = after(tuple(partial), later_in, *up_sum.both())
-    query_low, dk, dv = partial
-    key_low, value_low = tail(dk, dv, sk, v, slope_k, cosines, sines, later_in)
+            partial = after(tuple(partial), *up_sum.both())
+    query_low, key_low, value_low = partial
     if pieces:
-        up_sum.across([], [key_low])
-        query_low = after(query_low, *up_sum.both())
+        gdown = down_sum.line(there, [key_low])
+        query_low = after(query_low, gdown)
     gqkv = weight_gradients(
         coords, inputs, query_low, key_low, value_low, edges, layout(3 * part + LANES)
     )
     if pieces:
+        up_sum.across([], gqkv)
         rest_sum = Sum(*gqkv)
-        up_sum.beside([], gqkv)
-        rest_sum.core(up_sum.parts)
+        rest_sum.core(up_sum.both())
+        up_sum.beside([])
         rest_sum.across()
         gup = up_sum.line([], rest_sum.both())
         rest_sum.beside()

time: 340 us -> 318 us (0.935)
  Pallas kernels: 191 us -> 160 us
  waiting for transfers between devices: 71.1 us -> 86 us
  starting transfers between devices: 44.4 us -> 40.9 us
    pallas_call x22 -> x19, Pallas kernels: 191 us -> 160 us  [run(): function(*[pltpu.with_memory_space_constraint(value, pltpu.HBM) if large(...]
    ppermute x38, waiting for transfers between devices: 71.1 us -> 86 us  [send(): value = lax.ppermute(value, axes, table)]
    ppermute x38, starting transfers between devices: 44.4 us -> 40.9 us  [send(): value = lax.ppermute(value, axes, table)]
    unnamed x48 -> x62, local copies, waits for them, and re-layouts: 6.69 us -> 7.73 us
  transfers between devices with their start and end apart: 38 -> 38, of which waited for: 16 -> 17; matrix products, arithmetic and copies ran while one was open for 2% -> 3% of each run, Pallas kernels for 49% -> 43%
where the time goes in v4:
time: 318 us; the launch traced here: 312 us
  Pallas kernels  160 us (50%)
  waiting for transfers between devices  86 us (27%)
  starting transfers between devices  40.9 us (13%)
  local copies, waits for them, and re-layouts  14.1 us (4%)
  other arithmetic  9.34 us (3%)
    pallas_call x19, Pallas kernels, run(): function(*[pltpu.with_memory_space_constraint(value, pltpu.HBM) if large(...  160 us
    ppermute x38, waiting for transfers between devices, send(): value = lax.ppermute(value, axes, table)  86 us
    ppermute x38, starting transfers between devices, send(): value = lax.ppermute(value, axes, table)  40.9 us
    unnamed x62, local copies, waits for them, and re-layouts  7.73 us
  transfers between devices with their start and end apart: 38, of which 17 were waited for; matrix products, arithmetic and copies ran while one was open for 3% of the time, Pallas kernels for 43%

profile of v4, /device:TPU:0, one launch (start us, length us, event | category | flops | bytes accessed | tf_op | source)
XLA Modules:
  0.0 311.5 jit_solution(10540225114689022347)
XLA Ops:
  0.7 1.8 pack.1.refs_0_
  2.4 5.1 %collective-permute-start.2 = (bf16[48,1664]{1,0:T(8,128)(2,1)}, bf16[48,1664]{1,0:T(8,128)(2,1)S(1)}, u32[]{:S(2)}, u32[]{:S(2)}) collective-permute-start(bf16[48,1664]{1,0:T(8,128)(2,1)} %pack.1.refs_0_), channel_id=1, source_target_pairs={{0,24},{1,25},{2,26},{3,27},{4,28},{5,29},{6,30},{7,31},{8,16},{9,... | collective-permute-start | bytes 479240 | tf_op jit(solution)/shard_map/ppermute | solution.py:1201
  9.0 3.7 %collective-permute-done.2.refs_3_ = bf16[48,1664]{1,0:T(8,128)(2,1)S(1)} collective-permute-done((bf16[48,1664]{1,0:T(8,128)(2,1)}, bf16[48,1664]{1,0:T(8,128)(2,1)S(1)}, u32[]{:S(2)}, u32[]{:S(2)}) %collective-permute-start.2) | collective-permute-done | bytes 159776 | tf_op jit(solution)/shard_map/ppermute | solution.py:1201
  12.7 8.5 %collective-permute-done.1.refs_2_ = bf16[48,1664]{1,0:T(8,128)(2,1)S(1)} collective-permute-done((bf16[48,1664]{1,0:T(8,128)(2,1)}, bf16[48,1664]{1,0:T(8,128)(2,1)S(1)}, u32[]{:S(2)}, u32[]{:S(2)}) %collective-permute-start.1) | collective-permute-done | bytes 159776 | tf_op jit(solution)/shard_map/ppermute | solution.py:1201
  22.6 2.0 join.3
  26.4 1.8 add_select_fusion.cm_ref
  28.2 7.0 %collective-permute-done.3 = bf16[4,48,1664]{2,1,0:T(8,128)(2,1)S(1)} collective-permute-done((bf16[4,48,1664]{2,1,0:T(8,128)(2,1)}, bf16[4,48,1664]{2,1,0:T(8,128)(2,1)S(1)}, u32[]{:S(2)}, u32[]{:S(2)}) %collective-permute-start.3) | collective-permute-done | bytes 639008 | tf_op jit(solution)/shard_map/ppermute | solution.py:1201
  38.9 2.5 collective-permute-start.7
  41.4 1.9 collective-permute-start.5
  43.3 4.2 %collective-permute-done.7.refs_3_ = bf16[48,1536]{1,0:T(8,128)(2,1)S(1)} collective-permute-done((bf16[48,1536]{1,0:T(8,128)(2,1)S(1)}, bf16[48,1536]{1,0:T(8,128)(2,1)S(1)}, u32[]{:S(2)}, u32[]{:S(2)}) %collective-permute-start.7) | collective-permute-done | bytes 147488 | tf_op jit(solution)/shard_map/ppermute | solution.py:1201
  47.5 4.9 %collective-permute-done.6.refs_2_ = bf16[48,1536]{1,0:T(8,128)(2,1)S(1)} collective-permute-done((bf16[48,1536]{1,0:T(8,128)(2,1)S(1)}, bf16[48,1536]{1,0:T(8,128)(2,1)S(1)}, u32[]{:S(2)}, u32[]{:S(2)}) %collective-permute-start.6) | collective-permute-done | bytes 147488 | tf_op jit(solution)/shard_map/ppermute | solution.py:1201
  53.7 2.0 join.4
  57.2 9.3 %collective-permute-done.9 = bf16[4,48,1536]{2,1,0:T(8,128)(2,1)S(1)} collective-permute-done((bf16[4,48,1536]{2,1,0:T(8,128)(2,1)S(1)}, bf16[4,48,1536]{2,1,0:T(8,128)(2,1)S(1)}, u32[]{:S(2)}, u32[]{:S(2)}) %collective-permute-start.9) | collective-permute-done | bytes 589856 | tf_op jit(solution)/shard_map/ppermute | solution.py:1201
  67.7 1.5 collective-permute-start.12
  69.2 2.9 collective-permute-start.8
  72.1 14.5 %project.1 = (bf16[1024,768]{1,0:T(8,128)(2,1)}, bf16[1024,768]{1,0:T(8,128)(2,1)}, bf16[1024,768]{1,0:T(8,128)(2,1)}, bf16[1024,768]{1,0:T(8,128)(2,1)}, bf16[1...) custom-call(s32[4]{0:T(128)S(1)} %pad_add_fusion.coords_ref, ...), custom_call_target="tpu_custom_call" | custom-call | flops 3623878656 | bytes 16000000 | tf_op jit(solution)/shard_map/project/pallas_call | solution.py:182
  88.0 2.0 join.5
  90.9 3.1 collective-permute-start.15
  94.1 11.9 %attend.1 = (f32[1024,768]{1,0:T(8,128)S(1)}, f32[1024,768]{1,0:T(8,128)S(1)}) custom-call(bf16[1024,768]{1,0:T(8,128)(2,1)} %get-tuple-element.129.sq_ref, bf16[1024,768]{1,0:T(8,128)(2,1)} %get-tuple-element.130.sk_ref, bf16[1024,768]{1,0:T(8,128)(2,1)} %get-tuple-element.131.v_ref, f32[2,512,512]{2,1,0:T(8,128)} %add_select_fusion.cm_ref, ...), custom_call_target="tpu_custom_call" | custom-call | flops 8000000000 | bytes 14000000 | tf_op jit(solution)/shard_map/attend/pallas_call | solution.py:182
  106.0 4.9 %collective-permute-done.14 = bf16[4,48,1536]{2,1,0:T(8,128)(2,1)S(1)} collective-permute-done((bf16[4,48,1536]{2,1,0:T(8,128)(2,1)S(1)}, bf16[4,48,1536]{2,1,0:T(8,128)(2,1)S(1)}, u32[]{:S(2)}, u32[]{:S(2)}) %collective-permute-start.14) | collective-permute-done | bytes 589856 | tf_op jit(solution)/shard_map/ppermute | solution.py:1201
  111.2 2.3 unpack.1
  113.5 7.2 %mix.1 = (bf16[1024,768]{1,0:T(8,128)(2,1)}, f32[1024,768]{1,0:T(8,128)}, f32[1024,768]{1,0:T(8,128)S(1)}, f32[1024,128]{1,0:T(8,128)}, bf16[1024,768]{1,0:T(8,128)(2,1)S(1)}) custom-call(f32[1024,768]{1,0:T(8,128)S(1)} %get-tuple-element.141.num_ref, f32[1024,768]{1,0:T(8,128)S(1)} %get-tuple-element.142.den_ref, ...), custom_call_target="tpu_custom_call" | custom-call | flops 2415919104 | bytes 20000000 | tf_op jit(solution)/shard_map/mix/pallas_call | solution.py:182
  120.7 6.6 %collective-permute-done.17 = bf16[8,48,1536]{2,1,0:T(8,128)(2,1)S(1)} collective-permute-done((bf16[8,48,1536]{2,1,0:T(8,128)(2,1)S(1)}, bf16[8,48,1536]{2,1,0:T(8,128)(2,1)S(1)}, u32[]{:S(2)}, u32[]{:S(2)}) %collective-permute-start.17) | collective-permute-done | bytes 1179680 | tf_op jit(solution)/shard_map/ppermute | solution.py:1201
  127.7 11.8 %lift.1 = (bf16[1024,3072]{1,0:T(8,128)(2,1)S(1)}, bf16[1024,3072]{1,0:T(8,128)(2,1)S(1)}, bf16[1,2,768,1536]{3,2,1,0:T(8,128)(2,1)}) custom-call(s32[4]{0:T(128)S(1)} %pad_add_fusion.coords_ref, bf16[16,48,1536]{2,1,0:T(8,128)(2,1)} %copy-done.9, bf16[16,48,1536]{2,1,0:T(8,128)(2,1)} %copy-done.25, ...), custom_call_target="tpu_custom_call" | custom-call | flops 4831838208 | bytes 20000000 | tf_op jit(solution)/shard_map/lift/pallas_call | solution.py:182
  140.9 12.6 %drop.1 = (bf16[1024,768]{1,0:T(8,128)(2,1)}, bf16[1024,768]{1,0:T(8,128)(2,1)S(1)}, f32[1024,768]{1,0:T(8,128)S(1)}, f32[8,768]{1,0:T(8,128)S(1)}, bf16[1,2,768,1536]{3,2,1,0:T(8,128)(2,1)}) custom-call(s32[4]{0:T(128)S(1)} %pad_add_fusion.coords_ref, bf16[16,48,1536]{2,1,0:T(8,128)(2,1)} %copy-done.10, bf16[16,48,1536]{2,1,0:T(8,128)(2,1)} %copy-done.26, ...), custom_call_target="tpu_custom_call" | custom-call | flops 4831838208 | bytes 20000000 | tf_op jit(solution)/shard_map/drop/pallas_call | solution.py:182
  153.5 8.3 %down_gradient.1 = (bf16[16,48,1536]{2,1,0:T(8,128)(2,1)}, bf16[16,48,1536]{2,1,0:T(8,128)(2,1)}) custom-call(s32[4]{0:T(128)S(1)} %pad_add_fusion.coords_ref, bf16[1024,768]{1,0:T(8,128)(2,1)S(1)} %get-tuple-element.154.left_ref.branch_ref, bf16[1024,3072]{1,0:T(8,128)(2,1)S(1)} %get-tuple-element.150.refs_2_.refs_0_.refs_1_, ...), custom_call_target="tpu_custom_call" | custom-call | flops 4831838208 | bytes 18000000 | tf_op jit(solution)/shard_map/down_gradient/pallas_call | solution.py:182
  162.3 8.5 %bend.1 = (bf16[1024,3072]{1,0:T(8,128)(2,1)S(1)}, f32[8,3072]{1,0:T(8,128)}) custom-call(bf16[1024,768]{1,0:T(8,128)(2,1)S(1)} %get-tuple-element.154.left_ref.branch_ref, bf16[1,2,768,1536]{3,2,1,0:T(8,128)(2,1)} %get-tuple-element.155.down_ref, bf16[1024,3072]{1,0:T(8,128)(2,1)S(1)} %get-tuple-element.159.slope_ref), custom_call_target="tpu_custom_call" | custom-call | flops 4831838208 | bytes 20000000 | tf_op jit(solution)/shard_map/bend/pallas_call | solution.py:182
  171.6 10.5 %lower.1 = (f32[1024,768]{1,0:T(8,128)}, bf16[1024,768]{1,0:T(8,128)(2,1)S(1)}, f32[8,768]{1,0:T(8,128)S(1)}) custom-call(bf16[1024,3072]{1,0:T(8,128)(2,1)S(1)} %get-tuple-element.160.gl_ref.refs_0_.refs_1_, bf16[1,2,768,1536]{3,2,1,0:T(8,128)(2,1)} %get-tuple-element.161.up_ref, f32[1024,768]{1,0:T(8,128)S(1)} %get-tuple-element.164.second_ref, ...), custom_call_target="tpu_custom_call" | custom-call | flops 4831838208 | bytes 20000000 | tf_op jit(solution)/shard_map/lower/pallas_call | solution.py:182
  182.1 10.9 %unmix.1 = (bf16[16,48,2048]{2,1,0:T(8,128)(2,1)}, bf16[16,48,2048]{2,1,0:T(8,128)(2,1)}, bf16[1024,768]{1,0:T(8,128)(2,1)S(1)}, bf16[1024,768]{1,0:T(8,128)(2,1...) custom-call(s32[4]{0:T(128)S(1)} %pad_add_fusion.coords_ref, ...), custom_call_target="tpu_custom_call" | custom-call | flops 2415919104 | bytes 16000000 | tf_op jit(solution)/shard_map/unmix/pallas_call | solution.py:182
  193.3 2.5 collective-permute-start.22
  195.9 1.6 collective-permute-start.21
  197.4 8.0 %up_gradient.1 = (bf16[16,48,2048]{2,1,0:T(8,128)(2,1)}, bf16[16,48,2048]{2,1,0:T(8,128)(2,1)}) custom-call(s32[4]{0:T(128)S(1)} %pad_add_fusion.coords_ref, bf16[1024,768]{1,0:T(8,128)(2,1)S(1)} %get-tuple-element.179.refs_2_.left_ref, ...), custom_call_target="tpu_custom_call", output_to_operand_aliasing={{0}: (4, {}), {1}: (5, {})} | custom-call | flops 4831838208 | bytes 18000000 | tf_op jit(solution)/shard_map/up_gradient/pallas_call | solution.py:182
  205.4 6.7 %collective-permute-done.21.later_ref = bf16[6,256,128]{2,1,0:T(8,128)(2,1)S(1)} collective-permute-done((bf16[6,256,128]{2,1,0:T(8,128)(2,1)S(1)}, bf16[6,256,128]{2,1,0:T(8,128)(2,1)S(1)}, u32[]{:S(2)}, u32[]{:S(2)}) %collective-permute-start.21) | collective-permute-done | bytes 393248 | tf_op jit(solution)/shard_map/ppermute | solution.py:1201
  212.5 2.7 collective-permute-start.25
  215.2 1.6 collective-permute-start.26
  216.9 13.7 %unattend.2 = (bf16[1024,768]{1,0:T(8,128)(2,1)S(1)}, bf16[1024,768]{1,0:T(8,128)(2,1)S(1)}, bf16[1024,768]{1,0:T(8,128)(2,1)S(1)}) custom-call(bf16[1024,768]{1,0:T(8,128)(2,1)S(1)} %copy-done, bf16[1024,768]{1,0:T(8,128)(2,1)S(1)} %copy-done.1, bf16[1024,768]{1,0:T(8,128)(2,1)S(1)} %copy-done.2, bf16[1024,768]{1,0:T(8,128)(2,1)S(1)} %get-tuple-element.184.gn_ref, ...), custom_call_target="tpu_custom_call" | custom-call | flops 20000000000 | bytes 20000000 | tf_op jit(solution)/shard_map/unattend/pallas_call | solution.py:182
  232.0 2.1 collective-permute-start.27
  234.0 13.4 %unattend.3 = (bf16[1024,768]{1,0:T(8,128)(2,1)S(1)}, bf16[1024,768]{1,0:T(8,128)(2,1)S(1)}, bf16[1024,768]{1,0:T(8,128)(2,1)S(1)}) custom-call(bf16[1024,768]{1,0:T(8,128)(2,1)} %get-tuple-element.129.sq_ref, bf16[1024,768]{1,0:T(8,128)(2,1)} %get-tuple-element.130.sk_ref, ...), custom_call_target="tpu_custom_call", output_to_operand_aliasing={{0}: (14, {}), {1}: (15, {}), {2}: (16, {})} | custom-call | flops 20000000000 | bytes 20000000 | tf_op jit(solution)/shard_map/unattend/pallas_call | solution.py:182
  248.3 10.5 %weight_gradients.1 = (bf16[16,48,1280]{2,1,0:T(8,128)(2,1)}, bf16[16,48,1280]{2,1,0:T(8,128)(2,1)}) custom-call(s32[4]{0:T(128)S(1)} %pad_add_fusion.coords_ref, bf16[1024,768]{1,0:T(8,128)(2,1)} %x_ref.3, bf16[1024,768]{1,0:T(8,128)(2,1)S(1)} %get-tuple-element.205.q_ref, bf16[1024,768]{1,0:T(8,128)(2,1)S(1)} %get-tuple-element.199.k_ref, ...), custom_call_target="tpu_custom_call" | custom-call | flops 3623878656 | bytes 10000000 | tf_op jit(solution)/shard_map/weight_gradients/pallas_call | solution.py:182
  260.4 4.0 %collective-permute-done.28 = bf16[16,48,1280]{2,1,0:T(8,128)(2,1)S(1)} collective-permute-done((bf16[16,48,1280]{2,1,0:T(8,128)(2,1)S(1)}, bf16[16,48,1280]{2,1,0:T(8,128)(2,1)S(1)}, u32[]{:S(2)}, u32[]{:S(2)}) %collective-permute-start.28) | collective-permute-done | bytes 1966112 | tf_op jit(solution)/shard_map/ppermute | solution.py:1201
  265.0 7.9 %input_gradient.1 = bf16[1024,768]{1,0:T(8,128)(2,1)} custom-call(f32[1024,768]{1,0:T(8,128)} %get-tuple-element.166.first_ref, bf16[1024,768]{1,0:T(8,128)(2,1)S(1)} %get-tuple-element.205.q_ref, bf16[1024,768]{1,0:T(8,128)(2,1)S(1)} %get-tuple-element.199.k_ref, bf16[1024,768]{1,0:T(8,128)(2,1)S(1)} %get-tuple-element.206.v_ref, ...), custom_call_target="tpu_custom_call" | custom-call | flops 3623878656 | bytes 14000000 | tf_op jit(solution)/shard_map/input_gradient/pallas_call | solution.py:182
  272.9 4.1 %collective-permute-done.34 = bf16[4,48,2048]{2,1,0:T(8,128)(2,1)S(1)} collective-permute-done((bf16[4,48,2048]{2,1,0:T(8,128)(2,1)S(1)}, bf16[4,48,2048]{2,1,0:T(8,128)(2,1)S(1)}, u32[]{:S(2)}, u32[]{:S(2)}) %collective-permute-start.34) | collective-permute-done | bytes 786464 | tf_op jit(solution)/shard_map/ppermute | solution.py:1201
  278.7 2.0 collective-permute-start.36
  280.7 1.7 collective-permute-done.29
  282.8 5.7 %collective-permute-done.37 = bf16[48,2048]{1,0:T(8,128)(2,1)S(1)} collective-permute-done((bf16[48,2048]{1,0:T(8,128)(2,1)S(1)}, bf16[48,2048]{1,0:T(8,128)(2,1)S(1)}, u32[]{:S(2)}, u32[]{:S(2)}) %collective-permute-start.37) | collective-permute-done | bytes 196640 | tf_op jit(solution)/shard_map/ppermute | solution.py:1201
  288.5 7.7 %collective-permute-done.36 = bf16[48,2048]{1,0:T(8,128)(2,1)S(1)} collective-permute-done((bf16[48,2048]{1,0:T(8,128)(2,1)S(1)}, bf16[48,2048]{1,0:T(8,128)(2,1)S(1)}, u32[]{:S(2)}, u32[]{:S(2)}) %collective-permute-start.36) | collective-permute-done | bytes 196640 | tf_op jit(solution)/shard_map/ppermute | solution.py:1201
  298.6 2.0 collective-permute-start.32
  305.2 4.6 %collective-permute-done.32 = bf16[48,1280]{1,0:T(8,128)(2,1)S(1)} collective-permute-done((bf16[48,1280]{1,0:T(8,128)(2,1)S(1)}, bf16[48,1280]{1,0:T(8,128)(2,1)S(1)}, u32[]{:S(2)}, u32[]{:S(2)}) %collective-permute-start.32) | collective-permute-done | bytes 122912 | tf_op jit(solution)/shard_map/ppermute | solution.py:1201
  (150 shorter events, 33.5 us)
Async XLA Ops:
  2.4 10.3 %collective-permute-start.2 = (bf16[48,1664]{1,0:T(8,128)(2,1)}, bf16[48,1664]{1,0:T(8,128)(2,1)S(1)}, u32[]{:S(2)}, u32[]{:S(2)}) collective-permute-start(bf16[48,1664]{1,0:T(8,128)(2,1)} %pack.1.refs_0_), channel_id=1, source_target_pairs={{0,24},{1,25},{2,26},{3,27},{4,28},{5,29},{6,30},{7,31},{8,16},{9,... | collective-permute-start | bytes 479240 | tf_op jit(solution)/shard_map/ppermute | solution.py:1201
  7.5 13.7 %collective-permute-start.1 = (bf16[48,1664]{1,0:T(8,128)(2,1)}, bf16[48,1664]{1,0:T(8,128)(2,1)S(1)}, u32[]{:S(2)}, u32[]{:S(2)}) collective-permute-start(bf16[48,1664]{1,0:T(8,128)(2,1)} %pack.1.refs_0_), channel_id=1, source_target_pairs={{0,16},{1,17},{2,18},{3,19},{4,20},{5,21},{6,22},{7,23},{8,24},{9,... | collective-permute-start | bytes 479240 | tf_op jit(solution)/shard_map/ppermute | solution.py:1201
  7.5 13.7 %collective-permute-start = (bf16[48,1664]{1,0:T(8,128)(2,1)}, bf16[48,1664]{1,0:T(8,128)(2,1)S(1)}, u32[]{:S(2)}, u32[]{:S(2)}) collective-permute-start(bf16[48,1664]{1,0:T(8,128)(2,1)} %pack.1.refs_0_), channel_id=1, source_target_pairs={{0,8},{1,9},{2,10},{3,11},{4,12},{5,13},{6,14},{7,15},{8,0},{9,1},... | collective-permute-start | bytes 479240 | tf_op jit(solution)/shard_map/ppermute | solution.py:1201
  24.6 10.6 %copy-start.4 = (bf16[4,48,1664]{2,1,0:T(8,128)(2,1)S(1)}, bf16[4,48,1664]{2,1,0:T(8,128)(2,1)}, u32[]{:S(2)}) copy-start(bf16[4,48,1664]{2,1,0:T(8,128)(2,1)} %join.3) | copy-start | bytes 1916932
  24.6 10.6 %collective-permute-start.3 = (bf16[4,48,1664]{2,1,0:T(8,128)(2,1)}, bf16[4,48,1664]{2,1,0:T(8,128)(2,1)S(1)}, u32[]{:S(2)}, u32[]{:S(2)}) collective-permute-start(bf16[4,48,1664]{2,1,0:T(8,128)(2,1)} %join.3), channel_id=1, source_target_pairs={{0,1},{1,0},{2,6},{3,7},{4,5},{5,4},{6,2},{7,3},{8,9},{9,8},{10,14... | collective-permute-start | bytes 1916936 | tf_op jit(solution)/shard_map/ppermute | solution.py:1201
  28.2 10.7 %copy-start.16 = (bf16[48,1536]{1,0:T(8,128)(2,1)S(1)}, bf16[48,1536]{1,0:T(8,128)(2,1)}, u32[]{:S(2)}) copy-start(bf16[48,1536]{1,0:T(8,128)(2,1)} %refs_0_.3) | copy-start | bytes 442372
  37.4 18.3 %collective-permute-start.4 = (bf16[8,48,1664]{2,1,0:T(8,128)(2,1)S(1)}, bf16[8,48,1664]{2,1,0:T(8,128)(2,1)S(1)}, u32[]{:S(2)}, u32[]{:S(2)}) collective-permute-start(bf16[8,48,1664]{2,1,0:T(8,128)(2,1)S(1)} %pad_maximum_fusion.3), channel_id=1, source_target_pairs={{0,4},{1,5},{2,3},{3,2},{4,0},{5,1},{6,7},{7,6},{8,12},{9,13},{10,... | collective-permute-start | bytes 3833864 | tf_op jit(solution)/shard_map/ppermute | solution.py:1201
  38.9 8.6 %collective-permute-start.7 = (bf16[48,1536]{1,0:T(8,128)(2,1)S(1)}, bf16[48,1536]{1,0:T(8,128)(2,1)S(1)}, u32[]{:S(2)}, u32[]{:S(2)}) collective-permute-start(bf16[48,1536]{1,0:T(8,128)(2,1)S(1)} %copy-done.16), channel_id=1, source_target_pairs={{0,24},{1,25},{2,26},{3,27},{4,28},{5,29},{6,30},{7,31},{8,16},{9,... | collective-permute-start | bytes 442376 | tf_op jit(solution)/shard_map/ppermute | solution.py:1201
  41.4 11.0 %collective-permute-start.6 = (bf16[48,1536]{1,0:T(8,128)(2,1)S(1)}, bf16[48,1536]{1,0:T(8,128)(2,1)S(1)}, u32[]{:S(2)}, u32[]{:S(2)}) collective-permute-start(bf16[48,1536]{1,0:T(8,128)(2,1)S(1)} %copy-done.16), channel_id=1, source_target_pairs={{0,16},{1,17},{2,18},{3,19},{4,20},{5,21},{6,22},{7,23},{8,24},{9,... | collective-permute-start | bytes 442376 | tf_op jit(solution)/shard_map/ppermute | solution.py:1201
  41.4 11.0 %collective-permute-start.5 = (bf16[48,1536]{1,0:T(8,128)(2,1)S(1)}, bf16[48,1536]{1,0:T(8,128)(2,1)S(1)}, u32[]{:S(2)}, u32[]{:S(2)}) collective-permute-start(bf16[48,1536]{1,0:T(8,128)(2,1)S(1)} %copy-done.16), channel_id=1, source_target_pairs={{0,8},{1,9},{2,10},{3,11},{4,12},{5,13},{6,14},{7,15},{8,0},{9,1},... | collective-permute-start | bytes 442376 | tf_op jit(solution)/shard_map/ppermute | solution.py:1201
  56.0 16.1 %copy-start.7 = (bf16[16,48,1664]{2,1,0:T(8,128)(2,1)}, bf16[16,48,1664]{2,1,0:T(8,128)(2,1)S(1)}, u32[]{:S(2)}) copy-start(bf16[16,48,1664]{2,1,0:T(8,128)(2,1)S(1)} %pad_maximum_fusion.refs_0_) | copy-start | bytes 7667716
  56.0 11.7 %copy-start.17 = (bf16[1536,48]{0,1:T(8,128)(2,1)S(1)}, bf16[1536,48]{0,1:T(8,128)(2,1)}, u32[]{:S(2)}) copy-start(bf16[1536,48]{0,1:T(8,128)(2,1)} %param.32) | copy-start | bytes 442372
  56.0 10.6 %collective-permute-start.10 = (bf16[16,48,1664]{2,1,0:T(8,128)(2,1)S(1)}, bf16[16,48,1664]{2,1,0:T(8,128)(2,1)S(1)}, u32[]{:S(2)}, u32[]{:S(2)}) collective-permute-start(bf16[16,48,1664]{2,1,0:T(8,128)(2,1)S(1)} %pad_maximum_fusion.refs_0_), channel_id=1, source_target_pairs={{0,2},{1,3},{2,0},{3,1},{4,6},{5,7},{6,4},{7,5},{8,10},{9,11},{10,... | collective-permute-start | bytes 7667720 | tf_op jit(solution)/shard_map/ppermute | solution.py:1201
  56.7 9.9 %collective-permute-start.9 = (bf16[4,48,1536]{2,1,0:T(8,128)(2,1)S(1)}, bf16[4,48,1536]{2,1,0:T(8,128)(2,1)S(1)}, u32[]{:S(2)}, u32[]{:S(2)}) collective-permute-start(bf16[4,48,1536]{2,1,0:T(8,128)(2,1)S(1)} %copy-done.5), channel_id=1, source_target_pairs={{0,1},{1,0},{2,6},{3,7},{4,5},{5,4},{6,2},{7,3},{8,9},{9,8},{10,14... | collective-permute-start | bytes 1769480 | tf_op jit(solution)/shard_map/ppermute | solution.py:1201
  66.7 23.3 %collective-permute-start.13 = (bf16[8,48,1536]{2,1,0:T(8,128)(2,1)S(1)}, bf16[8,48,1536]{2,1,0:T(8,128)(2,1)S(1)}, u32[]{:S(2)}, u32[]{:S(2)}) collective-permute-start(bf16[8,48,1536]{2,1,0:T(8,128)(2,1)S(1)} %pad_maximum_fusion.4), channel_id=1, source_target_pairs={{0,4},{1,5},{2,3},{3,2},{4,0},{5,1},{6,7},{7,6},{8,12},{9,13},{10,... | collective-permute-start | bytes 3538952 | tf_op jit(solution)/shard_map/ppermute | solution.py:1201
  67.7 18.9 %collective-permute-start.12 = (bf16[48,1536]{1,0:T(8,128)(2,1)S(1)}, bf16[48,1536]{1,0:T(8,128)(2,1)S(1)}, u32[]{:S(2)}, u32[]{:S(2)}) collective-permute-start(bf16[48,1536]{1,0:T(8,128)(2,1)S(1)} %bitcast.56), channel_id=1, source_target_pairs={{0,24},{1,25},{2,26},{3,27},{4,28},{5,29},{6,30},{7,31},{8,16},{9,... | collective-permute-start | bytes 442376 | tf_op jit(solution)/shard_map/ppermute | solution.py:1201
  69.2 17.4 %collective-permute-start.11 = (bf16[48,1536]{1,0:T(8,128)(2,1)S(1)}, bf16[48,1536]{1,0:T(8,128)(2,1)S(1)}, u32[]{:S(2)}, u32[]{:S(2)}) collective-permute-start(bf16[48,1536]{1,0:T(8,128)(2,1)S(1)} %bitcast.57), channel_id=1, source_target_pairs={{0,16},{1,17},{2,18},{3,19},{4,20},{5,21},{6,22},{7,23},{8,24},{9,... | collective-permute-start | bytes 442376 | tf_op jit(solution)/shard_map/ppermute | solution.py:1201
  69.2 17.4 %collective-permute-start.8 = (bf16[48,1536]{1,0:T(8,128)(2,1)S(1)}, bf16[48,1536]{1,0:T(8,128)(2,1)S(1)}, u32[]{:S(2)}, u32[]{:S(2)}) collective-permute-start(bf16[48,1536]{1,0:T(8,128)(2,1)S(1)} %bitcast.58), channel_id=1, source_target_pairs={{0,8},{1,9},{2,10},{3,11},{4,12},{5,13},{6,14},{7,15},{8,0},{9,1},... | collective-permute-start | bytes 442376 | tf_op jit(solution)/shard_map/ppermute | solution.py:1201
  90.2 15.8 %copy-start.9 = (bf16[16,48,1536]{2,1,0:T(8,128)(2,1)}, bf16[16,48,1536]{2,1,0:T(8,128)(2,1)S(1)}, u32[]{:S(2)}) copy-start(bf16[16,48,1536]{2,1,0:T(8,128)(2,1)S(1)} %pad_maximum_fusion.1.refs_0_) | copy-start | bytes 7077892
  90.2 20.9 %collective-permute-start.16 = (bf16[16,48,1536]{2,1,0:T(8,128)(2,1)S(1)}, bf16[16,48,1536]{2,1,0:T(8,128)(2,1)S(1)}, u32[]{:S(2)}, u32[]{:S(2)}) collective-permute-start(bf16[16,48,1536]{2,1,0:T(8,128)(2,1)S(1)} %pad_maximum_fusion.1.refs_0_), channel_id=1, source_target_pairs={{0,2},{1,3},{2,0},{3,1},{4,6},{5,7},{6,4},{7,5},{8,10},{9,11},{10,... | collective-permute-start | bytes 7077896 | tf_op jit(solution)/shard_map/ppermute | solution.py:1201
  90.9 15.1 %collective-permute-start.15 = (bf16[6,256,128]{2,1,0:T(8,128)(2,1)S(1)}, bf16[6,256,128]{2,1,0:T(8,128)(2,1)S(1)}, u32[]{:S(2)}, u32[]{:S(2)}) collective-permute-start(bf16[6,256,128]{2,1,0:T(8,128)(2,1)S(1)} %copy-done.29), channel_id=1, source_target_pairs={{0,1},{2,3},{4,5},{6,7},{8,9},{10,11},{12,13},{14,15},{16,17},{18,... | collective-permute-start | bytes 1179656 | tf_op jit(solution)/shard_map/ppermute | solution.py:1201
  94.1 16.9 %collective-permute-start.14 = (bf16[4,48,1536]{2,1,0:T(8,128)(2,1)S(1)}, bf16[4,48,1536]{2,1,0:T(8,128)(2,1)S(1)}, u32[]{:S(2)}, u32[]{:S(2)}) collective-permute-start(bf16[4,48,1536]{2,1,0:T(8,128)(2,1)S(1)} %copy-done.6), channel_id=1, source_target_pairs={{0,1},{1,0},{2,6},{3,7},{4,5},{5,4},{6,2},{7,3},{8,9},{9,8},{10,14... | collective-permute-start | bytes 1769480 | tf_op jit(solution)/shard_map/ppermute | solution.py:1201
  111.1 16.3 %collective-permute-start.17 = (bf16[8,48,1536]{2,1,0:T(8,128)(2,1)S(1)}, bf16[8,48,1536]{2,1,0:T(8,128)(2,1)S(1)}, u32[]{:S(2)}, u32[]{:S(2)}) collective-permute-start(bf16[8,48,1536]{2,1,0:T(8,128)(2,1)S(1)} %pad_maximum_fusion.5), channel_id=1, source_target_pairs={{0,4},{1,5},{2,3},{3,2},{4,0},{5,1},{6,7},{7,6},{8,12},{9,13},{10,... | collective-permute-start | bytes 3538952 | tf_op jit(solution)/shard_map/ppermute | solution.py:1201
  127.6 11.9 %copy-start.10 = (bf16[16,48,1536]{2,1,0:T(8,128)(2,1)}, bf16[16,48,1536]{2,1,0:T(8,128)(2,1)S(1)}, u32[]{:S(2)}) copy-start(bf16[16,48,1536]{2,1,0:T(8,128)(2,1)S(1)} %pad_maximum_fusion.2.refs_0_) | copy-start | bytes 7077892
  127.6 11.9 %collective-permute-start.18 = (bf16[16,48,1536]{2,1,0:T(8,128)(2,1)S(1)}, bf16[16,48,1536]{2,1,0:T(8,128)(2,1)S(1)}, u32[]{:S(2)}, u32[]{:S(2)}) collective-permute-start(bf16[16,48,1536]{2,1,0:T(8,128)(2,1)S(1)} %pad_maximum_fusion.2.refs_0_), channel_id=1, source_target_pairs={{0,2},{1,3},{2,0},{3,1},{4,6},{5,7},{6,4},{7,5},{8,10},{9,11},{10,... | collective-permute-start | bytes 7077896 | tf_op jit(solution)/shard_map/ppermute | solution.py:1201
  161.8 9.0 %collective-permute-start.19 = (bf16[16,48,1536]{2,1,0:T(8,128)(2,1)}, bf16[16,48,1536]{2,1,0:T(8,128)(2,1)S(1)}, u32[]{:S(2)}, u32[]{:S(2)}) collective-permute-start(bf16[16,48,1536]{2,1,0:T(8,128)(2,1)} %get-tuple-element.158), channel_id=1, source_target_pairs={{0,2},{1,3},{2,0},{3,1},{4,6},{5,7},{6,4},{7,5},{8,10},{9,11},{10,... | collective-permute-start | bytes 7077896 | tf_op jit(solution)/shard_map/ppermute | solution.py:1201
  171.5 21.5 %collective-permute-start.20 = (bf16[8,48,1536]{2,1,0:T(8,128)(2,1)S(1)}, bf16[8,48,1536]{2,1,0:T(8,128)(2,1)S(1)}, u32[]{:S(2)}, u32[]{:S(2)}) collective-permute-start(bf16[8,48,1536]{2,1,0:T(8,128)(2,1)S(1)} %get-tuple-element.227), channel_id=1, source_target_pairs={{0,4},{1,5},{2,3},{3,2},{4,0},{5,1},{6,7},{7,6},{8,12},{9,13},{10,... | collective-permute-start | bytes 3538952 | tf_op jit(solution)/shard_map/ppermute | solution.py:1201
  193.3 18.8 %collective-permute-start.22 = (bf16[4,48,1536]{2,1,0:T(8,128)(2,1)S(1)}, bf16[4,48,1536]{2,1,0:T(8,128)(2,1)S(1)}, u32[]{:S(2)}, u32[]{:S(2)}) collective-permute-start(bf16[4,48,1536]{2,1,0:T(8,128)(2,1)S(1)} %get-tuple-element.233), channel_id=1, source_target_pairs={{0,1},{1,0},{2,6},{3,7},{4,5},{5,4},{6,2},{7,3},{8,9},{9,8},{10,14... | collective-permute-start | bytes 1769480 | tf_op jit(solution)/shard_map/ppermute | solution.py:1201
  195.9 21.0 %copy-start = (bf16[1024,768]{1,0:T(8,128)(2,1)S(1)}, bf16[1024,768]{1,0:T(8,128)(2,1)}, u32[]{:S(2)}) copy-start(bf16[1024,768]{1,0:T(8,128)(2,1)} %get-tuple-element.129.sq_ref) | copy-start | bytes 4718596
  195.9 21.0 %copy-start.1 = (bf16[1024,768]{1,0:T(8,128)(2,1)S(1)}, bf16[1024,768]{1,0:T(8,128)(2,1)}, u32[]{:S(2)}) copy-start(bf16[1024,768]{1,0:T(8,128)(2,1)} %get-tuple-element.130.sk_ref) | copy-start | bytes 4718596
  195.9 21.0 %copy-start.2 = (bf16[1024,768]{1,0:T(8,128)(2,1)S(1)}, bf16[1024,768]{1,0:T(8,128)(2,1)}, u32[]{:S(2)}) copy-start(bf16[1024,768]{1,0:T(8,128)(2,1)} %get-tuple-element.131.v_ref) | copy-start | bytes 4718596
  195.9 16.3 %collective-permute-start.21 = (bf16[6,256,128]{2,1,0:T(8,128)(2,1)S(1)}, bf16[6,256,128]{2,1,0:T(8,128)(2,1)S(1)}, u32[]{:S(2)}, u32[]{:S(2)}) collective-permute-start(bf16[6,256,128]{2,1,0:T(8,128)(2,1)S(1)} %copy-done.30), channel_id=1, source_target_pairs={{1,0},{3,2},{5,4},{7,6},{9,8},{11,10},{13,12},{15,14},{17,16},{19,... | collective-permute-start | bytes 1179656 | tf_op jit(solution)/shard_map/ppermute | solution.py:1201
  212.3 18.2 %collective-permute-start.23 = (bf16[16,48,2048]{2,1,0:T(8,128)(2,1)}, bf16[16,48,2048]{2,1,0:T(8,128)(2,1)S(1)}, u32[]{:S(2)}, u32[]{:S(2)}) collective-permute-start(bf16[16,48,2048]{2,1,0:T(8,128)(2,1)} %get-tuple-element.192), channel_id=1, source_target_pairs={{0,2},{1,3},{2,0},{3,1},{4,6},{5,7},{6,4},{7,5},{8,10},{9,11},{10,... | collective-permute-start | bytes 9437192 | tf_op jit(solution)/shard_map/ppermute | solution.py:1201
  212.4 35.1 %collective-permute-start.24 = (bf16[48,1536]{1,0:T(8,128)(2,1)S(1)}, bf16[48,1536]{1,0:T(8,128)(2,1)S(1)}, u32[]{:S(2)}, u32[]{:S(2)}) collective-permute-start(bf16[48,1536]{1,0:T(8,128)(2,1)S(1)} %get-tuple-element.198), channel_id=1, source_target_pairs={{0,8},{1,9},{2,10},{3,11},{4,12},{5,13},{6,14},{7,15},{8,0},{9,1},... | collective-permute-start | bytes 442376 | tf_op jit(solution)/shard_map/ppermute | solution.py:1201
  212.5 35.0 %collective-permute-start.25 = (bf16[48,1536]{1,0:T(8,128)(2,1)S(1)}, bf16[48,1536]{1,0:T(8,128)(2,1)S(1)}, u32[]{:S(2)}, u32[]{:S(2)}) collective-permute-start(bf16[48,1536]{1,0:T(8,128)(2,1)S(1)} %get-tuple-element.201), channel_id=1, source_target_pairs={{0,16},{1,17},{2,18},{3,19},{4,20},{5,21},{6,22},{7,23},{8,24},{9,... | collective-permute-start | bytes 442376 | tf_op jit(solution)/shard_map/ppermute | solution.py:1201
  215.2 32.2 %collective-permute-start.26 = (bf16[48,1536]{1,0:T(8,128)(2,1)S(1)}, bf16[48,1536]{1,0:T(8,128)(2,1)S(1)}, u32[]{:S(2)}, u32[]{:S(2)}) collective-permute-start(bf16[48,1536]{1,0:T(8,128)(2,1)S(1)} %get-tuple-element.203), channel_id=1, source_target_pairs={{0,24},{1,25},{2,26},{3,27},{4,28},{5,29},{6,30},{7,31},{8,16},{9,... | collective-permute-start | bytes 442376 | tf_op jit(solution)/shard_map/ppermute | solution.py:1201
  216.9 13.7 %copy-start.3 = (bf16[16,48,2048]{2,1,0:T(8,128)(2,1)S(1)}, bf16[16,48,2048]{2,1,0:T(8,128)(2,1)}, u32[]{:S(2)}) copy-start(bf16[16,48,2048]{2,1,0:T(8,128)(2,1)} %get-tuple-element.180) | copy-start | bytes 9437188
  232.0 26.8 %collective-permute-start.27 = (bf16[8,48,2048]{2,1,0:T(8,128)(2,1)S(1)}, bf16[8,48,2048]{2,1,0:T(8,128)(2,1)S(1)}, u32[]{:S(2)}, u32[]{:S(2)}) collective-permute-start(bf16[8,48,2048]{2,1,0:T(8,128)(2,1)S(1)} %get-tuple-element.225), channel_id=1, source_target_pairs={{0,4},{1,5},{2,3},{3,2},{4,0},{5,1},{6,7},{7,6},{8,12},{9,13},{10,... | collective-permute-start | bytes 4718600 | tf_op jit(solution)/shard_map/ppermute | solution.py:1201
  260.4 4.0 %collective-permute-start.28 = (bf16[16,48,1280]{2,1,0:T(8,128)(2,1)S(1)}, bf16[16,48,1280]{2,1,0:T(8,128)(2,1)S(1)}, u32[]{:S(2)}, u32[]{:S(2)}) collective-permute-start(bf16[16,48,1280]{2,1,0:T(8,128)(2,1)S(1)} %copy-done.27), channel_id=1, source_target_pairs={{0,2},{1,3},{2,0},{3,1},{4,6},{5,7},{6,4},{7,5},{8,10},{9,11},{10,... | collective-permute-start | bytes 5898248 | tf_op jit(solution)/shard_map/ppermute | solution.py:1201
  260.4 16.6 %collective-permute-start.34 = (bf16[4,48,2048]{2,1,0:T(8,128)(2,1)S(1)}, bf16[4,48,2048]{2,1,0:T(8,128)(2,1)S(1)}, u32[]{:S(2)}, u32[]{:S(2)}) collective-permute-start(bf16[4,48,2048]{2,1,0:T(8,128)(2,1)S(1)} %get-tuple-element.231), channel_id=1, source_target_pairs={{0,1},{1,0},{2,6},{3,7},{4,5},{5,4},{6,2},{7,3},{8,9},{9,8},{10,14... | collective-permute-start | bytes 2359304 | tf_op jit(solution)/shard_map/ppermute | solution.py:1201
  264.8 17.6 %collective-permute-start.29 = (bf16[8,48,1280]{2,1,0:T(8,128)(2,1)S(1)}, bf16[8,48,1280]{2,1,0:T(8,128)(2,1)S(1)}, u32[]{:S(2)}, u32[]{:S(2)}) collective-permute-start(bf16[8,48,1280]{2,1,0:T(8,128)(2,1)S(1)} %get-tuple-element.230), channel_id=1, source_target_pairs={{0,4},{1,5},{2,3},{3,2},{4,0},{5,1},{6,7},{7,6},{8,12},{9,13},{10,... | collective-permute-start | bytes 2949128 | tf_op jit(solution)/shard_map/ppermute | solution.py:1201
  277.1 19.1 %collective-permute-start.35 = (bf16[48,2048]{1,0:T(8,128)(2,1)S(1)}, bf16[48,2048]{1,0:T(8,128)(2,1)S(1)}, u32[]{:S(2)}, u32[]{:S(2)}) collective-permute-start(bf16[48,2048]{1,0:T(8,128)(2,1)S(1)} %get-tuple-element.237), channel_id=1, source_target_pairs={{0,8},{1,9},{2,10},{3,11},{4,12},{5,13},{6,14},{7,15},{8,0},{9,1},... | collective-permute-start | bytes 589832 | tf_op jit(solution)/shard_map/ppermute | solution.py:1201
  277.2 11.2 %collective-permute-start.37 = (bf16[48,2048]{1,0:T(8,128)(2,1)S(1)}, bf16[48,2048]{1,0:T(8,128)(2,1)S(1)}, u32[]{:S(2)}, u32[]{:S(2)}) collective-permute-start(bf16[48,2048]{1,0:T(8,128)(2,1)S(1)} %get-tuple-element.238), channel_id=1, source_target_pairs={{0,24},{1,25},{2,26},{3,27},{4,28},{5,29},{6,30},{7,31},{8,16},{9,... | collective-permute-start | bytes 589832 | tf_op jit(solution)/shard_map/ppermute | solution.py:1201
  278.7 17.5 %collective-permute-start.36 = (bf16[48,2048]{1,0:T(8,128)(2,1)S(1)}, bf16[48,2048]{1,0:T(8,128)(2,1)S(1)}, u32[]{:S(2)}, u32[]{:S(2)}) collective-permute-start(bf16[48,2048]{1,0:T(8,128)(2,1)S(1)} %get-tuple-element.239), channel_id=1, source_target_pairs={{0,16},{1,17},{2,18},{3,19},{4,20},{5,21},{6,22},{7,23},{8,24},{9,... | collective-permute-start | bytes 589832 | tf_op jit(solution)/shard_map/ppermute | solution.py:1201
  282.7 14.3 %collective-permute-start.30 = (bf16[4,48,1280]{2,1,0:T(8,128)(2,1)S(1)}, bf16[4,48,1280]{2,1,0:T(8,128)(2,1)S(1)}, u32[]{:S(2)}, u32[]{:S(2)}) collective-permute-start(bf16[4,48,1280]{2,1,0:T(8,128)(2,1)S(1)} %get-tuple-element.236), channel_id=1, source_target_pairs={{0,1},{1,0},{2,6},{3,7},{4,5},{5,4},{6,2},{7,3},{8,9},{9,8},{10,14... | collective-permute-start | bytes 1474568 | tf_op jit(solution)/shard_map/ppermute | solution.py:1201
  297.1 7.0 %collective-permute-start.31 = (bf16[48,1280]{1,0:T(8,128)(2,1)S(1)}, bf16[48,1280]{1,0:T(8,128)(2,1)S(1)}, u32[]{:S(2)}, u32[]{:S(2)}) collective-permute-start(bf16[48,1280]{1,0:T(8,128)(2,1)S(1)} %get-tuple-element.244), channel_id=1, source_target_pairs={{0,8},{1,9},{2,10},{3,11},{4,12},{5,13},{6,14},{7,15},{8,0},{9,1},... | collective-permute-start | bytes 368648 | tf_op jit(solution)/shard_map/ppermute | solution.py:1201
  297.1 8.0 %collective-permute-start.33 = (bf16[48,1280]{1,0:T(8,128)(2,1)S(1)}, bf16[48,1280]{1,0:T(8,128)(2,1)S(1)}, u32[]{:S(2)}, u32[]{:S(2)}) collective-permute-start(bf16[48,1280]{1,0:T(8,128)(2,1)S(1)} %get-tuple-element.245), channel_id=1, source_target_pairs={{0,24},{1,25},{2,26},{3,27},{4,28},{5,29},{6,30},{7,31},{8,16},{9,... | collective-permute-start | bytes 368648 | tf_op jit(solution)/shard_map/ppermute | solution.py:1201
  298.6 11.2 %collective-permute-start.32 = (bf16[48,1280]{1,0:T(8,128)(2,1)S(1)}, bf16[48,1280]{1,0:T(8,128)(2,1)S(1)}, u32[]{:S(2)}, u32[]{:S(2)}) collective-permute-start(bf16[48,1280]{1,0:T(8,128)(2,1)S(1)} %get-tuple-element.246), channel_id=1, source_target_pairs={{0,16},{1,17},{2,18},{3,19},{4,20},{5,21},{6,22},{7,23},{8,24},{9,... | collective-permute-start | bytes 368648 | tf_op jit(solution)/shard_map/ppermute | solution.py:1201
  (21 other events, 64.1 us)
